TPU v7x, 128 devices: a whole 4x4x4 slice. The times are simulated.
128 devices in a mesh: seq: 16 (over y, x), exp: 8 (over z, core).
Axes of the slice: x: 4, y: 4, z: 4, core: 2. Of those that a mesh axis runs over, the one named last changes fastest.
Arguments:
- stream: bfloat16 [2048, 4096], P('seq', 'exp'), may hold values from -6 to 6
- mixer_in: bfloat16 [2048, 8192], P('seq', 'exp'), may hold values from -6 to 6
- gate_in: bfloat16 [2048, 8192], P('seq', 'exp'), may hold values from -6 to 6
- dt_raw: bfloat16 [2048, 8192], P('seq', 'exp'), may hold values from -2 to 13
- dt_bias: float32 [8192], P('exp'), may hold values from -13 to -2
- a_log: float32 [8192, 16], P('exp'), may hold values from -1.2 to 0.7
- conv_weight: float32 [8192, 4], P('exp'), may hold values from -3 to 3
- conv_bias: float32 [8192], P('exp'), may hold values from -6 to 6
- b_proj: float32 [2048, 16], P('seq'), may hold values from -6 to 6
- c_proj: float32 [2048, 16], P('seq'), may hold values from -6 to 6
- d_skip: float32 [8192], P('exp'), may hold values from 0.3 to 3
- w_out: bfloat16 [8192, 4096], P('exp', 'seq'), may hold values from -0.0625 to 0.0625
- expert_index: int32 [2048, 2], P('seq'), may hold values from 0 to 7, all different within a row; in each aligned block of 128 rows (0 to 127, 128 to 255, ...) at most 48 rows name the same one
- gate_weights: float32 [2048, 2], P('seq'), may hold values from 0.05 to 0.6
- norm_gain: float32 [4096], replicated, may hold values from 0.1 to 1.9
- w_gate: bfloat16 [8, 4096, 12288], P('exp', None, 'seq'), may hold values from -0.09375 to 0.09375
- w_up: bfloat16 [8, 4096, 12288], P('exp', None, 'seq'), may hold values from -0.09375 to 0.09375
- w_down: bfloat16 [8, 12288, 4096], P('exp', 'seq'), may hold values from -0.0546875 to 0.0546875
Outputs:
- block_out: bfloat16 [2048, 4096], P('seq', 'exp')
Inputs may be any that keep to these rules, and one draw needn't show every extreme that they name: `expert_index`: the two experts of a position differ. Among the 128 positions of one seq shard (aligned blocks), no expert is chosen by more than 48 routes, and in every draw some expert is chosen by exactly 48.
All inputs are finite; a program needn't handle non-finite values.
Results may differ from a plain program's by a relative error of at most 0.012.
Values may be sent and summed in bfloat16 or wider, within the bound.
No kernel may reach another device: no remote copies, remote signals or barrier semaphores. Data moves between devices by JAX's collectives and lax.ppermute only.
A program may use at most 192 MiB of HBM per device.

v0:
```python
import jax
import jax.numpy as jnp
from jax import lax
from jax.experimental import pallas as pl
from jax.experimental.pallas import tpu as pltpu
from jax.sharding import PartitionSpec as P

KCONV = 4
SIDE = 4
STATES = 16
LOG2E = 1.4426950408889634
F32 = jnp.float32
BF16 = jnp.bfloat16


def shift(value, axis, distance):
    cells = [(y, x) for y in range(SIDE) for x in range(SIDE)]
    if axis == "x":
        route = [(y * SIDE + x, y * SIDE + (x + distance) % SIDE) for y, x in cells]
    else:
        route = [(y * SIDE + x, (y + distance) % SIDE * SIDE + x) for y, x in cells]
    return lax.ppermute(value, "seq", route)


def ring_gather(block, axis):
    return [block] + [shift(block, axis, distance) for distance in range(1, SIDE)]


def grid_gather(block, order):
    near = jnp.stack(ring_gather(block, order[0]))
    return ring_gather(near, order[1])


def ring_scatter(blocks, axis):
    total = blocks[0].astype(F32)
    for k in (1, 3, 2):
        total = total + shift(blocks[k].astype(BF16), axis, -k).astype(F32)
    return total


def first_pass(x_ref, rim_ref, dt_ref, dtb_ref, cw_ref, cb_ref, rate_ref, b_ref,
               step_ref, act_ref, fin_ref, pad_ref):
    tokens, channels = x_ref.shape
    lanes = 128
    pad_ref[8 : 8 + tokens, :] = x_ref[...].astype(F32)
    pad_ref[0:8, :] = rim_ref[...].astype(F32)
    for k in range(channels // lanes):
        cols = slice(k * lanes, (k + 1) * lanes)
        total = cb_ref[:, cols]
        for tap in range(KCONV):
            low = 8 - (KCONV - 1) + tap
            total = total + cw_ref[tap : tap + 1, cols] * pad_ref[low : low + tokens, cols]
        act_ref[:, k, :] = total * jax.nn.sigmoid(total)
        raw = dt_ref[:, cols].astype(F32) + dtb_ref[:, cols]
        step_ref[:, k, :] = jnp.maximum(raw, 0.0) + jnp.log1p(jnp.exp(-jnp.abs(raw)))

    def advance(t, carry):
        states, summed = carry
        step = step_ref[t]
        source = step * act_ref[t]
        states = tuple(
            jnp.exp2(step * rate_ref[n]) * states[n] + b_ref[t, n] * source for n in range(STATES)
        )
        return states, summed + step

    zero = jnp.zeros((8, lanes), F32)
    states, summed = lax.fori_loop(0, tokens, advance, ((zero,) * STATES, zero), unroll=2)
    for n in range(STATES):
        fin_ref[n] = states[n]
    fin_ref[STATES] = summed


def second_pass(step_ref, act_ref, gate_ref, enter_ref, rate_ref, skip_ref, b_ref, c_ref,
                out_ref, y_ref):
    tokens, channels = gate_ref.shape
    lanes = 128
    skip = skip_ref[...]

    def advance(t, states):
        step = step_ref[t]
        act = act_ref[t]
        source = step * act
        sums = [skip * act, None]
        after = []
        for n in range(STATES):
            state = jnp.exp2(step * rate_ref[n]) * states[n] + b_ref[t, n] * source
            term = c_ref[t, n] * state
            sums[n % 2] = term if sums[n % 2] is None else sums[n % 2] + term
            after.append(state)
        y_ref[t] = sums[0] + sums[1]
        return tuple(after)

    lax.fori_loop(0, tokens, advance, tuple(enter_ref[n] for n in range(STATES)), unroll=2)
    for k in range(channels // lanes):
        cols = slice(k * lanes, (k + 1) * lanes)
        gate = gate_ref[:, cols].astype(F32)
        out_ref[:, cols] = (y_ref[:, k, :] * (gate * jax.nn.sigmoid(gate))).astype(BF16)


def entering_state(final, rate):
    along_x = lax.axis_index("seq") % SIDE
    along_y = lax.axis_index("seq") // SIDE

    def chain(earlier, latter):
        decay = jnp.exp2(rate * latter[1])
        return decay * earlier[0] + latter[0], earlier[1] + latter[1]

    def masked(pair, reached):
        return jnp.where(reached, pair[0], 0.0), jnp.where(reached, pair[1], 0.0)

    def split(packed):
        return packed[:STATES], packed[STATES]

    def spread(packed, axis, place):
        others = [split(shift(packed, axis, d)) for d in range(1, SIDE)]
        before = masked(others[2], place >= 3)
        for d in (2, 1):
            before = chain(before, masked(others[d - 1], place >= d))
        return before, others

    own = split(final)
    before_x, others = spread(final, "x", along_x)
    total = chain(before_x, own)
    for d in (3, 2, 1):
        total = chain(total, masked(others[d - 1], along_x < d))
    packed = jnp.concatenate([total[0], total[1][None]], 0)
    before_y, _ = spread(packed, "y", along_y)
    return chain(before_y, before_x)[0]


def mixer(mixer_in, gate_in, dt_raw, dt_bias, a_log, conv_weight, conv_bias, b_proj, c_proj, d_skip):
    tokens, channels = mixer_in.shape
    count, index = lax.axis_size("seq"), lax.axis_index("seq")
    rim = lax.ppermute(mixer_in[tokens - 8 :], "seq", [(i, i + 1) for i in range(count - 1)])
    rate = (-LOG2E * jnp.exp(a_log)).T.reshape(STATES, 8, 128)
    vmem = pl.BlockSpec(memory_space=pltpu.VMEM)
    smem = pl.BlockSpec(memory_space=pltpu.SMEM)
    wide = jax.ShapeDtypeStruct((tokens, 8, 128), F32)
    step, act, final = pl.pallas_call(
        first_pass,
        out_shape=(wide, wide, jax.ShapeDtypeStruct((STATES + 1, 8, 128), F32)),
        in_specs=[vmem] * 7 + [smem],
        out_specs=[vmem] * 3,
        scratch_shapes=[pltpu.VMEM((tokens + 8, channels), F32)],
        compiler_params=pltpu.CompilerParams(vmem_limit_bytes=32 << 20),
        name="scan_state",
    )(mixer_in, rim, dt_raw, dt_bias[None, :], conv_weight.T, conv_bias[None, :], rate, b_proj)
    enter = entering_state(final, rate)
    return pl.pallas_call(
        second_pass,
        out_shape=jax.ShapeDtypeStruct((tokens, channels), BF16),
        in_specs=[vmem] * 6 + [smem] * 2,
        out_specs=vmem,
        scratch_shapes=[pltpu.VMEM((tokens, 8, 128), F32)],
        compiler_params=pltpu.CompilerParams(vmem_limit_bytes=32 << 20),
        name="scan_output",
    )(step, act, gate_in, enter, rate, d_skip.reshape(8, 128), b_proj, c_proj)


def project_kernel(place_ref, mixed_ref, fixed_ref, *refs):
    parts, out_ref = (refs[:SIDE], refs[SIDE : 2 * SIDE]), refs[2 * SIDE]
    depth = fixed_ref.shape[1]
    part = parts[0][0].shape[1]
    y, x = place_ref[0], place_ref[1]
    for i in range(SIDE):
        for j in range(SIDE):
            row = lax.rem(y - i + SIDE, SIDE)
            col = lax.rem(x - j + SIDE, SIDE)
            home = row * SIDE + col
            total = jnp.dot(
                mixed_ref[:, :depth], fixed_ref[home], preferred_element_type=F32
            )
            total += jnp.dot(
                mixed_ref[:, depth : depth + part], parts[0][i][j], preferred_element_type=F32
            )
            total += jnp.dot(
                mixed_ref[:, depth + part :], parts[1][j][i], preferred_element_type=F32
            )
            out_ref[home] = total.astype(BF16)


def project(mixed, w_out_parts):
    fixed, first, second = w_out_parts
    place = lax.axis_index("seq")
    place = jnp.stack([place // SIDE, place % SIDE]).astype(jnp.int32)
    vmem = pl.BlockSpec(memory_space=pltpu.VMEM)
    return pl.pallas_call(
        project_kernel,
        out_shape=jax.ShapeDtypeStruct((SIDE * SIDE, mixed.shape[0], fixed.shape[2]), BF16),
        in_specs=[pl.BlockSpec(memory_space=pltpu.SMEM)] + [vmem] * (2 + 2 * SIDE),
        out_specs=vmem,
        compiler_params=pltpu.CompilerParams(vmem_limit_bytes=40 << 20),
        name="project",
    )(place, mixed, fixed, *first, *second)


def local(
    stream,
    mixer_in,
    gate_in,
    dt_raw,
    dt_bias,
    a_log,
    conv_weight,
    conv_bias,
    b_proj,
    c_proj,
    d_skip,
    w_out,
    expert_index,
    gate_weights,
    norm_gain,
    w_gate,
    w_up,
    w_down,
):
    tokens = mixer_in.shape[0]
    experts = lax.axis_size("exp")
    groups = lax.axis_size("seq")
    capacity = 3 * tokens // experts
    width = stream.shape[1]
    depth = w_out.shape[0] // 2
    part = depth // 2
    out_parts = (
        lax.all_gather(w_out[:depth], "seq", axis=0),
        grid_gather(w_out[depth : depth + part], "xy"),
        grid_gather(w_out[depth + part :], "yx"),
    )
    mixed = mixer(
        mixer_in, gate_in, dt_raw, dt_bias, a_log, conv_weight, conv_bias, b_proj, c_proj, d_skip
    )
    proj = project(mixed, out_parts)
    proj = proj.reshape(experts, groups // experts, tokens, -1)
    proj = lax.all_to_all(proj, "exp", split_axis=0, concat_axis=0)
    projected = jnp.sum(proj.astype(F32), axis=0).transpose(1, 0, 2).reshape(tokens, width)
    middle = (stream.astype(F32) + projected).astype(BF16)

    flat_exp = expert_index.reshape(-1)
    onehot = (flat_exp[:, None] == jnp.arange(experts, dtype=jnp.int32)[None, :]).astype(jnp.int32)
    ranks = jnp.cumsum(onehot, axis=0) - onehot
    slots = jnp.sum(ranks * onehot, axis=1)
    slot_id = (flat_exp * capacity + slots).reshape(tokens, 2)
    places = jnp.arange(experts * capacity, dtype=jnp.int32)
    chosen = (
        (slot_id[:, 0][None, :] == places[:, None]) | (slot_id[:, 1][None, :] == places[:, None])
    ).astype(BF16)
    outgoing = jnp.dot(chosen, middle, preferred_element_type=F32).astype(BF16)
    outgoing = outgoing.reshape(experts, capacity, width)
    arrived = lax.all_to_all(outgoing, "exp", split_axis=0, concat_axis=2, tiled=True)[0].astype(F32)
    mean_square = jnp.mean(arrived * arrived, axis=1, keepdims=True)
    normed = (arrived * lax.rsqrt(mean_square + 1e-05) * norm_gain[None, :]).astype(BF16)

    half = capacity // 2
    first = grid_gather(normed[:half], "xy")
    second = grid_gather(normed[half:], "yx")

    def feed(offsets):
        rows = jnp.stack([part[k] for part in (first, second) for k in offsets])
        flat = rows.reshape(-1, rows.shape[-1])
        gate_proj = jnp.dot(flat, w_gate[0], preferred_element_type=F32)
        up_proj = jnp.dot(flat, w_up[0], preferred_element_type=F32)
        hidden = lax.optimization_barrier((jax.nn.silu(gate_proj) * up_proj).astype(BF16))
        out = jnp.dot(hidden, w_down[0], preferred_element_type=F32).astype(BF16)
        return out.reshape((2, len(offsets)) + rows.shape[1:])

    fed = {}
    for offsets in ((0,), (1, 3), (2,)):
        out = feed(offsets)
        for at, k in enumerate(offsets):
            fed[k] = out[:, at]
    sums = []
    for which, order in ((0, "yx"), (1, "xy")):
        near = ring_scatter([fed[k][which] for k in range(SIDE)], order[0])
        sums.append(ring_scatter([near[k] for k in range(SIDE)], order[1]))
    summed = jnp.concatenate(sums, 0).astype(BF16)
    summed = summed.reshape(capacity, experts, width).transpose(1, 0, 2)
    returned = lax.all_to_all(summed, "exp", split_axis=0, concat_axis=0)
    returned = returned.reshape(experts * capacity, width)
    expert_sum = 0.0
    for k in range(2):
        pick = (slot_id[:, k][:, None] == places[None, :]).astype(BF16)
        picked = jnp.dot(pick, returned, preferred_element_type=F32)
        expert_sum = expert_sum + gate_weights[:, k][:, None] * picked
    return (middle.astype(F32) + expert_sum).astype(BF16)


def solution(mesh):
    return jax.shard_map(
        local,
        mesh=mesh,
        in_specs=(
            P("seq", "exp"),
            P("seq", "exp"),
            P("seq", "exp"),
            P("seq", "exp"),
            P("exp"),
            P("exp", None),
            P("exp", None),
            P("exp"),
            P("seq", None),
            P("seq", None),
            P("exp"),
            P("exp", "seq"),
            P("seq", None),
            P("seq", None),
            P(),
            P("exp", None, "seq"),
            P("exp", None, "seq"),
            P("exp", "seq", None),
        ),
        out_specs=P("seq", "exp"),
        check_vma=False,
    )
```

profile of v0, /device:TPU:1, one launch (start us, length us, event | category | flops | bytes accessed | tf_op | source)
XLA Modules:
  0.0 269.4 jit_solution(7106404521088160134)
XLA Ops:
  6.6 1.8 slice.159
  9.5 2.1 collective-permute-start.7
  11.6 2.5 collective-permute-start.8
  15.2 2.2 collective-permute-start
  19.7 4.9 %collective-permute-start.14 = (bf16[256,256]{1,0:T(8,128)(2,1)S(1)}, bf16[256,256]{1,0:T(8,128)(2,1)S(1)}, u32[]{:S(2)}, u32[]{:S(2)}) collective-permute-start(bf16[256,256]{1,0:T(8,128)(2,1)S(1)} %get-tuple-element.37), channel_id=1, source_target_pairs={{0,64},{8,72},{16,80},{24,88},{32,96},{40,104},{48,112},{56,120},{... | collective-permute-start | bytes 393224 | tf_op jit(solution)/shard_map/ppermute | solution.py:22
  24.7 4.9 %scan_state.1 = (f32[128,8,128]{2,1,0:T(8,128)S(1)}, f32[128,8,128]{2,1,0:T(8,128)S(1)}, f32[17,8,128]{2,1,0:T(8,128)S(1)}) custom-call(bf16[128,1024]{1,0:T(8,128)(2,1)S(1)} %copy-done.5, bf16[8,1024]{1,0:T(8,128)(2,1)S(1)} %collective-permute-done.rim_ref, bf16[128,1024]{1,0:T(8,128)(2,1)S(1)} %copy-done.8, f32[1,1024]{1,0:T(1,128)S(1)} %bitcast.204, ...), custom_call_target="tpu_custom_call" | custom-call | tf_op jit(solution)/shard_map/scan_state/pallas_call | solution.py:139
  31.3 2.1 collective-permute-done.1
  35.3 1.7 collective-permute-done.3
  38.2 2.3 collective-permute-start.6
  41.8 5.5 %collective-permute-done.5 = f32[17,8,128]{2,1,0:T(8,128)S(1)} collective-permute-done((f32[17,8,128]{2,1,0:T(8,128)S(1)}, f32[17,8,128]{2,1,0:T(8,128)S(1)}, u32[]{:S(2)}, u32[]{:S(2)}) %collective-permute-start.5) | collective-permute-done | bytes 69664 | tf_op jit(solution)/shard_map/ppermute | solution.py:22
  47.7 3.7 %collective-permute-start.16 = (bf16[4,256,256]{2,1,0:T(8,128)(2,1)S(1)}, bf16[4,256,256]{2,1,0:T(8,128)(2,1)S(1)}, u32[]{:S(2)}, u32[]{:S(2)}) collective-permute-start(bf16[4,256,256]{2,1,0:T(8,128)(2,1)S(1)} %pad_maximum_fusion.6.refs_4_), channel_id=1, source_target_pairs={{0,8},{8,16},{16,24},{24,0},{32,40},{40,48},{48,56},{56,32},{64,72... | collective-permute-start | bytes 1572872 | tf_op jit(solution)/shard_map/ppermute | solution.py:22
  52.2 1.6 collective-permute-start.18
  53.9 6.2 %scan_output.1.mixed_ref = bf16[128,1024]{1,0:T(8,128)(2,1)S(1)} custom-call(f32[128,8,128]{2,1,0:T(8,128)S(1)} %get-tuple-element.8.step_ref, f32[128,8,128]{2,1,0:T(8,128)S(1)} %get-tuple-element.9.act_ref, bf16[128,1024]{1,0:T(8,128)(2,1)S(1)} %copy-done.6, f32[16,8,128]{2,1,0:T(8,128)S(1)} %fusion.57.enter_ref, f32[16,8,128]{2,1,0:T(8,128)S(1)} %bitcast.202, ...), custom_call_target="tpu_custom_call" | custom-call | tf_op jit(solution)/shard_map/scan_output/pallas_call | solution.py:149
  60.1 10.6 %collective-permute-done.11.refs_2_ = bf16[4,256,256]{2,1,0:T(8,128)(2,1)S(1)} collective-permute-done((bf16[4,256,256]{2,1,0:T(8,128)(2,1)S(1)}, bf16[4,256,256]{2,1,0:T(8,128)(2,1)S(1)}, u32[]{:S(2)}, u32[]{:S(2)}) %collective-permute-start.11) | collective-permute-done | bytes 524320 | tf_op jit(solution)/shard_map/ppermute | solution.py:22
  70.7 7.9 %collective-permute-done.12.refs_3_ = bf16[4,256,256]{2,1,0:T(8,128)(2,1)S(1)} collective-permute-done((bf16[4,256,256]{2,1,0:T(8,128)(2,1)S(1)}, bf16[4,256,256]{2,1,0:T(8,128)(2,1)S(1)}, u32[]{:S(2)}, u32[]{:S(2)}) %collective-permute-start.12) | collective-permute-done | bytes 524320 | tf_op jit(solution)/shard_map/ppermute | solution.py:22
  78.7 3.1 %collective-permute-done.17.refs_6_ = bf16[4,256,256]{2,1,0:T(8,128)(2,1)S(1)} collective-permute-done((bf16[4,256,256]{2,1,0:T(8,128)(2,1)S(1)}, bf16[4,256,256]{2,1,0:T(8,128)(2,1)S(1)}, u32[]{:S(2)}, u32[]{:S(2)}) %collective-permute-start.17) | collective-permute-done | bytes 524320 | tf_op jit(solution)/shard_map/ppermute | solution.py:22
  83.4 2.2 copy-done
  87.7 2.8 %project.1 = bf16[16,128,256]{2,1,0:T(8,128)(2,1)} custom-call(s32[2]{0:T(128)S(1)} %pad_add_fusion.place_ref, bf16[128,1024]{1,0:T(8,128)(2,1)S(1)} %scan_output.1.mixed_ref, bf16[16,512,256]{2,1,0:T(8,128)(2,1)S(1)} %bitcast.200, bf16[4,256,256]{2,1,0:T(8,128)(2,1)S(1)} %pad_maximum_fusion.5.refs_0_, ...), custom_call_target="tpu_custom_call" | custom-call | tf_op jit(solution)/shard_map/project/pallas_call | solution.py:187
  90.5 13.4 %all-to-all-start = ((bf16[8,2,128,256]{3,2,1,0:T(8,128)(2,1)}), bf16[8,2,128,256]{3,2,1,0:T(8,128)(2,1)S(1)}, u32[]{:S(2)}, u32[]{:S(2)}) async-start(bf16[8,2,128,256]{3,2,1,0:T(8,128)(2,1)} %bitcast.25), calls=%async_computation | async-start | bytes 2097152 | tf_op jit(solution)/shard_map/all_to_all | solution.py:234
  105.5 13.5 %all-to-all-done = bf16[8,2,128,256]{3,2,1,0:T(8,128)(2,1)S(1)} async-done(((bf16[8,2,128,256]{3,2,1,0:T(8,128)(2,1)}), bf16[8,2,128,256]{3,2,1,0:T(8,128)(2,1)S(1)}, u32[]{:S(2)}, u32[]{:S(2)}) %all-to-all-start) | async-done | bytes 1048608 | tf_op jit(solution)/shard_map/all_to_all | solution.py:234
  119.5 11.3 %all_to_all.19 = bf16[8,48,512]{2,1,0:T(8,128)(2,1)S(1)} all-to-all(bf16[8,48,512]{2,1,0:T(8,128)(2,1)S(1)} %bitcast.221), channel_id=1, replica_groups=mesh['seq'=16,'exp'=8] {'exp'}, dimensions={0} | all-to-all | bytes 786432 | tf_op jit(solution)/shard_map/all_to_all | solution.py:249
  133.0 1.7 collective-permute-start.21
  135.4 2.0 collective-permute-start.23
  137.4 5.7 %collective-permute-done.19 = bf16[24,4096]{1,0:T(8,128)(2,1)S(1)} collective-permute-done((bf16[24,4096]{1,0:T(8,128)(2,1)S(1)}, bf16[24,4096]{1,0:T(8,128)(2,1)S(1)}, u32[]{:S(2)}, u32[]{:S(2)}) %collective-permute-start.19) | collective-permute-done | bytes 196640 | tf_op jit(solution)/shard_map/ppermute | solution.py:22
  143.0 1.7 collective-permute-start.24
  145.0 2.7 collective-permute-start.26
  147.8 2.7 collective-permute-start.28
  150.5 2.4 collective-permute-start.31
  155.8 1.4 fusion.34
  159.2 5.0 %collective-permute-done.25 = bf16[4,24,4096]{2,1,0:T(8,128)(2,1)S(1)} collective-permute-done((bf16[4,24,4096]{2,1,0:T(8,128)(2,1)S(1)}, bf16[4,24,4096]{2,1,0:T(8,128)(2,1)S(1)}, u32[]{:S(2)}, u32[]{:S(2)}) %collective-permute-start.25) | collective-permute-done | bytes 786464 | tf_op jit(solution)/shard_map/ppermute | solution.py:22
  166.3 2.6 fusion.14
  168.9 2.7 multiply_convert_fusion
  171.6 2.8 %fusion.18 = bf16[384,4096]{1,0:T(8,128)(2,1)S(1)} fusion(bf16[384,768]{1,0:T(8,128)(2,1)S(1)} %multiply_convert_fusion, bf16[1,768,4096]{2,1,0:T(8,128)(2,1)S(1)} %bitcast.253), kind=kOutput, calls=%fused_computation.18 | convolution fusion | flops 2417491968 | bytes 10027008 | tf_op jit(solution)/shard_map/dot_general | solution.py:263
  174.6 4.0 %collective-permute-start.29 = (bf16[4,24,4096]{2,1,0:T(8,128)(2,1)S(1)}, bf16[4,24,4096]{2,1,0:T(8,128)(2,1)S(1)}, u32[]{:S(2)}, u32[]{:S(2)}) collective-permute-start(bf16[4,24,4096]{2,1,0:T(8,128)(2,1)S(1)} %get-tuple-element.17), channel_id=1, source_target_pairs={{0,96},{8,104},{16,112},{24,120},{32,0},{40,8},{48,16},{56,24},{64... | collective-permute-start | bytes 2359304 | tf_op jit(solution)/shard_map/ppermute | solution.py:22
  181.1 1.4 multiply_convert_fusion.2
  184.1 3.6 %collective-permute-start.33 = (bf16[4,24,4096]{2,1,0:T(8,128)(2,1)S(1)}, bf16[4,24,4096]{2,1,0:T(8,128)(2,1)S(1)}, u32[]{:S(2)}, u32[]{:S(2)}) collective-permute-start(bf16[4,24,4096]{2,1,0:T(8,128)(2,1)S(1)} %bitcast.234), channel_id=1, source_target_pairs={{0,64},{8,72},{16,80},{24,88},{32,96},{40,104},{48,112},{56,120},{... | collective-permute-start | bytes 2359304 | tf_op jit(solution)/shard_map/ppermute | solution.py:22
  187.8 4.7 %collective-permute-start.37 = (bf16[4,24,4096]{2,1,0:T(8,128)(2,1)S(1)}, bf16[4,24,4096]{2,1,0:T(8,128)(2,1)S(1)}, u32[]{:S(2)}, u32[]{:S(2)}) collective-permute-start(bf16[4,24,4096]{2,1,0:T(8,128)(2,1)S(1)} %get-tuple-element.19), channel_id=1, source_target_pairs={{0,24},{8,0},{16,8},{24,16},{32,56},{40,32},{48,40},{56,48},{64,88... | collective-permute-start | bytes 2359304 | tf_op jit(solution)/shard_map/ppermute | solution.py:22
  192.5 4.7 %collective-permute-done.29 = bf16[4,24,4096]{2,1,0:T(8,128)(2,1)S(1)} collective-permute-done((bf16[4,24,4096]{2,1,0:T(8,128)(2,1)S(1)}, bf16[4,24,4096]{2,1,0:T(8,128)(2,1)S(1)}, u32[]{:S(2)}, u32[]{:S(2)}) %collective-permute-start.29) | collective-permute-done | bytes 786464 | tf_op jit(solution)/shard_map/ppermute | solution.py:22
  197.2 1.9 collective-permute-done.30
  199.7 2.6 collective-permute-start.34
  202.3 4.6 %collective-permute-start.35 = (bf16[24,4096]{1,0:T(8,128)(2,1)S(1)}, bf16[24,4096]{1,0:T(8,128)(2,1)S(1)}, u32[]{:S(2)}, u32[]{:S(2)}) collective-permute-start(bf16[24,4096]{1,0:T(8,128)(2,1)S(1)} %get-tuple-element.27), channel_id=1, source_target_pairs={{0,8},{8,16},{16,24},{24,0},{32,40},{40,48},{48,56},{56,32},{64,72... | collective-permute-start | bytes 589832 | tf_op jit(solution)/shard_map/ppermute | solution.py:22
  206.9 3.7 %collective-permute-done.37 = bf16[4,24,4096]{2,1,0:T(8,128)(2,1)S(1)} collective-permute-done((bf16[4,24,4096]{2,1,0:T(8,128)(2,1)S(1)}, bf16[4,24,4096]{2,1,0:T(8,128)(2,1)S(1)}, u32[]{:S(2)}, u32[]{:S(2)}) %collective-permute-start.37) | collective-permute-done | bytes 786464 | tf_op jit(solution)/shard_map/ppermute | solution.py:22
  211.6 4.0 %collective-permute-done.39 = bf16[4,24,4096]{2,1,0:T(8,128)(2,1)S(1)} collective-permute-done((bf16[4,24,4096]{2,1,0:T(8,128)(2,1)S(1)}, bf16[4,24,4096]{2,1,0:T(8,128)(2,1)S(1)}, u32[]{:S(2)}, u32[]{:S(2)}) %collective-permute-start.39) | collective-permute-done | bytes 786464 | tf_op jit(solution)/shard_map/ppermute | solution.py:22
  216.2 8.1 %collective-permute-start.41 = (bf16[24,4096]{1,0:T(8,128)(2,1)S(1)}, bf16[24,4096]{1,0:T(8,128)(2,1)S(1)}, u32[]{:S(2)}, u32[]{:S(2)}) collective-permute-start(bf16[24,4096]{1,0:T(8,128)(2,1)S(1)} %get-tuple-element.30), channel_id=1, source_target_pairs={{0,32},{8,40},{16,48},{24,56},{32,64},{40,72},{48,80},{56,88},{64,... | collective-permute-start | bytes 589832 | tf_op jit(solution)/shard_map/ppermute | solution.py:22
  224.3 3.3 %collective-permute-start.42 = (bf16[24,4096]{1,0:T(8,128)(2,1)S(1)}, bf16[24,4096]{1,0:T(8,128)(2,1)S(1)}, u32[]{:S(2)}, u32[]{:S(2)}) collective-permute-start(bf16[24,4096]{1,0:T(8,128)(2,1)S(1)} %get-tuple-element.29), channel_id=1, source_target_pairs={{0,64},{8,72},{16,80},{24,88},{32,96},{40,104},{48,112},{56,120},{... | collective-permute-start | bytes 589832 | tf_op jit(solution)/shard_map/ppermute | solution.py:22
  227.8 3.7 %collective-permute-done.42 = bf16[24,4096]{1,0:T(8,128)(2,1)S(1)} collective-permute-done((bf16[24,4096]{1,0:T(8,128)(2,1)S(1)}, bf16[24,4096]{1,0:T(8,128)(2,1)S(1)}, u32[]{:S(2)}, u32[]{:S(2)}) %collective-permute-start.42) | collective-permute-done | bytes 196640 | tf_op jit(solution)/shard_map/ppermute | solution.py:22
  232.6 20.7 %all-to-all-start.2 = ((bf16[8,48,512]{2,1,0:T(8,128)(2,1)}), bf16[8,48,512]{2,1,0:T(8,128)(2,1)S(1)}, u32[]{:S(2)}, u32[]{:S(2)}) async-start(bf16[8,48,512]{2,1,0:T(8,128)(2,1)} %copy.57), calls=%async_computation.2 | async-start | bytes 786432 | tf_op jit(solution)/shard_map/all_to_all | solution.py:277
  253.3 8.1 %all-to-all-done.2 = bf16[8,48,512]{2,1,0:T(8,128)(2,1)S(1)} async-done(((bf16[8,48,512]{2,1,0:T(8,128)(2,1)}), bf16[8,48,512]{2,1,0:T(8,128)(2,1)S(1)}, u32[]{:S(2)}, u32[]{:S(2)}) %all-to-all-start.2) | async-done | bytes 393248 | tf_op jit(solution)/shard_map/all_to_all | solution.py:277
  (172 shorter events, 36.5 us)
Async XLA Ops:
  6.6 76.8 %all-gather.3.cloned.1.call-start = ((), (), s32[]{:S(2)}) async-start(), calls=%async_computation.3 | async-start | bytes 4456448 | tf_op jit(solution)/shard_map/all_gather | solution.py:225
  9.5 20.2 %collective-permute-start.7 = (bf16[256,256]{1,0:T(8,128)(2,1)S(1)}, bf16[256,256]{1,0:T(8,128)(2,1)S(1)}, u32[]{:S(2)}, u32[]{:S(2)}) collective-permute-start(bf16[256,256]{1,0:T(8,128)(2,1)S(1)} %get-tuple-element.38), channel_id=1, source_target_pairs={{0,8},{8,16},{16,24},{24,0},{32,40},{40,48},{48,56},{56,32},{64,72... | collective-permute-start | bytes 393224 | tf_op jit(solution)/shard_map/ppermute | solution.py:22
  11.6 18.2 %collective-permute-start.8 = (bf16[256,256]{1,0:T(8,128)(2,1)S(1)}, bf16[256,256]{1,0:T(8,128)(2,1)S(1)}, u32[]{:S(2)}, u32[]{:S(2)}) collective-permute-start(bf16[256,256]{1,0:T(8,128)(2,1)S(1)} %get-tuple-element.38), channel_id=1, source_target_pairs={{0,16},{8,24},{16,0},{24,8},{32,48},{40,56},{48,32},{56,40},{64,80... | collective-permute-start | bytes 393224 | tf_op jit(solution)/shard_map/ppermute | solution.py:22
  14.0 16.0 %collective-permute-start.9 = (bf16[256,256]{1,0:T(8,128)(2,1)S(1)}, bf16[256,256]{1,0:T(8,128)(2,1)S(1)}, u32[]{:S(2)}, u32[]{:S(2)}) collective-permute-start(bf16[256,256]{1,0:T(8,128)(2,1)S(1)} %get-tuple-element.38), channel_id=1, source_target_pairs={{0,24},{8,0},{16,8},{24,16},{32,56},{40,32},{48,40},{56,48},{64,88... | collective-permute-start | bytes 393224 | tf_op jit(solution)/shard_map/ppermute | solution.py:22
  15.2 4.6 %collective-permute-start = (bf16[8,1024]{1,0:T(8,128)(2,1)S(1)}, bf16[8,1024]{1,0:T(8,128)(2,1)S(1)}, u32[]{:S(2)}, u32[]{:S(2)}) collective-permute-start(bf16[8,1024]{1,0:T(8,128)(2,1)S(1)} %slice.145), channel_id=1, source_target_pairs={{0,8},{8,16},{16,24},{24,32},{32,40},{40,48},{48,56},{56,64},{64,7... | collective-permute-start | bytes 49160 | tf_op jit(solution)/shard_map/ppermute | solution.py:134
  17.4 20.5 %collective-permute-start.13 = (bf16[256,256]{1,0:T(8,128)(2,1)S(1)}, bf16[256,256]{1,0:T(8,128)(2,1)S(1)}, u32[]{:S(2)}, u32[]{:S(2)}) collective-permute-start(bf16[256,256]{1,0:T(8,128)(2,1)S(1)} %get-tuple-element.37), channel_id=1, source_target_pairs={{0,32},{8,40},{16,48},{24,56},{32,64},{40,72},{48,80},{56,88},{64,... | collective-permute-start | bytes 393224 | tf_op jit(solution)/shard_map/ppermute | solution.py:22
  19.7 18.5 %collective-permute-start.14 = (bf16[256,256]{1,0:T(8,128)(2,1)S(1)}, bf16[256,256]{1,0:T(8,128)(2,1)S(1)}, u32[]{:S(2)}, u32[]{:S(2)}) collective-permute-start(bf16[256,256]{1,0:T(8,128)(2,1)S(1)} %get-tuple-element.37), channel_id=1, source_target_pairs={{0,64},{8,72},{16,80},{24,88},{32,96},{40,104},{48,112},{56,120},{... | collective-permute-start | bytes 393224 | tf_op jit(solution)/shard_map/ppermute | solution.py:22
  29.6 3.8 %collective-permute-start.1 = (f32[17,8,128]{2,1,0:T(8,128)S(1)}, f32[17,8,128]{2,1,0:T(8,128)S(1)}, u32[]{:S(2)}, u32[]{:S(2)}) collective-permute-start(f32[17,8,128]{2,1,0:T(8,128)S(1)} %get-tuple-element.10), channel_id=1, source_target_pairs={{0,24},{8,0},{16,8},{24,16},{32,56},{40,32},{48,40},{56,48},{64,88... | collective-permute-start | bytes 208904 | tf_op jit(solution)/shard_map/ppermute | solution.py:22
  29.7 5.0 %collective-permute-start.2 = (f32[17,8,128]{2,1,0:T(8,128)S(1)}, f32[17,8,128]{2,1,0:T(8,128)S(1)}, u32[]{:S(2)}, u32[]{:S(2)}) collective-permute-start(f32[17,8,128]{2,1,0:T(8,128)S(1)} %get-tuple-element.10), channel_id=1, source_target_pairs={{0,16},{8,24},{16,0},{24,8},{32,48},{40,56},{48,32},{56,40},{64,80... | collective-permute-start | bytes 208904 | tf_op jit(solution)/shard_map/ppermute | solution.py:22
  30.0 7.0 %collective-permute-start.3 = (f32[17,8,128]{2,1,0:T(8,128)S(1)}, f32[17,8,128]{2,1,0:T(8,128)S(1)}, u32[]{:S(2)}, u32[]{:S(2)}) collective-permute-start(f32[17,8,128]{2,1,0:T(8,128)S(1)} %get-tuple-element.10), channel_id=1, source_target_pairs={{0,8},{8,16},{16,24},{24,0},{32,40},{40,48},{48,56},{56,32},{64,72... | collective-permute-start | bytes 208904 | tf_op jit(solution)/shard_map/ppermute | solution.py:22
  31.3 22.7 %copy-start.7 = (f32[128,16]{1,0:T(8,128)S(1)}, f32[128,16]{1,0:T(8,128)}, u32[]{:S(2)}) copy-start(f32[128,16]{1,0:T(8,128)} %copy.51.c_ref) | copy-start | bytes 24580
  31.3 22.7 %copy-start.12 = (f32[1024]{0:T(1024)S(1)}, f32[1024]{0:T(1024)}, u32[]{:S(2)}) copy-start(f32[1024]{0:T(1024)} %param.28) | copy-start | bytes 12292
  33.4 7.1 %collective-permute-start.15 = (bf16[256,256]{1,0:T(8,128)(2,1)S(1)}, bf16[256,256]{1,0:T(8,128)(2,1)S(1)}, u32[]{:S(2)}, u32[]{:S(2)}) collective-permute-start(bf16[256,256]{1,0:T(8,128)(2,1)S(1)} %get-tuple-element.37), channel_id=1, source_target_pairs={{0,96},{8,104},{16,112},{24,120},{32,0},{40,8},{48,16},{56,24},{64... | collective-permute-start | bytes 393224 | tf_op jit(solution)/shard_map/ppermute | solution.py:22
  34.7 17.5 %collective-permute-start.10 = (bf16[4,256,256]{2,1,0:T(8,128)(2,1)S(1)}, bf16[4,256,256]{2,1,0:T(8,128)(2,1)S(1)}, u32[]{:S(2)}, u32[]{:S(2)}) collective-permute-start(bf16[4,256,256]{2,1,0:T(8,128)(2,1)S(1)} %pad_maximum_fusion.5.refs_0_), channel_id=1, source_target_pairs={{0,32},{8,40},{16,48},{24,56},{32,64},{40,72},{48,80},{56,88},{64,... | collective-permute-start | bytes 1572872 | tf_op jit(solution)/shard_map/ppermute | solution.py:22
  37.2 10.1 %collective-permute-start.5 = (f32[17,8,128]{2,1,0:T(8,128)S(1)}, f32[17,8,128]{2,1,0:T(8,128)S(1)}, u32[]{:S(2)}, u32[]{:S(2)}) collective-permute-start(f32[17,8,128]{2,1,0:T(8,128)S(1)} %pad_maximum_fusion.7), channel_id=1, source_target_pairs={{0,64},{8,72},{16,80},{24,88},{32,96},{40,104},{48,112},{56,120},{... | collective-permute-start | bytes 208904 | tf_op jit(solution)/shard_map/ppermute | solution.py:22
  37.9 9.8 %collective-permute-start.4 = (f32[17,8,128]{2,1,0:T(8,128)S(1)}, f32[17,8,128]{2,1,0:T(8,128)S(1)}, u32[]{:S(2)}, u32[]{:S(2)}) collective-permute-start(f32[17,8,128]{2,1,0:T(8,128)S(1)} %pad_maximum_fusion.7), channel_id=1, source_target_pairs={{0,32},{8,40},{16,48},{24,56},{32,64},{40,72},{48,80},{56,88},{64,... | collective-permute-start | bytes 208904 | tf_op jit(solution)/shard_map/ppermute | solution.py:22
  38.2 13.2 %collective-permute-start.6 = (f32[17,8,128]{2,1,0:T(8,128)S(1)}, f32[17,8,128]{2,1,0:T(8,128)S(1)}, u32[]{:S(2)}, u32[]{:S(2)}) collective-permute-start(f32[17,8,128]{2,1,0:T(8,128)S(1)} %pad_maximum_fusion.7), channel_id=1, source_target_pairs={{0,96},{8,104},{16,112},{24,120},{32,0},{40,8},{48,16},{56,24},{64... | collective-permute-start | bytes 208904 | tf_op jit(solution)/shard_map/ppermute | solution.py:22
  40.6 30.1 %collective-permute-start.11 = (bf16[4,256,256]{2,1,0:T(8,128)(2,1)S(1)}, bf16[4,256,256]{2,1,0:T(8,128)(2,1)S(1)}, u32[]{:S(2)}, u32[]{:S(2)}) collective-permute-start(bf16[4,256,256]{2,1,0:T(8,128)(2,1)S(1)} %pad_maximum_fusion.5.refs_0_), channel_id=1, source_target_pairs={{0,64},{8,72},{16,80},{24,88},{32,96},{40,104},{48,112},{56,120},{... | collective-permute-start | bytes 1572872 | tf_op jit(solution)/shard_map/ppermute | solution.py:22
  47.3 31.4 %collective-permute-start.12 = (bf16[4,256,256]{2,1,0:T(8,128)(2,1)S(1)}, bf16[4,256,256]{2,1,0:T(8,128)(2,1)S(1)}, u32[]{:S(2)}, u32[]{:S(2)}) collective-permute-start(bf16[4,256,256]{2,1,0:T(8,128)(2,1)S(1)} %pad_maximum_fusion.5.refs_0_), channel_id=1, source_target_pairs={{0,96},{8,104},{16,112},{24,120},{32,0},{40,8},{48,16},{56,24},{64... | collective-permute-start | bytes 1572872 | tf_op jit(solution)/shard_map/ppermute | solution.py:22
  47.7 31.0 %collective-permute-start.16 = (bf16[4,256,256]{2,1,0:T(8,128)(2,1)S(1)}, bf16[4,256,256]{2,1,0:T(8,128)(2,1)S(1)}, u32[]{:S(2)}, u32[]{:S(2)}) collective-permute-start(bf16[4,256,256]{2,1,0:T(8,128)(2,1)S(1)} %pad_maximum_fusion.6.refs_4_), channel_id=1, source_target_pairs={{0,8},{8,16},{16,24},{24,0},{32,40},{40,48},{48,56},{56,32},{64,72... | collective-permute-start | bytes 1572872 | tf_op jit(solution)/shard_map/ppermute | solution.py:22
  51.4 30.4 %collective-permute-start.17 = (bf16[4,256,256]{2,1,0:T(8,128)(2,1)S(1)}, bf16[4,256,256]{2,1,0:T(8,128)(2,1)S(1)}, u32[]{:S(2)}, u32[]{:S(2)}) collective-permute-start(bf16[4,256,256]{2,1,0:T(8,128)(2,1)S(1)} %pad_maximum_fusion.6.refs_4_), channel_id=1, source_target_pairs={{0,16},{8,24},{16,0},{24,8},{32,48},{40,56},{48,32},{56,40},{64,80... | collective-permute-start | bytes 1572872 | tf_op jit(solution)/shard_map/ppermute | solution.py:22
  52.2 30.4 %collective-permute-start.18 = (bf16[4,256,256]{2,1,0:T(8,128)(2,1)S(1)}, bf16[4,256,256]{2,1,0:T(8,128)(2,1)S(1)}, u32[]{:S(2)}, u32[]{:S(2)}) collective-permute-start(bf16[4,256,256]{2,1,0:T(8,128)(2,1)S(1)} %pad_maximum_fusion.6.refs_4_), channel_id=1, source_target_pairs={{0,24},{8,0},{16,8},{24,16},{32,56},{40,32},{48,40},{56,48},{64,88... | collective-permute-start | bytes 1572872 | tf_op jit(solution)/shard_map/ppermute | solution.py:22
  90.5 28.5 %all-to-all-start = ((bf16[8,2,128,256]{3,2,1,0:T(8,128)(2,1)}), bf16[8,2,128,256]{3,2,1,0:T(8,128)(2,1)S(1)}, u32[]{:S(2)}, u32[]{:S(2)}) async-start(bf16[8,2,128,256]{3,2,1,0:T(8,128)(2,1)} %bitcast.25), calls=%async_computation | async-start | bytes 2097152 | tf_op jit(solution)/shard_map/all_to_all | solution.py:234
  131.7 11.3 %collective-permute-start.19 = (bf16[24,4096]{1,0:T(8,128)(2,1)S(1)}, bf16[24,4096]{1,0:T(8,128)(2,1)S(1)}, u32[]{:S(2)}, u32[]{:S(2)}) collective-permute-start(bf16[24,4096]{1,0:T(8,128)(2,1)S(1)} %get-tuple-element.42), channel_id=1, source_target_pairs={{0,8},{8,16},{16,24},{24,0},{32,40},{40,48},{48,56},{56,32},{64,72... | collective-permute-start | bytes 589832 | tf_op jit(solution)/shard_map/ppermute | solution.py:22
  132.0 12.7 %collective-permute-start.20 = (bf16[24,4096]{1,0:T(8,128)(2,1)S(1)}, bf16[24,4096]{1,0:T(8,128)(2,1)S(1)}, u32[]{:S(2)}, u32[]{:S(2)}) collective-permute-start(bf16[24,4096]{1,0:T(8,128)(2,1)S(1)} %get-tuple-element.42), channel_id=1, source_target_pairs={{0,16},{8,24},{16,0},{24,8},{32,48},{40,56},{48,32},{56,40},{64,80... | collective-permute-start | bytes 589832 | tf_op jit(solution)/shard_map/ppermute | solution.py:22
  133.0 11.8 %collective-permute-start.21 = (bf16[24,4096]{1,0:T(8,128)(2,1)S(1)}, bf16[24,4096]{1,0:T(8,128)(2,1)S(1)}, u32[]{:S(2)}, u32[]{:S(2)}) collective-permute-start(bf16[24,4096]{1,0:T(8,128)(2,1)S(1)} %get-tuple-element.42), channel_id=1, source_target_pairs={{0,24},{8,0},{16,8},{24,16},{32,56},{40,32},{48,40},{56,48},{64,88... | collective-permute-start | bytes 589832 | tf_op jit(solution)/shard_map/ppermute | solution.py:22
  134.7 13.0 %collective-permute-start.22 = (bf16[24,4096]{1,0:T(8,128)(2,1)S(1)}, bf16[24,4096]{1,0:T(8,128)(2,1)S(1)}, u32[]{:S(2)}, u32[]{:S(2)}) collective-permute-start(bf16[24,4096]{1,0:T(8,128)(2,1)S(1)} %get-tuple-element.41), channel_id=1, source_target_pairs={{0,32},{8,40},{16,48},{24,56},{32,64},{40,72},{48,80},{56,88},{64,... | collective-permute-start | bytes 589832 | tf_op jit(solution)/shard_map/ppermute | solution.py:22
  135.4 12.2 %collective-permute-start.23 = (bf16[24,4096]{1,0:T(8,128)(2,1)S(1)}, bf16[24,4096]{1,0:T(8,128)(2,1)S(1)}, u32[]{:S(2)}, u32[]{:S(2)}) collective-permute-start(bf16[24,4096]{1,0:T(8,128)(2,1)S(1)} %get-tuple-element.41), channel_id=1, source_target_pairs={{0,64},{8,72},{16,80},{24,88},{32,96},{40,104},{48,112},{56,120},{... | collective-permute-start | bytes 589832 | tf_op jit(solution)/shard_map/ppermute | solution.py:22
  143.0 4.6 %collective-permute-start.24 = (bf16[24,4096]{1,0:T(8,128)(2,1)S(1)}, bf16[24,4096]{1,0:T(8,128)(2,1)S(1)}, u32[]{:S(2)}, u32[]{:S(2)}) collective-permute-start(bf16[24,4096]{1,0:T(8,128)(2,1)S(1)} %get-tuple-element.41), channel_id=1, source_target_pairs={{0,96},{8,104},{16,112},{24,120},{32,0},{40,8},{48,16},{56,24},{64... | collective-permute-start | bytes 589832 | tf_op jit(solution)/shard_map/ppermute | solution.py:22
  144.9 19.3 %collective-permute-start.25 = (bf16[4,24,4096]{2,1,0:T(8,128)(2,1)S(1)}, bf16[4,24,4096]{2,1,0:T(8,128)(2,1)S(1)}, u32[]{:S(2)}, u32[]{:S(2)}) collective-permute-start(bf16[4,24,4096]{2,1,0:T(8,128)(2,1)S(1)} %get-tuple-element.32), channel_id=1, source_target_pairs={{0,32},{8,40},{16,48},{24,56},{32,64},{40,72},{48,80},{56,88},{64,... | collective-permute-start | bytes 2359304 | tf_op jit(solution)/shard_map/ppermute | solution.py:22
  145.0 20.9 %collective-permute-start.26 = (bf16[4,24,4096]{2,1,0:T(8,128)(2,1)S(1)}, bf16[4,24,4096]{2,1,0:T(8,128)(2,1)S(1)}, u32[]{:S(2)}, u32[]{:S(2)}) collective-permute-start(bf16[4,24,4096]{2,1,0:T(8,128)(2,1)S(1)} %get-tuple-element.32), channel_id=1, source_target_pairs={{0,96},{8,104},{16,112},{24,120},{32,0},{40,8},{48,16},{56,24},{64... | collective-permute-start | bytes 2359304 | tf_op jit(solution)/shard_map/ppermute | solution.py:22
  147.8 18.1 %collective-permute-start.27 = (bf16[4,24,4096]{2,1,0:T(8,128)(2,1)S(1)}, bf16[4,24,4096]{2,1,0:T(8,128)(2,1)S(1)}, u32[]{:S(2)}, u32[]{:S(2)}) collective-permute-start(bf16[4,24,4096]{2,1,0:T(8,128)(2,1)S(1)} %get-tuple-element.34), channel_id=1, source_target_pairs={{0,8},{8,16},{16,24},{24,0},{32,40},{40,48},{48,56},{56,32},{64,72... | collective-permute-start | bytes 2359304 | tf_op jit(solution)/shard_map/ppermute | solution.py:22
  147.8 18.0 %collective-permute-start.28 = (bf16[4,24,4096]{2,1,0:T(8,128)(2,1)S(1)}, bf16[4,24,4096]{2,1,0:T(8,128)(2,1)S(1)}, u32[]{:S(2)}, u32[]{:S(2)}) collective-permute-start(bf16[4,24,4096]{2,1,0:T(8,128)(2,1)S(1)} %get-tuple-element.34), channel_id=1, source_target_pairs={{0,24},{8,0},{16,8},{24,16},{32,56},{40,32},{48,40},{56,48},{64,88... | collective-permute-start | bytes 2359304 | tf_op jit(solution)/shard_map/ppermute | solution.py:22
  150.5 29.0 %collective-permute-start.31 = (bf16[4,24,4096]{2,1,0:T(8,128)(2,1)S(1)}, bf16[4,24,4096]{2,1,0:T(8,128)(2,1)S(1)}, u32[]{:S(2)}, u32[]{:S(2)}) collective-permute-start(bf16[4,24,4096]{2,1,0:T(8,128)(2,1)S(1)} %get-tuple-element.32), channel_id=1, source_target_pairs={{0,64},{8,72},{16,80},{24,88},{32,96},{40,104},{48,112},{56,120},{... | collective-permute-start | bytes 2359304 | tf_op jit(solution)/shard_map/ppermute | solution.py:22
  164.2 15.3 %collective-permute-start.32 = (bf16[4,24,4096]{2,1,0:T(8,128)(2,1)S(1)}, bf16[4,24,4096]{2,1,0:T(8,128)(2,1)S(1)}, u32[]{:S(2)}, u32[]{:S(2)}) collective-permute-start(bf16[4,24,4096]{2,1,0:T(8,128)(2,1)S(1)} %get-tuple-element.34), channel_id=1, source_target_pairs={{0,16},{8,24},{16,0},{24,8},{32,48},{40,56},{48,32},{56,40},{64,80... | collective-permute-start | bytes 2359304 | tf_op jit(solution)/shard_map/ppermute | solution.py:22
  174.6 22.6 %collective-permute-start.29 = (bf16[4,24,4096]{2,1,0:T(8,128)(2,1)S(1)}, bf16[4,24,4096]{2,1,0:T(8,128)(2,1)S(1)}, u32[]{:S(2)}, u32[]{:S(2)}) collective-permute-start(bf16[4,24,4096]{2,1,0:T(8,128)(2,1)S(1)} %get-tuple-element.17), channel_id=1, source_target_pairs={{0,96},{8,104},{16,112},{24,120},{32,0},{40,8},{48,16},{56,24},{64... | collective-permute-start | bytes 2359304 | tf_op jit(solution)/shard_map/ppermute | solution.py:22
  178.6 20.5 %collective-permute-start.30 = (bf16[4,24,4096]{2,1,0:T(8,128)(2,1)S(1)}, bf16[4,24,4096]{2,1,0:T(8,128)(2,1)S(1)}, u32[]{:S(2)}, u32[]{:S(2)}) collective-permute-start(bf16[4,24,4096]{2,1,0:T(8,128)(2,1)S(1)} %get-tuple-element.20), channel_id=1, source_target_pairs={{0,32},{8,40},{16,48},{24,56},{32,64},{40,72},{48,80},{56,88},{64,... | collective-permute-start | bytes 2359304 | tf_op jit(solution)/shard_map/ppermute | solution.py:22
  184.1 15.0 %collective-permute-start.33 = (bf16[4,24,4096]{2,1,0:T(8,128)(2,1)S(1)}, bf16[4,24,4096]{2,1,0:T(8,128)(2,1)S(1)}, u32[]{:S(2)}, u32[]{:S(2)}) collective-permute-start(bf16[4,24,4096]{2,1,0:T(8,128)(2,1)S(1)} %bitcast.234), channel_id=1, source_target_pairs={{0,64},{8,72},{16,80},{24,88},{32,96},{40,104},{48,112},{56,120},{... | collective-permute-start | bytes 2359304 | tf_op jit(solution)/shard_map/ppermute | solution.py:22
  187.8 22.8 %collective-permute-start.37 = (bf16[4,24,4096]{2,1,0:T(8,128)(2,1)S(1)}, bf16[4,24,4096]{2,1,0:T(8,128)(2,1)S(1)}, u32[]{:S(2)}, u32[]{:S(2)}) collective-permute-start(bf16[4,24,4096]{2,1,0:T(8,128)(2,1)S(1)} %get-tuple-element.19), channel_id=1, source_target_pairs={{0,24},{8,0},{16,8},{24,16},{32,56},{40,32},{48,40},{56,48},{64,88... | collective-permute-start | bytes 2359304 | tf_op jit(solution)/shard_map/ppermute | solution.py:22
  192.5 19.1 %collective-permute-start.38 = (bf16[4,24,4096]{2,1,0:T(8,128)(2,1)S(1)}, bf16[4,24,4096]{2,1,0:T(8,128)(2,1)S(1)}, u32[]{:S(2)}, u32[]{:S(2)}) collective-permute-start(bf16[4,24,4096]{2,1,0:T(8,128)(2,1)S(1)} %get-tuple-element.18), channel_id=1, source_target_pairs={{0,8},{8,16},{16,24},{24,0},{32,40},{40,48},{48,56},{56,32},{64,72... | collective-permute-start | bytes 2359304 | tf_op jit(solution)/shard_map/ppermute | solution.py:22
  197.2 18.4 %collective-permute-start.39 = (bf16[4,24,4096]{2,1,0:T(8,128)(2,1)S(1)}, bf16[4,24,4096]{2,1,0:T(8,128)(2,1)S(1)}, u32[]{:S(2)}, u32[]{:S(2)}) collective-permute-start(bf16[4,24,4096]{2,1,0:T(8,128)(2,1)S(1)} %bitcast.231), channel_id=1, source_target_pairs={{0,16},{8,24},{16,0},{24,8},{32,48},{40,56},{48,32},{56,40},{64,80... | collective-permute-start | bytes 2359304 | tf_op jit(solution)/shard_map/ppermute | solution.py:22
  199.7 24.7 %collective-permute-start.34 = (bf16[24,4096]{1,0:T(8,128)(2,1)S(1)}, bf16[24,4096]{1,0:T(8,128)(2,1)S(1)}, u32[]{:S(2)}, u32[]{:S(2)}) collective-permute-start(bf16[24,4096]{1,0:T(8,128)(2,1)S(1)} %get-tuple-element.25), channel_id=1, source_target_pairs={{0,24},{8,0},{16,8},{24,16},{32,56},{40,32},{48,40},{56,48},{64,88... | collective-permute-start | bytes 589832 | tf_op jit(solution)/shard_map/ppermute | solution.py:22
  202.3 25.3 %collective-permute-start.35 = (bf16[24,4096]{1,0:T(8,128)(2,1)S(1)}, bf16[24,4096]{1,0:T(8,128)(2,1)S(1)}, u32[]{:S(2)}, u32[]{:S(2)}) collective-permute-start(bf16[24,4096]{1,0:T(8,128)(2,1)S(1)} %get-tuple-element.27), channel_id=1, source_target_pairs={{0,8},{8,16},{16,24},{24,0},{32,40},{40,48},{48,56},{56,32},{64,72... | collective-permute-start | bytes 589832 | tf_op jit(solution)/shard_map/ppermute | solution.py:22
  210.6 17.0 %collective-permute-start.36 = (bf16[24,4096]{1,0:T(8,128)(2,1)S(1)}, bf16[24,4096]{1,0:T(8,128)(2,1)S(1)}, u32[]{:S(2)}, u32[]{:S(2)}) collective-permute-start(bf16[24,4096]{1,0:T(8,128)(2,1)S(1)} %get-tuple-element.26), channel_id=1, source_target_pairs={{0,16},{8,24},{16,0},{24,8},{32,48},{40,56},{48,32},{56,40},{64,80... | collective-permute-start | bytes 589832 | tf_op jit(solution)/shard_map/ppermute | solution.py:22
  216.2 11.6 %collective-permute-start.40 = (bf16[24,4096]{1,0:T(8,128)(2,1)S(1)}, bf16[24,4096]{1,0:T(8,128)(2,1)S(1)}, u32[]{:S(2)}, u32[]{:S(2)}) collective-permute-start(bf16[24,4096]{1,0:T(8,128)(2,1)S(1)} %get-tuple-element.28), channel_id=1, source_target_pairs={{0,96},{8,104},{16,112},{24,120},{32,0},{40,8},{48,16},{56,24},{64... | collective-permute-start | bytes 589832 | tf_op jit(solution)/shard_map/ppermute | solution.py:22
  216.2 11.6 %collective-permute-start.41 = (bf16[24,4096]{1,0:T(8,128)(2,1)S(1)}, bf16[24,4096]{1,0:T(8,128)(2,1)S(1)}, u32[]{:S(2)}, u32[]{:S(2)}) collective-permute-start(bf16[24,4096]{1,0:T(8,128)(2,1)S(1)} %get-tuple-element.30), channel_id=1, source_target_pairs={{0,32},{8,40},{16,48},{24,56},{32,64},{40,72},{48,80},{56,88},{64,... | collective-permute-start | bytes 589832 | tf_op jit(solution)/shard_map/ppermute | solution.py:22
  224.3 7.2 %collective-permute-start.42 = (bf16[24,4096]{1,0:T(8,128)(2,1)S(1)}, bf16[24,4096]{1,0:T(8,128)(2,1)S(1)}, u32[]{:S(2)}, u32[]{:S(2)}) collective-permute-start(bf16[24,4096]{1,0:T(8,128)(2,1)S(1)} %get-tuple-element.29), channel_id=1, source_target_pairs={{0,64},{8,72},{16,80},{24,88},{32,96},{40,104},{48,112},{56,120},{... | collective-permute-start | bytes 589832 | tf_op jit(solution)/shard_map/ppermute | solution.py:22
  232.6 28.8 %all-to-all-start.2 = ((bf16[8,48,512]{2,1,0:T(8,128)(2,1)}), bf16[8,48,512]{2,1,0:T(8,128)(2,1)S(1)}, u32[]{:S(2)}, u32[]{:S(2)}) async-start(bf16[8,48,512]{2,1,0:T(8,128)(2,1)} %copy.57), calls=%async_computation.2 | async-start | bytes 786432 | tf_op jit(solution)/shard_map/all_to_all | solution.py:277
  (24 other events, 239.3 us)
Sparse Core Ops, SparseCore 0:
  9.6 73.2 all-gather.2
where the time goes:
time: 271 us; the launch traced here: 269 us
  starting transfers between devices  109 us (40%)
  waiting for transfers between devices  84.8 us (31%)
  matrix products  18.2 us (7%)
  local copies, waits for them, and re-layouts  14.3 us (5%)
  Pallas kernels  14 us (5%)
  between operations  14 us (5%)
  blocking collectives  11.3 us (4%)
  other arithmetic  3.95 us (1%)
    ppermute x42, starting transfers between devices, shift(): return lax.ppermute(value, 'seq', route)  72.7 us
    ppermute x42, waiting for transfers between devices, shift(): return lax.ppermute(value, 'seq', route)  63.2 us
    all_to_all x1, starting transfers between devices, local(): returned = lax.all_to_all(summed, 'exp', split_axis=0, concat_axis=0)  20.7 us
    all_to_all x1, waiting for transfers between devices, local(): proj = lax.all_to_all(proj, 'exp', split_axis=0, concat_axis=0)  13.5 us
    all_to_all x1, starting transfers between devices, local(): proj = lax.all_to_all(proj, 'exp', split_axis=0, concat_axis=0)  13.4 us
    all_to_all x1, blocking collectives, local(): lax.all_to_all(outgoing, 'exp', split_axis=0, concat_axis=2, tiled=True)[0]  11.3 us
    unnamed x59, local copies, waits for them, and re-layouts  9.26 us
    all_to_all x1, waiting for transfers between devices, local(): returned = lax.all_to_all(summed, 'exp', split_axis=0, concat_axis=0)  8.09 us
  transfers between devices with their start and end apart: 46, of which 20 were waited for; matrix products, arithmetic and copies ran while one was open for 9% of the time, Pallas kernels for 4%

commit v1 on v0

--- a/solution.py
+++ b/solution.py
@@ -20,6 +20,22 @@
     else:
         route = [(y * SIDE + x, (y + distance) % SIDE * SIDE + x) for y, x in cells]
     return lax.ppermute(value, "seq", route)
+
+
+def keeper_shift(value, axis, distance):
+    route = []
+    for y in range(SIDE):
+        for x in range(SIDE):
+            for z in range(SIDE):
+                start = [y, x, z, x // 2]
+                end = [y, x, z, x // 2]
+                if axis == "core":
+                    start[3] = 1 - start[3]
+                else:
+                    at = "yxz".index(axis)
+                    end[at] = (end[at] + distance) % SIDE
+                route.append(tuple((v[0] * SIDE + v[1]) * 2 * SIDE + v[2] * 2 + v[3] for v in (start, end)))
+    return lax.ppermute(value, ("seq", "exp"), route)
 
 
 def ring_gather(block, axis):
@@ -157,41 +173,42 @@
     )(step, act, gate_in, enter, rate, d_skip.reshape(8, 128), b_proj, c_proj)
 
 
-def project_kernel(place_ref, mixed_ref, fixed_ref, *refs):
-    parts, out_ref = (refs[:SIDE], refs[SIDE : 2 * SIDE]), refs[2 * SIDE]
-    depth = fixed_ref.shape[1]
-    part = parts[0][0].shape[1]
-    y, x = place_ref[0], place_ref[1]
+def project_kernel(place_ref, *refs):
+    rows, columns, out_ref = refs[:SIDE], refs[SIDE : 2 * SIDE], refs[2 * SIDE]
+    y, z = place_ref[0], place_ref[1]
     for i in range(SIDE):
+        far = lax.rem(y - i - z + 2 * SIDE, SIDE)
         for j in range(SIDE):
-            row = lax.rem(y - i + SIDE, SIDE)
-            col = lax.rem(x - j + SIDE, SIDE)
-            home = row * SIDE + col
-            total = jnp.dot(
-                mixed_ref[:, :depth], fixed_ref[home], preferred_element_type=F32
-            )
-            total += jnp.dot(
-                mixed_ref[:, depth : depth + part], parts[0][i][j], preferred_element_type=F32
-            )
-            total += jnp.dot(
-                mixed_ref[:, depth + part :], parts[1][j][i], preferred_element_type=F32
-            )
-            out_ref[home] = total.astype(BF16)
-
-
-def project(mixed, w_out_parts):
-    fixed, first, second = w_out_parts
-    place = lax.axis_index("seq")
-    place = jnp.stack([place // SIDE, place % SIDE]).astype(jnp.int32)
+            out_ref[far, j] = jnp.dot(
+                rows[j][...], columns[i][...], preferred_element_type=F32
+            ).astype(BF16)
+
+
+def project(mixed, w_out_blocks):
+    rows = ring_gather(mixed, "x")
+    place = jnp.stack([lax.axis_index("seq") // SIDE, lax.axis_index("exp") // 2]).astype(jnp.int32)
     vmem = pl.BlockSpec(memory_space=pltpu.VMEM)
-    return pl.pallas_call(
+    tokens, columns = mixed.shape[0], w_out_blocks[0].shape[1]
+    partial = pl.pallas_call(
         project_kernel,
-        out_shape=jax.ShapeDtypeStruct((SIDE * SIDE, mixed.shape[0], fixed.shape[2]), BF16),
-        in_specs=[pl.BlockSpec(memory_space=pltpu.SMEM)] + [vmem] * (2 + 2 * SIDE),
+        out_shape=jax.ShapeDtypeStruct((SIDE, SIDE, tokens, columns), BF16),
+        in_specs=[pl.BlockSpec(memory_space=pltpu.SMEM)] + [vmem] * (2 * SIDE),
         out_specs=vmem,
         compiler_params=pltpu.CompilerParams(vmem_limit_bytes=40 << 20),
         name="project",
-    )(place, mixed, fixed, *first, *second)
+    )(place, *rows, *w_out_blocks)
+    total = partial.astype(F32) + keeper_shift(partial, "core", 0).astype(F32)
+    near = total[0]
+    for d in range(1, SIDE):
+        near = near + keeper_shift(total[d].astype(BF16), "z", d).astype(F32)
+    x, core = lax.axis_index("seq") % SIDE, lax.axis_index("exp") % 2
+    near = near.astype(BF16)
+    got = [jnp.where(core == x // 2, near[0], jnp.zeros_like(near[0]))]
+    got += [keeper_shift(near[k], "x", -k) for k in range(1, SIDE)]
+    even, odd = got[0] + got[2], got[1] + got[3]
+    return jnp.concatenate(
+        [jnp.where(x % 2 == 0, even, odd), jnp.where(x % 2 == 0, odd, even)], axis=1
+    ).astype(F32)
 
 
 def local(
@@ -219,20 +236,11 @@
     groups = lax.axis_size("seq")
     capacity = 3 * tokens // experts
     width = stream.shape[1]
-    depth = w_out.shape[0] // 2
-    part = depth // 2
-    out_parts = (
-        lax.all_gather(w_out[:depth], "seq", axis=0),
-        grid_gather(w_out[depth : depth + part], "xy"),
-        grid_gather(w_out[depth + part :], "yx"),
-    )
+    out_blocks = ring_gather(w_out, "y")
     mixed = mixer(
         mixer_in, gate_in, dt_raw, dt_bias, a_log, conv_weight, conv_bias, b_proj, c_proj, d_skip
     )
-    proj = project(mixed, out_parts)
-    proj = proj.reshape(experts, groups // experts, tokens, -1)
-    proj = lax.all_to_all(proj, "exp", split_axis=0, concat_axis=0)
-    projected = jnp.sum(proj.astype(F32), axis=0).transpose(1, 0, 2).reshape(tokens, width)
+    projected = project(mixed, out_blocks)
     middle = (stream.astype(F32) + projected).astype(BF16)
 
     flat_exp = expert_index.reshape(-1)

time: 271 us -> 252 us (0.930)
  starting transfers between devices: 109 us -> 95 us
  between operations: 14 us -> 0.63 us
  other arithmetic: 3.95 us -> 7.17 us
    ppermute x0 -> x7, waiting for transfers between devices: none -> 18.3 us  [keeper_shift(): return lax.ppermute(value, ('seq', 'exp'), route)]
    all_to_all x1 -> x0, waiting for transfers between devices: 13.5 us -> none  [local(): proj = lax.all_to_all(proj, 'exp', split_axis=0, concat_axis=0)]
    all_to_all x1 -> x0, starting transfers between devices: 13.4 us -> none  [local(): proj = lax.all_to_all(proj, 'exp', split_axis=0, concat_axis=0)]
    ppermute x42 -> x36, starting transfers between devices: 72.7 us -> 61.3 us  [shift(): return lax.ppermute(value, 'seq', route)]
    ppermute x0 -> x7, starting transfers between devices: none -> 11 us  [keeper_shift(): return lax.ppermute(value, ('seq', 'exp'), route)]
    unnamed x59 -> x55, local copies, waits for them, and re-layouts: 9.26 us -> 12.7 us
    ppermute x42 -> x36, waiting for transfers between devices: 63.2 us -> 60.8 us  [shift(): return lax.ppermute(value, 'seq', route)]
  transfers between devices with their start and end apart: 46 -> 45, of which waited for: 20 -> 21; matrix products, arithmetic and copies ran while one was open for 9% -> 9% of each run, Pallas kernels for 4% -> 0%
where the time goes in v1:
time: 252 us; the launch traced here: 251 us
  starting transfers between devices  95 us (38%)
  waiting for transfers between devices  87.2 us (35%)
  matrix products  18.2 us (7%)
  local copies, waits for them, and re-layouts  16.4 us (7%)
  blocking collectives  13.9 us (6%)
  Pallas kernels  12.9 us (5%)
  other arithmetic  7.17 us (3%)
    ppermute x36, starting transfers between devices, shift(): return lax.ppermute(value, 'seq', route)  61.3 us
    ppermute x36, waiting for transfers between devices, shift(): return lax.ppermute(value, 'seq', route)  60.8 us
    all_to_all x1, starting transfers between devices, local(): returned = lax.all_to_all(summed, 'exp', split_axis=0, concat_axis=0)  18.6 us
    ppermute x7, waiting for transfers between devices, keeper_shift(): return lax.ppermute(value, ('seq', 'exp'), route)  18.3 us
    all_to_all x1, blocking collectives, local(): lax.all_to_all(outgoing, 'exp', split_axis=0, concat_axis=2, tiled=True)[0]  13.9 us
    unnamed x55, local copies, waits for them, and re-layouts  12.7 us
    ppermute x7, starting transfers between devices, keeper_shift(): return lax.ppermute(value, ('seq', 'exp'), route)  11 us
    all_to_all x1, waiting for transfers between devices, local(): returned = lax.all_to_all(summed, 'exp', split_axis=0, concat_axis=0)  8.09 us
  transfers between devices with their start and end apart: 45, of which 21 were waited for; matrix products, arithmetic and copies ran while one was open for 9% of the time, Pallas kernels for 0%

profile of v1, /device:TPU:1, one launch (start us, length us, event | category | flops | bytes accessed | tf_op | source)
XLA Modules:
  0.0 251.4 jit_solution(2326019881952662096)
XLA Ops:
  0.7 4.1 %collective-permute-start = (bf16[8,1024]{1,0:T(8,128)(2,1)S(1)}, bf16[8,1024]{1,0:T(8,128)(2,1)S(1)}, u32[]{:S(2)}, u32[]{:S(2)}) collective-permute-start(bf16[8,1024]{1,0:T(8,128)(2,1)S(1)} %slice.163), channel_id=1, source_target_pairs={{0,8},{8,16},{16,24},{24,32},{32,40},{40,48},{48,56},{56,64},{64,7... | collective-permute-start | bytes 49160 | tf_op jit(solution)/shard_map/ppermute | solution.py:150
  10.5 4.9 %scan_state.1 = (f32[128,8,128]{2,1,0:T(8,128)S(1)}, f32[128,8,128]{2,1,0:T(8,128)S(1)}, f32[17,8,128]{2,1,0:T(8,128)S(1)}) custom-call(bf16[128,1024]{1,0:T(8,128)(2,1)S(1)} %copy-done.1, bf16[8,1024]{1,0:T(8,128)(2,1)S(1)} %collective-permute-done.rim_ref, bf16[128,1024]{1,0:T(8,128)(2,1)S(1)} %copy-done.9, f32[1,1024]{1,0:T(1,128)S(1)} %bitcast.218, ...), custom_call_target="tpu_custom_call" | custom-call | tf_op jit(solution)/shard_map/scan_state/pallas_call | solution.py:155
  15.4 2.6 %collective-permute-start.1 = (f32[17,8,128]{2,1,0:T(8,128)S(1)}, f32[17,8,128]{2,1,0:T(8,128)S(1)}, u32[]{:S(2)}, u32[]{:S(2)}) collective-permute-start(f32[17,8,128]{2,1,0:T(8,128)S(1)} %get-tuple-element.10), channel_id=1, source_target_pairs={{0,24},{8,0},{16,8},{24,16},{32,56},{40,32},{48,40},{56,48},{64,88... | collective-permute-start | bytes 208904 | tf_op jit(solution)/shard_map/ppermute | solution.py:22
  19.4 3.3 %collective-permute-done.2 = f32[17,8,128]{2,1,0:T(8,128)S(1)} collective-permute-done((f32[17,8,128]{2,1,0:T(8,128)S(1)}, f32[17,8,128]{2,1,0:T(8,128)S(1)}, u32[]{:S(2)}, u32[]{:S(2)}) %collective-permute-start.2) | collective-permute-done | bytes 69664 | tf_op jit(solution)/shard_map/ppermute | solution.py:22
  23.5 2.7 %collective-permute-start.5 = (f32[17,8,128]{2,1,0:T(8,128)S(1)}, f32[17,8,128]{2,1,0:T(8,128)S(1)}, u32[]{:S(2)}, u32[]{:S(2)}) collective-permute-start(f32[17,8,128]{2,1,0:T(8,128)S(1)} %pad_maximum_fusion.5), channel_id=1, source_target_pairs={{0,64},{8,72},{16,80},{24,88},{32,96},{40,104},{48,112},{56,120},{... | collective-permute-start | bytes 208904 | tf_op jit(solution)/shard_map/ppermute | solution.py:22
  27.5 2.3 collective-permute-start.6
  29.8 2.4 collective-permute-done.4
  32.3 6.1 %scan_output.1.refs_0_ = bf16[128,1024]{1,0:T(8,128)(2,1)S(1)} custom-call(f32[128,8,128]{2,1,0:T(8,128)S(1)} %get-tuple-element.8.step_ref, f32[128,8,128]{2,1,0:T(8,128)S(1)} %get-tuple-element.9.act_ref, bf16[128,1024]{1,0:T(8,128)(2,1)S(1)} %copy-done.2, f32[16,8,128]{2,1,0:T(8,128)S(1)} %fusion.63.enter_ref, f32[16,8,128]{2,1,0:T(8,128)S(1)} %bitcast.216, ...), custom_call_target="tpu_custom_call" | custom-call | tf_op jit(solution)/shard_map/scan_output/pallas_call | solution.py:165
  38.8 4.0 %collective-permute-start.11 = (bf16[1024,256]{1,0:T(8,128)(2,1)S(1)}, bf16[1024,256]{1,0:T(8,128)(2,1)S(1)}, u32[]{:S(2)}, u32[]{:S(2)}) collective-permute-start(bf16[1024,256]{1,0:T(8,128)(2,1)S(1)} %copy-done), channel_id=1, source_target_pairs={{0,64},{8,72},{16,80},{24,88},{32,96},{40,104},{48,112},{56,120},{... | collective-permute-start | bytes 1572872 | tf_op jit(solution)/shard_map/ppermute | solution.py:22
  42.8 2.3 collective-permute-start.8
  46.1 6.1 %collective-permute-done.8.refs_2_ = bf16[128,1024]{1,0:T(8,128)(2,1)S(1)} collective-permute-done((bf16[128,1024]{1,0:T(8,128)(2,1)S(1)}, bf16[128,1024]{1,0:T(8,128)(2,1)S(1)}, u32[]{:S(2)}, u32[]{:S(2)}) %collective-permute-start.8) | collective-permute-done | bytes 262176 | tf_op jit(solution)/shard_map/ppermute | solution.py:22
  53.6 8.0 %collective-permute-done.11.refs_6_ = bf16[1024,256]{1,0:T(8,128)(2,1)S(1)} collective-permute-done((bf16[1024,256]{1,0:T(8,128)(2,1)S(1)}, bf16[1024,256]{1,0:T(8,128)(2,1)S(1)}, u32[]{:S(2)}, u32[]{:S(2)}) %collective-permute-start.11) | collective-permute-done | bytes 524320 | tf_op jit(solution)/shard_map/ppermute | solution.py:22
  61.6 3.2 %collective-permute-done.12.refs_7_ = bf16[1024,256]{1,0:T(8,128)(2,1)S(1)} collective-permute-done((bf16[1024,256]{1,0:T(8,128)(2,1)S(1)}, bf16[1024,256]{1,0:T(8,128)(2,1)S(1)}, u32[]{:S(2)}, u32[]{:S(2)}) %collective-permute-start.12) | collective-permute-done | bytes 524320 | tf_op jit(solution)/shard_map/ppermute | solution.py:22
  67.7 1.8 project.1
  69.5 5.0 %collective-permute-start.13 = (bf16[4,4,128,256]{3,2,1,0:T(8,128)(2,1)S(1)}, bf16[4,4,128,256]{3,2,1,0:T(8,128)(2,1)}, u32[]{:S(2)}, u32[]{:S(2)}) collective-permute-start(bf16[4,4,128,256]{3,2,1,0:T(8,128)(2,1)S(1)} %project.1), channel_id=1, source_target_pairs={{1,0},{3,2},{5,4},{7,6},{9,8},{11,10},{13,12},{15,14},{16,17},{18,... | collective-permute-start | bytes 3145736 | tf_op jit(solution)/shard_map/ppermute | solution.py:38
  75.9 1.6 fusion.78
  85.8 14.0 %collective-permute-done.17 = bf16[128,256]{1,0:T(8,128)(2,1)S(1)} collective-permute-done((bf16[128,256]{1,0:T(8,128)(2,1)S(1)}, bf16[128,256]{1,0:T(8,128)(2,1)S(1)}, u32[]{:S(2)}, u32[]{:S(2)}) %collective-permute-start.17) | collective-permute-done | bytes 65568 | tf_op jit(solution)/shard_map/ppermute | solution.py:38
  99.8 4.1 %collective-permute-done.19 = bf16[128,256]{1,0:T(8,128)(2,1)S(1)} collective-permute-done((bf16[128,256]{1,0:T(8,128)(2,1)S(1)}, bf16[128,256]{1,0:T(8,128)(2,1)S(1)}, u32[]{:S(2)}, u32[]{:S(2)}) %collective-permute-start.19) | collective-permute-done | bytes 65568 | tf_op jit(solution)/shard_map/ppermute | solution.py:38
  104.2 13.9 %all_to_all.14 = bf16[8,48,512]{2,1,0:T(8,128)(2,1)S(1)} all-to-all(bf16[8,48,512]{2,1,0:T(8,128)(2,1)S(1)} %bitcast.233), channel_id=1, replica_groups=mesh['seq'=16,'exp'=8] {'exp'}, dimensions={0} | all-to-all | bytes 786432 | tf_op jit(solution)/shard_map/all_to_all | solution.py:257
  118.8 2.1 collective-permute-start.20
  121.1 2.3 collective-permute-start.22
  123.4 3.0 %collective-permute-start.24 = (bf16[24,4096]{1,0:T(8,128)(2,1)S(1)}, bf16[24,4096]{1,0:T(8,128)(2,1)S(1)}, u32[]{:S(2)}, u32[]{:S(2)}) collective-permute-start(bf16[24,4096]{1,0:T(8,128)(2,1)S(1)} %get-tuple-element.44), channel_id=1, source_target_pairs={{0,64},{8,72},{16,80},{24,88},{32,96},{40,104},{48,112},{56,120},{... | collective-permute-start | bytes 589832 | tf_op jit(solution)/shard_map/ppermute | solution.py:22
  127.6 2.0 collective-permute-done.21
  130.6 2.7 %collective-permute-start.27 = (bf16[4,24,4096]{2,1,0:T(8,128)(2,1)S(1)}, bf16[4,24,4096]{2,1,0:T(8,128)(2,1)S(1)}, u32[]{:S(2)}, u32[]{:S(2)}) collective-permute-start(bf16[4,24,4096]{2,1,0:T(8,128)(2,1)S(1)} %get-tuple-element.37), channel_id=1, source_target_pairs={{0,96},{8,104},{16,112},{24,120},{32,0},{40,8},{48,16},{56,24},{64... | collective-permute-start | bytes 2359304 | tf_op jit(solution)/shard_map/ppermute | solution.py:22
  134.2 1.5 collective-permute-start.28
  137.9 1.4 fusion.16
  140.6 1.4 fusion.34
  142.6 1.4 fusion.21
  144.0 6.6 %collective-permute-done.26 = bf16[4,24,4096]{2,1,0:T(8,128)(2,1)S(1)} collective-permute-done((bf16[4,24,4096]{2,1,0:T(8,128)(2,1)S(1)}, bf16[4,24,4096]{2,1,0:T(8,128)(2,1)S(1)}, u32[]{:S(2)}, u32[]{:S(2)}) %collective-permute-start.26) | collective-permute-done | bytes 786464 | tf_op jit(solution)/shard_map/ppermute | solution.py:22
  152.2 2.6 %fusion.14 = f32[384,768]{1,0:T(8,128)S(1)} fusion(bf16[384,4096]{1,0:T(8,128)(2,1)S(1)} %bitcast.223, bf16[1,4096,768]{2,1,0:T(8,128)(2,1)S(1)} %bitcast.254), kind=kOutput, calls=%fused_computation.14 | convolution fusion | flops 2415919104 | bytes 10616832 | tf_op jit(solution)/shard_map/dot_general | solution.py:268
  154.8 2.7 %multiply_convert_fusion = bf16[384,768]{1,0:T(8,128)(2,1)S(1)} fusion(f32[384,768]{1,0:T(8,128)S(1)} %fusion.14, bf16[384,4096]{1,0:T(8,128)(2,1)S(1)} %bitcast.224, bf16[1,4096,768]{2,1,0:T(8,128)(2,1)S(1)} %bitcast.256), kind=kOutput, calls=%fused_computation.34 | convolution fusion | flops 2417688576 | bytes 11206656 | tf_op jit(solution)/shard_map/dot_general | solution.py:269
  157.5 2.8 %fusion.18 = bf16[384,4096]{1,0:T(8,128)(2,1)S(1)} fusion(bf16[384,768]{1,0:T(8,128)(2,1)S(1)} %multiply_convert_fusion, bf16[1,768,4096]{2,1,0:T(8,128)(2,1)S(1)} %bitcast.258), kind=kOutput, calls=%fused_computation.18 | convolution fusion | flops 2417491968 | bytes 10027008 | tf_op jit(solution)/shard_map/dot_general | solution.py:271
  160.5 2.9 %collective-permute-start.30 = (bf16[4,24,4096]{2,1,0:T(8,128)(2,1)S(1)}, bf16[4,24,4096]{2,1,0:T(8,128)(2,1)S(1)}, u32[]{:S(2)}, u32[]{:S(2)}) collective-permute-start(bf16[4,24,4096]{2,1,0:T(8,128)(2,1)S(1)} %get-tuple-element.17), channel_id=1, source_target_pairs={{0,96},{8,104},{16,112},{24,120},{32,0},{40,8},{48,16},{56,24},{64... | collective-permute-start | bytes 2359304 | tf_op jit(solution)/shard_map/ppermute | solution.py:22
  163.4 5.1 %collective-permute-done.32 = bf16[4,24,4096]{2,1,0:T(8,128)(2,1)S(1)} collective-permute-done((bf16[4,24,4096]{2,1,0:T(8,128)(2,1)S(1)}, bf16[4,24,4096]{2,1,0:T(8,128)(2,1)S(1)}, u32[]{:S(2)}, u32[]{:S(2)}) %collective-permute-start.32) | collective-permute-done | bytes 786464 | tf_op jit(solution)/shard_map/ppermute | solution.py:22
  168.6 1.5 collective-permute-done.33
  170.2 1.4 fusion.12
  171.7 1.4 multiply_convert_fusion.2
  173.1 1.4 fusion.24
  177.6 4.6 %collective-permute-done.30 = bf16[4,24,4096]{2,1,0:T(8,128)(2,1)S(1)} collective-permute-done((bf16[4,24,4096]{2,1,0:T(8,128)(2,1)S(1)}, bf16[4,24,4096]{2,1,0:T(8,128)(2,1)S(1)}, u32[]{:S(2)}, u32[]{:S(2)}) %collective-permute-start.30) | collective-permute-done | bytes 786464 | tf_op jit(solution)/shard_map/ppermute | solution.py:22
  182.2 5.6 %collective-permute-done.34 = bf16[4,24,4096]{2,1,0:T(8,128)(2,1)S(1)} collective-permute-done((bf16[4,24,4096]{2,1,0:T(8,128)(2,1)S(1)}, bf16[4,24,4096]{2,1,0:T(8,128)(2,1)S(1)}, u32[]{:S(2)}, u32[]{:S(2)}) %collective-permute-start.34) | collective-permute-done | bytes 786464 | tf_op jit(solution)/shard_map/ppermute | solution.py:22
  190.2 1.7 collective-permute-start.37
  191.9 6.1 %collective-permute-done.39 = bf16[4,24,4096]{2,1,0:T(8,128)(2,1)S(1)} collective-permute-done((bf16[4,24,4096]{2,1,0:T(8,128)(2,1)S(1)}, bf16[4,24,4096]{2,1,0:T(8,128)(2,1)S(1)}, u32[]{:S(2)}, u32[]{:S(2)}) %collective-permute-start.39) | collective-permute-done | bytes 786464 | tf_op jit(solution)/shard_map/ppermute | solution.py:22
  198.6 1.5 collective-permute-start.41
  200.1 15.2 %collective-permute-start.42 = (bf16[24,4096]{1,0:T(8,128)(2,1)S(1)}, bf16[24,4096]{1,0:T(8,128)(2,1)S(1)}, u32[]{:S(2)}, u32[]{:S(2)}) collective-permute-start(bf16[24,4096]{1,0:T(8,128)(2,1)S(1)} %get-tuple-element.35), channel_id=1, source_target_pairs={{0,32},{8,40},{16,48},{24,56},{32,64},{40,72},{48,80},{56,88},{64,... | collective-permute-start | bytes 589832 | tf_op jit(solution)/shard_map/ppermute | solution.py:22
  215.2 3.6 %collective-permute-start.43 = (bf16[24,4096]{1,0:T(8,128)(2,1)S(1)}, bf16[24,4096]{1,0:T(8,128)(2,1)S(1)}, u32[]{:S(2)}, u32[]{:S(2)}) collective-permute-start(bf16[24,4096]{1,0:T(8,128)(2,1)S(1)} %get-tuple-element.34), channel_id=1, source_target_pairs={{0,64},{8,72},{16,80},{24,88},{32,96},{40,104},{48,112},{56,120},{... | collective-permute-start | bytes 589832 | tf_op jit(solution)/shard_map/ppermute | solution.py:22
  219.1 3.3 %collective-permute-done.43 = bf16[24,4096]{1,0:T(8,128)(2,1)S(1)} collective-permute-done((bf16[24,4096]{1,0:T(8,128)(2,1)S(1)}, bf16[24,4096]{1,0:T(8,128)(2,1)S(1)}, u32[]{:S(2)}, u32[]{:S(2)}) %collective-permute-start.43) | collective-permute-done | bytes 196640 | tf_op jit(solution)/shard_map/ppermute | solution.py:22
  223.5 18.6 %all-to-all-start.1 = ((bf16[8,48,512]{2,1,0:T(8,128)(2,1)}), bf16[8,48,512]{2,1,0:T(8,128)(2,1)S(1)}, u32[]{:S(2)}, u32[]{:S(2)}) async-start(bf16[8,48,512]{2,1,0:T(8,128)(2,1)} %copy.55), calls=%async_computation.1 | async-start | bytes 786432 | tf_op jit(solution)/shard_map/all_to_all | solution.py:285
  242.1 8.1 %all-to-all-done.1 = bf16[8,48,512]{2,1,0:T(8,128)(2,1)S(1)} async-done(((bf16[8,48,512]{2,1,0:T(8,128)(2,1)}), bf16[8,48,512]{2,1,0:T(8,128)(2,1)S(1)}, u32[]{:S(2)}, u32[]{:S(2)}) %all-to-all-start.1) | async-done | bytes 393248 | tf_op jit(solution)/shard_map/all_to_all | solution.py:285
  (164 shorter events, 43.4 us)
Async XLA Ops:
  0.0 32.3 %copy-start.13 = (f32[1024]{0:T(1024)S(1)}, f32[1024]{0:T(1024)}, u32[]{:S(2)}) copy-start(f32[1024]{0:T(1024)} %param.28) | copy-start | bytes 12292
  0.7 38.1 %copy-start = (bf16[1024,256]{1,0:T(8,128)(2,1)S(1)}, bf16[1024,256]{1,0:T(8,128)(2,1)}, u32[]{:S(2)}) copy-start(bf16[1024,256]{1,0:T(8,128)(2,1)} %refs_4_.1) | copy-start | bytes 1572868
  0.7 5.8 %collective-permute-start = (bf16[8,1024]{1,0:T(8,128)(2,1)S(1)}, bf16[8,1024]{1,0:T(8,128)(2,1)S(1)}, u32[]{:S(2)}, u32[]{:S(2)}) collective-permute-start(bf16[8,1024]{1,0:T(8,128)(2,1)S(1)} %slice.163), channel_id=1, source_target_pairs={{0,8},{8,16},{16,24},{24,32},{32,40},{40,48},{48,56},{56,64},{64,7... | collective-permute-start | bytes 49160 | tf_op jit(solution)/shard_map/ppermute | solution.py:150
  15.4 3.9 %collective-permute-start.1 = (f32[17,8,128]{2,1,0:T(8,128)S(1)}, f32[17,8,128]{2,1,0:T(8,128)S(1)}, u32[]{:S(2)}, u32[]{:S(2)}) collective-permute-start(f32[17,8,128]{2,1,0:T(8,128)S(1)} %get-tuple-element.10), channel_id=1, source_target_pairs={{0,24},{8,0},{16,8},{24,16},{32,56},{40,32},{48,40},{56,48},{64,88... | collective-permute-start | bytes 208904 | tf_op jit(solution)/shard_map/ppermute | solution.py:22
  18.0 4.7 %collective-permute-start.2 = (f32[17,8,128]{2,1,0:T(8,128)S(1)}, f32[17,8,128]{2,1,0:T(8,128)S(1)}, u32[]{:S(2)}, u32[]{:S(2)}) collective-permute-start(f32[17,8,128]{2,1,0:T(8,128)S(1)} %get-tuple-element.10), channel_id=1, source_target_pairs={{0,16},{8,24},{16,0},{24,8},{32,48},{40,56},{48,32},{56,40},{64,80... | collective-permute-start | bytes 208904 | tf_op jit(solution)/shard_map/ppermute | solution.py:22
  18.5 4.9 %collective-permute-start.3 = (f32[17,8,128]{2,1,0:T(8,128)S(1)}, f32[17,8,128]{2,1,0:T(8,128)S(1)}, u32[]{:S(2)}, u32[]{:S(2)}) collective-permute-start(f32[17,8,128]{2,1,0:T(8,128)S(1)} %get-tuple-element.10), channel_id=1, source_target_pairs={{0,8},{8,16},{16,24},{24,0},{32,40},{40,48},{48,56},{56,32},{64,72... | collective-permute-start | bytes 208904 | tf_op jit(solution)/shard_map/ppermute | solution.py:22
  23.5 6.2 %collective-permute-start.5 = (f32[17,8,128]{2,1,0:T(8,128)S(1)}, f32[17,8,128]{2,1,0:T(8,128)S(1)}, u32[]{:S(2)}, u32[]{:S(2)}) collective-permute-start(f32[17,8,128]{2,1,0:T(8,128)S(1)} %pad_maximum_fusion.5), channel_id=1, source_target_pairs={{0,64},{8,72},{16,80},{24,88},{32,96},{40,104},{48,112},{56,120},{... | collective-permute-start | bytes 208904 | tf_op jit(solution)/shard_map/ppermute | solution.py:22
  27.0 5.2 %collective-permute-start.4 = (f32[17,8,128]{2,1,0:T(8,128)S(1)}, f32[17,8,128]{2,1,0:T(8,128)S(1)}, u32[]{:S(2)}, u32[]{:S(2)}) collective-permute-start(f32[17,8,128]{2,1,0:T(8,128)S(1)} %pad_maximum_fusion.5), channel_id=1, source_target_pairs={{0,32},{8,40},{16,48},{24,56},{32,64},{40,72},{48,80},{56,88},{64,... | collective-permute-start | bytes 208904 | tf_op jit(solution)/shard_map/ppermute | solution.py:22
  27.5 4.8 %collective-permute-start.6 = (f32[17,8,128]{2,1,0:T(8,128)S(1)}, f32[17,8,128]{2,1,0:T(8,128)S(1)}, u32[]{:S(2)}, u32[]{:S(2)}) collective-permute-start(f32[17,8,128]{2,1,0:T(8,128)S(1)} %pad_maximum_fusion.5), channel_id=1, source_target_pairs={{0,96},{8,104},{16,112},{24,120},{32,0},{40,8},{48,16},{56,24},{64... | collective-permute-start | bytes 208904 | tf_op jit(solution)/shard_map/ppermute | solution.py:22
  38.5 6.6 %collective-permute-start.7 = (bf16[128,1024]{1,0:T(8,128)(2,1)S(1)}, bf16[128,1024]{1,0:T(8,128)(2,1)S(1)}, u32[]{:S(2)}, u32[]{:S(2)}) collective-permute-start(bf16[128,1024]{1,0:T(8,128)(2,1)S(1)} %scan_output.1.refs_0_), channel_id=1, source_target_pairs={{0,8},{8,16},{16,24},{24,0},{32,40},{40,48},{48,56},{56,32},{64,72... | collective-permute-start | bytes 786440 | tf_op jit(solution)/shard_map/ppermute | solution.py:22
  38.8 14.8 %collective-permute-start.10 = (bf16[1024,256]{1,0:T(8,128)(2,1)S(1)}, bf16[1024,256]{1,0:T(8,128)(2,1)S(1)}, u32[]{:S(2)}, u32[]{:S(2)}) collective-permute-start(bf16[1024,256]{1,0:T(8,128)(2,1)S(1)} %copy-done), channel_id=1, source_target_pairs={{0,32},{8,40},{16,48},{24,56},{32,64},{40,72},{48,80},{56,88},{64,... | collective-permute-start | bytes 1572872 | tf_op jit(solution)/shard_map/ppermute | solution.py:22
  38.8 22.8 %collective-permute-start.11 = (bf16[1024,256]{1,0:T(8,128)(2,1)S(1)}, bf16[1024,256]{1,0:T(8,128)(2,1)S(1)}, u32[]{:S(2)}, u32[]{:S(2)}) collective-permute-start(bf16[1024,256]{1,0:T(8,128)(2,1)S(1)} %copy-done), channel_id=1, source_target_pairs={{0,64},{8,72},{16,80},{24,88},{32,96},{40,104},{48,112},{56,120},{... | collective-permute-start | bytes 1572872 | tf_op jit(solution)/shard_map/ppermute | solution.py:22
  42.8 22.0 %collective-permute-start.12 = (bf16[1024,256]{1,0:T(8,128)(2,1)S(1)}, bf16[1024,256]{1,0:T(8,128)(2,1)S(1)}, u32[]{:S(2)}, u32[]{:S(2)}) collective-permute-start(bf16[1024,256]{1,0:T(8,128)(2,1)S(1)} %copy-done), channel_id=1, source_target_pairs={{0,96},{8,104},{16,112},{24,120},{32,0},{40,8},{48,16},{56,24},{64... | collective-permute-start | bytes 1572872 | tf_op jit(solution)/shard_map/ppermute | solution.py:22
  42.8 9.4 %collective-permute-start.8 = (bf16[128,1024]{1,0:T(8,128)(2,1)S(1)}, bf16[128,1024]{1,0:T(8,128)(2,1)S(1)}, u32[]{:S(2)}, u32[]{:S(2)}) collective-permute-start(bf16[128,1024]{1,0:T(8,128)(2,1)S(1)} %scan_output.1.refs_0_), channel_id=1, source_target_pairs={{0,16},{8,24},{16,0},{24,8},{32,48},{40,56},{48,32},{56,40},{64,80... | collective-permute-start | bytes 786440 | tf_op jit(solution)/shard_map/ppermute | solution.py:22
  45.8 7.1 %collective-permute-start.9 = (bf16[128,1024]{1,0:T(8,128)(2,1)S(1)}, bf16[128,1024]{1,0:T(8,128)(2,1)S(1)}, u32[]{:S(2)}, u32[]{:S(2)}) collective-permute-start(bf16[128,1024]{1,0:T(8,128)(2,1)S(1)} %scan_output.1.refs_0_), channel_id=1, source_target_pairs={{0,24},{8,0},{16,8},{24,16},{32,56},{40,32},{48,40},{56,48},{64,88... | collective-permute-start | bytes 786440 | tf_op jit(solution)/shard_map/ppermute | solution.py:22
  46.0 28.5 %copy-start.16 = (s32[128,2]{0,1:T(2,128)S(1)}, s32[128,2]{0,1:T(2,128)}, u32[]{:S(2)}) copy-start(s32[128,2]{0,1:T(2,128)} %param.30) | copy-start | bytes 3076
  69.5 6.4 %collective-permute-start.13 = (bf16[4,4,128,256]{3,2,1,0:T(8,128)(2,1)S(1)}, bf16[4,4,128,256]{3,2,1,0:T(8,128)(2,1)}, u32[]{:S(2)}, u32[]{:S(2)}) collective-permute-start(bf16[4,4,128,256]{3,2,1,0:T(8,128)(2,1)S(1)} %project.1), channel_id=1, source_target_pairs={{1,0},{3,2},{5,4},{7,6},{9,8},{11,10},{13,12},{15,14},{16,17},{18,... | collective-permute-start | bytes 3145736 | tf_op jit(solution)/shard_map/ppermute | solution.py:38
  78.3 3.0 %collective-permute-start.14 = (bf16[4,128,256]{2,1,0:T(8,128)(2,1)}, bf16[4,128,256]{2,1,0:T(8,128)(2,1)S(1)}, u32[]{:S(2)}, u32[]{:S(2)}) collective-permute-start(bf16[4,128,256]{2,1,0:T(8,128)(2,1)} %get-tuple-element.27), channel_id=1, source_target_pairs={{0,2},{2,4},{4,6},{6,0},{8,10},{10,12},{12,14},{14,8},{17,19},{19,... | collective-permute-start | bytes 786440 | tf_op jit(solution)/shard_map/ppermute | solution.py:38
  78.9 2.4 collective-permute-start.15
  79.6 1.7 collective-permute-start.16
  82.4 17.4 %collective-permute-start.17 = (bf16[128,256]{1,0:T(8,128)(2,1)S(1)}, bf16[128,256]{1,0:T(8,128)(2,1)S(1)}, u32[]{:S(2)}, u32[]{:S(2)}) collective-permute-start(bf16[128,256]{1,0:T(8,128)(2,1)S(1)} %get-tuple-element.46), channel_id=1, source_target_pairs={{0,16},{2,18},{4,20},{6,22},{8,24},{10,26},{12,28},{14,30},{17,1},... | collective-permute-start | bytes 196616 | tf_op jit(solution)/shard_map/ppermute | solution.py:38
  83.7 16.1 %collective-permute-start.18 = (bf16[128,256]{1,0:T(8,128)(2,1)S(1)}, bf16[128,256]{1,0:T(8,128)(2,1)S(1)}, u32[]{:S(2)}, u32[]{:S(2)}) collective-permute-start(bf16[128,256]{1,0:T(8,128)(2,1)S(1)} %get-tuple-element.48), channel_id=1, source_target_pairs={{0,24},{2,26},{4,28},{6,30},{8,0},{10,2},{12,4},{14,6},{17,9},{19,... | collective-permute-start | bytes 196616 | tf_op jit(solution)/shard_map/ppermute | solution.py:38
  84.4 19.5 %collective-permute-start.19 = (bf16[128,256]{1,0:T(8,128)(2,1)S(1)}, bf16[128,256]{1,0:T(8,128)(2,1)S(1)}, u32[]{:S(2)}, u32[]{:S(2)}) collective-permute-start(bf16[128,256]{1,0:T(8,128)(2,1)S(1)} %get-tuple-element.47), channel_id=1, source_target_pairs={{0,8},{2,10},{4,12},{6,14},{8,16},{10,18},{12,20},{14,22},{17,25},... | collective-permute-start | bytes 196616 | tf_op jit(solution)/shard_map/ppermute | solution.py:38
  118.8 7.6 %collective-permute-start.20 = (bf16[24,4096]{1,0:T(8,128)(2,1)S(1)}, bf16[24,4096]{1,0:T(8,128)(2,1)S(1)}, u32[]{:S(2)}, u32[]{:S(2)}) collective-permute-start(bf16[24,4096]{1,0:T(8,128)(2,1)S(1)} %get-tuple-element.45), channel_id=1, source_target_pairs={{0,8},{8,16},{16,24},{24,0},{32,40},{40,48},{48,56},{56,32},{64,72... | collective-permute-start | bytes 589832 | tf_op jit(solution)/shard_map/ppermute | solution.py:22
  120.9 8.7 %collective-permute-start.21 = (bf16[24,4096]{1,0:T(8,128)(2,1)S(1)}, bf16[24,4096]{1,0:T(8,128)(2,1)S(1)}, u32[]{:S(2)}, u32[]{:S(2)}) collective-permute-start(bf16[24,4096]{1,0:T(8,128)(2,1)S(1)} %get-tuple-element.45), channel_id=1, source_target_pairs={{0,16},{8,24},{16,0},{24,8},{32,48},{40,56},{48,32},{56,40},{64,80... | collective-permute-start | bytes 589832 | tf_op jit(solution)/shard_map/ppermute | solution.py:22
  121.1 9.4 %collective-permute-start.22 = (bf16[24,4096]{1,0:T(8,128)(2,1)S(1)}, bf16[24,4096]{1,0:T(8,128)(2,1)S(1)}, u32[]{:S(2)}, u32[]{:S(2)}) collective-permute-start(bf16[24,4096]{1,0:T(8,128)(2,1)S(1)} %get-tuple-element.45), channel_id=1, source_target_pairs={{0,24},{8,0},{16,8},{24,16},{32,56},{40,32},{48,40},{56,48},{64,88... | collective-permute-start | bytes 589832 | tf_op jit(solution)/shard_map/ppermute | solution.py:22
  123.4 9.9 %collective-permute-start.23 = (bf16[24,4096]{1,0:T(8,128)(2,1)S(1)}, bf16[24,4096]{1,0:T(8,128)(2,1)S(1)}, u32[]{:S(2)}, u32[]{:S(2)}) collective-permute-start(bf16[24,4096]{1,0:T(8,128)(2,1)S(1)} %get-tuple-element.44), channel_id=1, source_target_pairs={{0,32},{8,40},{16,48},{24,56},{32,64},{40,72},{48,80},{56,88},{64,... | collective-permute-start | bytes 589832 | tf_op jit(solution)/shard_map/ppermute | solution.py:22
  123.4 10.7 %collective-permute-start.24 = (bf16[24,4096]{1,0:T(8,128)(2,1)S(1)}, bf16[24,4096]{1,0:T(8,128)(2,1)S(1)}, u32[]{:S(2)}, u32[]{:S(2)}) collective-permute-start(bf16[24,4096]{1,0:T(8,128)(2,1)S(1)} %get-tuple-element.44), channel_id=1, source_target_pairs={{0,64},{8,72},{16,80},{24,88},{32,96},{40,104},{48,112},{56,120},{... | collective-permute-start | bytes 589832 | tf_op jit(solution)/shard_map/ppermute | solution.py:22
  126.4 7.7 %collective-permute-start.25 = (bf16[24,4096]{1,0:T(8,128)(2,1)S(1)}, bf16[24,4096]{1,0:T(8,128)(2,1)S(1)}, u32[]{:S(2)}, u32[]{:S(2)}) collective-permute-start(bf16[24,4096]{1,0:T(8,128)(2,1)S(1)} %get-tuple-element.44), channel_id=1, source_target_pairs={{0,96},{8,104},{16,112},{24,120},{32,0},{40,8},{48,16},{56,24},{64... | collective-permute-start | bytes 589832 | tf_op jit(solution)/shard_map/ppermute | solution.py:22
  130.5 20.1 %collective-permute-start.26 = (bf16[4,24,4096]{2,1,0:T(8,128)(2,1)S(1)}, bf16[4,24,4096]{2,1,0:T(8,128)(2,1)S(1)}, u32[]{:S(2)}, u32[]{:S(2)}) collective-permute-start(bf16[4,24,4096]{2,1,0:T(8,128)(2,1)S(1)} %get-tuple-element.37), channel_id=1, source_target_pairs={{0,32},{8,40},{16,48},{24,56},{32,64},{40,72},{48,80},{56,88},{64,... | collective-permute-start | bytes 2359304 | tf_op jit(solution)/shard_map/ppermute | solution.py:22
  130.6 21.1 %collective-permute-start.27 = (bf16[4,24,4096]{2,1,0:T(8,128)(2,1)S(1)}, bf16[4,24,4096]{2,1,0:T(8,128)(2,1)S(1)}, u32[]{:S(2)}, u32[]{:S(2)}) collective-permute-start(bf16[4,24,4096]{2,1,0:T(8,128)(2,1)S(1)} %get-tuple-element.37), channel_id=1, source_target_pairs={{0,96},{8,104},{16,112},{24,120},{32,0},{40,8},{48,16},{56,24},{64... | collective-permute-start | bytes 2359304 | tf_op jit(solution)/shard_map/ppermute | solution.py:22
  134.2 17.5 %collective-permute-start.28 = (bf16[4,24,4096]{2,1,0:T(8,128)(2,1)S(1)}, bf16[4,24,4096]{2,1,0:T(8,128)(2,1)S(1)}, u32[]{:S(2)}, u32[]{:S(2)}) collective-permute-start(bf16[4,24,4096]{2,1,0:T(8,128)(2,1)S(1)} %get-tuple-element.39), channel_id=1, source_target_pairs={{0,8},{8,16},{16,24},{24,0},{32,40},{40,48},{48,56},{56,32},{64,72... | collective-permute-start | bytes 2359304 | tf_op jit(solution)/shard_map/ppermute | solution.py:22
  135.8 15.9 %collective-permute-start.29 = (bf16[4,24,4096]{2,1,0:T(8,128)(2,1)S(1)}, bf16[4,24,4096]{2,1,0:T(8,128)(2,1)S(1)}, u32[]{:S(2)}, u32[]{:S(2)}) collective-permute-start(bf16[4,24,4096]{2,1,0:T(8,128)(2,1)S(1)} %get-tuple-element.39), channel_id=1, source_target_pairs={{0,24},{8,0},{16,8},{24,16},{32,56},{40,32},{48,40},{56,48},{64,88... | collective-permute-start | bytes 2359304 | tf_op jit(solution)/shard_map/ppermute | solution.py:22
  137.0 31.6 %collective-permute-start.32 = (bf16[4,24,4096]{2,1,0:T(8,128)(2,1)S(1)}, bf16[4,24,4096]{2,1,0:T(8,128)(2,1)S(1)}, u32[]{:S(2)}, u32[]{:S(2)}) collective-permute-start(bf16[4,24,4096]{2,1,0:T(8,128)(2,1)S(1)} %get-tuple-element.37), channel_id=1, source_target_pairs={{0,64},{8,72},{16,80},{24,88},{32,96},{40,104},{48,112},{56,120},{... | collective-permute-start | bytes 2359304 | tf_op jit(solution)/shard_map/ppermute | solution.py:22
  150.6 19.5 %collective-permute-start.33 = (bf16[4,24,4096]{2,1,0:T(8,128)(2,1)S(1)}, bf16[4,24,4096]{2,1,0:T(8,128)(2,1)S(1)}, u32[]{:S(2)}, u32[]{:S(2)}) collective-permute-start(bf16[4,24,4096]{2,1,0:T(8,128)(2,1)S(1)} %get-tuple-element.39), channel_id=1, source_target_pairs={{0,16},{8,24},{16,0},{24,8},{32,48},{40,56},{48,32},{56,40},{64,80... | collective-permute-start | bytes 2359304 | tf_op jit(solution)/shard_map/ppermute | solution.py:22
  160.5 21.7 %collective-permute-start.30 = (bf16[4,24,4096]{2,1,0:T(8,128)(2,1)S(1)}, bf16[4,24,4096]{2,1,0:T(8,128)(2,1)S(1)}, u32[]{:S(2)}, u32[]{:S(2)}) collective-permute-start(bf16[4,24,4096]{2,1,0:T(8,128)(2,1)S(1)} %get-tuple-element.17), channel_id=1, source_target_pairs={{0,96},{8,104},{16,112},{24,120},{32,0},{40,8},{48,16},{56,24},{64... | collective-permute-start | bytes 2359304 | tf_op jit(solution)/shard_map/ppermute | solution.py:22
  163.4 18.8 %collective-permute-start.31 = (bf16[4,24,4096]{2,1,0:T(8,128)(2,1)S(1)}, bf16[4,24,4096]{2,1,0:T(8,128)(2,1)S(1)}, u32[]{:S(2)}, u32[]{:S(2)}) collective-permute-start(bf16[4,24,4096]{2,1,0:T(8,128)(2,1)S(1)} %get-tuple-element.20), channel_id=1, source_target_pairs={{0,32},{8,40},{16,48},{24,56},{32,64},{40,72},{48,80},{56,88},{64,... | collective-permute-start | bytes 2359304 | tf_op jit(solution)/shard_map/ppermute | solution.py:22
  174.7 13.0 %collective-permute-start.34 = (bf16[4,24,4096]{2,1,0:T(8,128)(2,1)S(1)}, bf16[4,24,4096]{2,1,0:T(8,128)(2,1)S(1)}, u32[]{:S(2)}, u32[]{:S(2)}) collective-permute-start(bf16[4,24,4096]{2,1,0:T(8,128)(2,1)S(1)} %bitcast.245), channel_id=1, source_target_pairs={{0,64},{8,72},{16,80},{24,88},{32,96},{40,104},{48,112},{56,120},{... | collective-permute-start | bytes 2359304 | tf_op jit(solution)/shard_map/ppermute | solution.py:22
  176.1 14.2 %collective-permute-start.38 = (bf16[4,24,4096]{2,1,0:T(8,128)(2,1)S(1)}, bf16[4,24,4096]{2,1,0:T(8,128)(2,1)S(1)}, u32[]{:S(2)}, u32[]{:S(2)}) collective-permute-start(bf16[4,24,4096]{2,1,0:T(8,128)(2,1)S(1)} %get-tuple-element.19), channel_id=1, source_target_pairs={{0,24},{8,0},{16,8},{24,16},{32,56},{40,32},{48,40},{56,48},{64,88... | collective-permute-start | bytes 2359304 | tf_op jit(solution)/shard_map/ppermute | solution.py:22
  177.2 20.8 %collective-permute-start.39 = (bf16[4,24,4096]{2,1,0:T(8,128)(2,1)S(1)}, bf16[4,24,4096]{2,1,0:T(8,128)(2,1)S(1)}, u32[]{:S(2)}, u32[]{:S(2)}) collective-permute-start(bf16[4,24,4096]{2,1,0:T(8,128)(2,1)S(1)} %get-tuple-element.18), channel_id=1, source_target_pairs={{0,8},{8,16},{16,24},{24,0},{32,40},{40,48},{48,56},{56,32},{64,72... | collective-permute-start | bytes 2359304 | tf_op jit(solution)/shard_map/ppermute | solution.py:22
  182.2 15.8 %collective-permute-start.40 = (bf16[4,24,4096]{2,1,0:T(8,128)(2,1)S(1)}, bf16[4,24,4096]{2,1,0:T(8,128)(2,1)S(1)}, u32[]{:S(2)}, u32[]{:S(2)}) collective-permute-start(bf16[4,24,4096]{2,1,0:T(8,128)(2,1)S(1)} %bitcast.242), channel_id=1, source_target_pairs={{0,16},{8,24},{16,0},{24,8},{32,48},{40,56},{48,32},{56,40},{64,80... | collective-permute-start | bytes 2359304 | tf_op jit(solution)/shard_map/ppermute | solution.py:22
  188.3 26.9 %collective-permute-start.35 = (bf16[24,4096]{1,0:T(8,128)(2,1)S(1)}, bf16[24,4096]{1,0:T(8,128)(2,1)S(1)}, u32[]{:S(2)}, u32[]{:S(2)}) collective-permute-start(bf16[24,4096]{1,0:T(8,128)(2,1)S(1)} %get-tuple-element.30), channel_id=1, source_target_pairs={{0,24},{8,0},{16,8},{24,16},{32,56},{40,32},{48,40},{56,48},{64,88... | collective-permute-start | bytes 589832 | tf_op jit(solution)/shard_map/ppermute | solution.py:22
  189.3 29.5 %collective-permute-start.36 = (bf16[24,4096]{1,0:T(8,128)(2,1)S(1)}, bf16[24,4096]{1,0:T(8,128)(2,1)S(1)}, u32[]{:S(2)}, u32[]{:S(2)}) collective-permute-start(bf16[24,4096]{1,0:T(8,128)(2,1)S(1)} %get-tuple-element.32), channel_id=1, source_target_pairs={{0,8},{8,16},{16,24},{24,0},{32,40},{40,48},{48,56},{56,32},{64,72... | collective-permute-start | bytes 589832 | tf_op jit(solution)/shard_map/ppermute | solution.py:22
  190.2 28.6 %collective-permute-start.37 = (bf16[24,4096]{1,0:T(8,128)(2,1)S(1)}, bf16[24,4096]{1,0:T(8,128)(2,1)S(1)}, u32[]{:S(2)}, u32[]{:S(2)}) collective-permute-start(bf16[24,4096]{1,0:T(8,128)(2,1)S(1)} %get-tuple-element.31), channel_id=1, source_target_pairs={{0,16},{8,24},{16,0},{24,8},{32,48},{40,56},{48,32},{56,40},{64,80... | collective-permute-start | bytes 589832 | tf_op jit(solution)/shard_map/ppermute | solution.py:22
  198.6 20.5 %collective-permute-start.41 = (bf16[24,4096]{1,0:T(8,128)(2,1)S(1)}, bf16[24,4096]{1,0:T(8,128)(2,1)S(1)}, u32[]{:S(2)}, u32[]{:S(2)}) collective-permute-start(bf16[24,4096]{1,0:T(8,128)(2,1)S(1)} %get-tuple-element.33), channel_id=1, source_target_pairs={{0,96},{8,104},{16,112},{24,120},{32,0},{40,8},{48,16},{56,24},{64... | collective-permute-start | bytes 589832 | tf_op jit(solution)/shard_map/ppermute | solution.py:22
  200.1 19.0 %collective-permute-start.42 = (bf16[24,4096]{1,0:T(8,128)(2,1)S(1)}, bf16[24,4096]{1,0:T(8,128)(2,1)S(1)}, u32[]{:S(2)}, u32[]{:S(2)}) collective-permute-start(bf16[24,4096]{1,0:T(8,128)(2,1)S(1)} %get-tuple-element.35), channel_id=1, source_target_pairs={{0,32},{8,40},{16,48},{24,56},{32,64},{40,72},{48,80},{56,88},{64,... | collective-permute-start | bytes 589832 | tf_op jit(solution)/shard_map/ppermute | solution.py:22
  215.2 7.2 %collective-permute-start.43 = (bf16[24,4096]{1,0:T(8,128)(2,1)S(1)}, bf16[24,4096]{1,0:T(8,128)(2,1)S(1)}, u32[]{:S(2)}, u32[]{:S(2)}) collective-permute-start(bf16[24,4096]{1,0:T(8,128)(2,1)S(1)} %get-tuple-element.34), channel_id=1, source_target_pairs={{0,64},{8,72},{16,80},{24,88},{32,96},{40,104},{48,112},{56,120},{... | collective-permute-start | bytes 589832 | tf_op jit(solution)/shard_map/ppermute | solution.py:22
  223.5 26.7 %all-to-all-start.1 = ((bf16[8,48,512]{2,1,0:T(8,128)(2,1)}), bf16[8,48,512]{2,1,0:T(8,128)(2,1)S(1)}, u32[]{:S(2)}, u32[]{:S(2)}) async-start(bf16[8,48,512]{2,1,0:T(8,128)(2,1)} %copy.55), calls=%async_computation.1 | async-start | bytes 786432 | tf_op jit(solution)/shard_map/all_to_all | solution.py:285
  (21 other events, 132.9 us)

commit v2 on v1

--- a/solution.py
+++ b/solution.py
@@ -22,20 +22,9 @@
     return lax.ppermute(value, "seq", route)
 
 
-def keeper_shift(value, axis, distance):
-    route = []
-    for y in range(SIDE):
-        for x in range(SIDE):
-            for z in range(SIDE):
-                start = [y, x, z, x // 2]
-                end = [y, x, z, x // 2]
-                if axis == "core":
-                    start[3] = 1 - start[3]
-                else:
-                    at = "yxz".index(axis)
-                    end[at] = (end[at] + distance) % SIDE
-                route.append(tuple((v[0] * SIDE + v[1]) * 2 * SIDE + v[2] * 2 + v[3] for v in (start, end)))
-    return lax.ppermute(value, ("seq", "exp"), route)
+def partner(value):
+    cells = range(SIDE * SIDE)
+    return lax.ppermute(value, "seq", [(i, i ^ 1) for i in cells])
 
 
 def ring_gather(block, axis):
@@ -173,42 +162,30 @@
     )(step, act, gate_in, enter, rate, d_skip.reshape(8, 128), b_proj, c_proj)
 
 
-def project_kernel(place_ref, *refs):
-    rows, columns, out_ref = refs[:SIDE], refs[SIDE : 2 * SIDE], refs[2 * SIDE]
-    y, z = place_ref[0], place_ref[1]
-    for i in range(SIDE):
-        far = lax.rem(y - i - z + 2 * SIDE, SIDE)
-        for j in range(SIDE):
-            out_ref[far, j] = jnp.dot(
-                rows[j][...], columns[i][...], preferred_element_type=F32
-            ).astype(BF16)
-
-
-def project(mixed, w_out_blocks):
-    rows = ring_gather(mixed, "x")
-    place = jnp.stack([lax.axis_index("seq") // SIDE, lax.axis_index("exp") // 2]).astype(jnp.int32)
-    vmem = pl.BlockSpec(memory_space=pltpu.VMEM)
-    tokens, columns = mixed.shape[0], w_out_blocks[0].shape[1]
+def project_kernel(own_ref, other_ref, weight_ref, out_ref):
+    for k, rows in enumerate((own_ref, other_ref)):
+        out_ref[0, k] = jnp.dot(rows[...], weight_ref[0], preferred_element_type=F32).astype(BF16)
+
+
+def project(mixed, weights):
+    owners, channels, columns = weights.shape
+    tokens = mixed.shape[0]
+    whole = pl.BlockSpec((tokens, channels), lambda e: (0, 0))
     partial = pl.pallas_call(
         project_kernel,
-        out_shape=jax.ShapeDtypeStruct((SIDE, SIDE, tokens, columns), BF16),
-        in_specs=[pl.BlockSpec(memory_space=pltpu.SMEM)] + [vmem] * (2 * SIDE),
-        out_specs=vmem,
-        compiler_params=pltpu.CompilerParams(vmem_limit_bytes=40 << 20),
+        grid=(owners,),
+        out_shape=jax.ShapeDtypeStruct((owners, 2, tokens, columns), BF16),
+        in_specs=[whole, whole, pl.BlockSpec((1, channels, columns), lambda e: (e, 0, 0))],
+        out_specs=pl.BlockSpec((1, 2, tokens, columns), lambda e: (e, 0, 0, 0)),
         name="project",
-    )(place, *rows, *w_out_blocks)
-    total = partial.astype(F32) + keeper_shift(partial, "core", 0).astype(F32)
-    near = total[0]
-    for d in range(1, SIDE):
-        near = near + keeper_shift(total[d].astype(BF16), "z", d).astype(F32)
-    x, core = lax.axis_index("seq") % SIDE, lax.axis_index("exp") % 2
-    near = near.astype(BF16)
-    got = [jnp.where(core == x // 2, near[0], jnp.zeros_like(near[0]))]
-    got += [keeper_shift(near[k], "x", -k) for k in range(1, SIDE)]
-    even, odd = got[0] + got[2], got[1] + got[3]
+    )(mixed, partner(mixed), weights)
+    partial = lax.all_to_all(partial, "exp", split_axis=0, concat_axis=0)
+    total = jnp.sum(partial.astype(F32), axis=0)
+    other = partner(total[1].astype(BF16)).astype(F32)
+    is_even = lax.axis_index("seq") % 2 == 0
     return jnp.concatenate(
-        [jnp.where(x % 2 == 0, even, odd), jnp.where(x % 2 == 0, odd, even)], axis=1
-    ).astype(F32)
+        [jnp.where(is_even, total[0], other), jnp.where(is_even, other, total[0])], axis=1
+    )
 
 
 def local(
@@ -236,7 +213,8 @@
     groups = lax.axis_size("seq")
     capacity = 3 * tokens // experts
     width = stream.shape[1]
-    out_blocks = ring_gather(w_out, "y")
+    parity = [[i for i in range(groups) if i % 2 == p] for p in range(2)]
+    out_blocks = lax.all_gather(w_out, "seq", axis=0, axis_index_groups=parity)
     mixed = mixer(
         mixer_in, gate_in, dt_raw, dt_bias, a_log, conv_weight, conv_bias, b_proj, c_proj, d_skip
     )

time: 252 us -> 278 us (1.10)
  waiting for transfers between devices: 87.2 us -> 105 us
  between operations: 0.63 us -> 13.9 us
  local copies, waits for them, and re-layouts: 16.4 us -> 10.3 us
  Pallas kernels: 12.9 us -> 18.2 us
    all_gather x0 -> x1, waiting for transfers between devices: none -> 25.8 us  [local(): out_blocks = lax.all_gather(w_out, 'seq', axis=0, axis_index_groups=parity)]
    ppermute x36 -> x30, waiting for transfers between devices: 60.8 us -> 40.2 us  [shift(): return lax.ppermute(value, 'seq', route)]
    all_to_all x0 -> x1, waiting for transfers between devices: none -> 13.5 us  [project(): partial = lax.all_to_all(partial, 'exp', split_axis=0, concat_axis=0)]
    ppermute x7 -> x2, starting transfers between devices: 11 us -> 0.17 us  [partner(): return lax.ppermute(value, 'seq', [(i, i ^ 1) for i in cells])]
    all_to_all x0 -> x1, starting transfers between devices: none -> 5.74 us  [project(): partial = lax.all_to_all(partial, 'exp', split_axis=0, concat_axis=0)]
    unnamed x55 -> x47, local copies, waits for them, and re-layouts: 12.7 us -> 7.38 us
    pallas_call x1, Pallas kernels: 1.83 us -> 7.11 us  [project(): pl.pallas_call(project_kernel, grid=(owners,), out_shape=jax.ShapeDtypeSt...]
    ppermute x36 -> x30, starting transfers between devices: 61.3 us -> 65.2 us  [shift(): return lax.ppermute(value, 'seq', route)]
  transfers between devices with their start and end apart: 45 -> 36, of which waited for: 21 -> 19; matrix products, arithmetic and copies ran while one was open for 9% -> 9% of each run, Pallas kernels for 0% -> 4%
where the time goes in v2:
time: 278 us; the launch traced here: 277 us
  waiting for transfers between devices  105 us (38%)
  starting transfers between devices  94.4 us (34%)
  Pallas kernels  18.2 us (7%)
  matrix products  18.2 us (7%)
  between operations  13.9 us (5%)
  blocking collectives  12.5 us (4%)
  local copies, waits for them, and re-layouts  10.3 us (4%)
  other arithmetic  4.59 us (2%)
    ppermute x30, starting transfers between devices, shift(): return lax.ppermute(value, 'seq', route)  65.2 us
    ppermute x30, waiting for transfers between devices, shift(): return lax.ppermute(value, 'seq', route)  40.2 us
    all_gather x1, waiting for transfers between devices, local(): out_blocks = lax.all_gather(w_out, 'seq', axis=0, axis_index_groups=parity)  25.8 us
    all_to_all x1, starting transfers between devices, local(): returned = lax.all_to_all(summed, 'exp', split_axis=0, concat_axis=0)  19.4 us
    ppermute x2, waiting for transfers between devices, partner(): return lax.ppermute(value, 'seq', [(i, i ^ 1) for i in cells])  16.4 us
    all_to_all x1, waiting for transfers between devices, project(): partial = lax.all_to_all(partial, 'exp', split_axis=0, concat_axis=0)  13.5 us
    all_to_all x1, blocking collectives, local(): lax.all_to_all(outgoing, 'exp', split_axis=0, concat_axis=2, tiled=True)[0]  12.5 us
    all_to_all x1, waiting for transfers between devices, local(): returned = lax.all_to_all(summed, 'exp', split_axis=0, concat_axis=0)  8.09 us
  transfers between devices with their start and end apart: 36, of which 19 were waited for; matrix products, arithmetic and copies ran while one was open for 9% of the time, Pallas kernels for 4%

profile of v2, /device:TPU:1, one launch (start us, length us, event | category | flops | bytes accessed | tf_op | source)
XLA Modules:
  0.0 276.7 jit_solution(3574043134573024854)
XLA Ops:
  8.0 3.9 %collective-permute-start = (bf16[8,1024]{1,0:T(8,128)(2,1)S(1)}, bf16[8,1024]{1,0:T(8,128)(2,1)S(1)}, u32[]{:S(2)}, u32[]{:S(2)}) collective-permute-start(bf16[8,1024]{1,0:T(8,128)(2,1)S(1)} %slice.144), channel_id=1, source_target_pairs={{0,8},{8,16},{16,24},{24,32},{32,40},{40,48},{48,56},{56,64},{64,7... | collective-permute-start | bytes 49160 | tf_op jit(solution)/shard_map/ppermute | solution.py:139
  17.6 4.9 %scan_state.1 = (f32[128,8,128]{2,1,0:T(8,128)S(1)}, f32[128,8,128]{2,1,0:T(8,128)S(1)}, f32[17,8,128]{2,1,0:T(8,128)S(1)}) custom-call(bf16[128,1024]{1,0:T(8,128)(2,1)S(1)} %copy-done.1, bf16[8,1024]{1,0:T(8,128)(2,1)S(1)} %collective-permute-done.rim_ref, bf16[128,1024]{1,0:T(8,128)(2,1)S(1)} %copy-done.3, f32[1,1024]{1,0:T(1,128)S(1)} %bitcast.195, ...), custom_call_target="tpu_custom_call" | custom-call | tf_op jit(solution)/shard_map/scan_state/pallas_call | solution.py:144
  22.6 2.6 collective-permute-start.1
  25.9 1.8 collective-permute-done.1
  27.7 3.9 %collective-permute-done.2 = f32[17,8,128]{2,1,0:T(8,128)S(1)} collective-permute-done((f32[17,8,128]{2,1,0:T(8,128)S(1)}, f32[17,8,128]{2,1,0:T(8,128)S(1)}, u32[]{:S(2)}, u32[]{:S(2)}) %collective-permute-start.2) | collective-permute-done | bytes 69664 | tf_op jit(solution)/shard_map/ppermute | solution.py:22
  31.6 4.4 %collective-permute-done.3 = f32[17,8,128]{2,1,0:T(8,128)S(1)} collective-permute-done((f32[17,8,128]{2,1,0:T(8,128)S(1)}, f32[17,8,128]{2,1,0:T(8,128)S(1)}, u32[]{:S(2)}, u32[]{:S(2)}) %collective-permute-start.3) | collective-permute-done | bytes 69664 | tf_op jit(solution)/shard_map/ppermute | solution.py:22
  36.1 2.7 collective-permute-start.5
  39.3 2.3 collective-permute-start.6
  42.8 2.4 collective-permute-done.4
  45.4 6.1 %scan_output.1.own_ref = bf16[128,1024]{1,0:T(8,128)(2,1)S(1)} custom-call(f32[128,8,128]{2,1,0:T(8,128)S(1)} %get-tuple-element.8.step_ref, f32[128,8,128]{2,1,0:T(8,128)S(1)} %get-tuple-element.9.act_ref, bf16[128,1024]{1,0:T(8,128)(2,1)S(1)} %copy-done.2, f32[16,8,128]{2,1,0:T(8,128)S(1)} %fusion.59.enter_ref, f32[16,8,128]{2,1,0:T(8,128)S(1)} %bitcast.193, ...), custom_call_target="tpu_custom_call" | custom-call | tf_op jit(solution)/shard_map/scan_output/pallas_call | solution.py:154
  51.6 13.3 %collective-permute-done.7.other_ref = bf16[128,1024]{1,0:T(8,128)(2,1)S(1)} collective-permute-done((bf16[128,1024]{1,0:T(8,128)(2,1)S(1)}, bf16[128,1024]{1,0:T(8,128)(2,1)S(1)}, u32[]{:S(2)}, u32[]{:S(2)}) %collective-permute-start.7) | collective-permute-done | bytes 262176 | tf_op jit(solution)/shard_map/ppermute | solution.py:27
  64.9 25.8 %all-gather.3.cloned.1.call-done = bf16[8192,256]{1,0:T(8,128)(2,1)} async-done(((bf16[1024,256]{1,0:T(8,128)(2,1)}), bf16[8192,256]{1,0:T(8,128)(2,1)}) %all-gather.3.cloned.1.call-update) | async-done | bytes 4194320 | tf_op jit(solution)/shard_map/all_gather | solution.py:217
  90.7 7.1 %project.1 = bf16[8,2,128,256]{3,2,1,0:T(8,128)(2,1)} custom-call(bf16[128,1024]{1,0:T(8,128)(2,1)} %copy-done, bf16[128,1024]{1,0:T(8,128)(2,1)} %copy-done.9, bf16[8,1024,256]{2,1,0:T(8,128)(2,1)} %bitcast.198), custom_call_target="tpu_custom_call" | custom-call | tf_op jit(solution)/shard_map/project/pallas_call | solution.py:174
  97.8 5.7 %all-to-all-start = ((bf16[8,2,128,256]{3,2,1,0:T(8,128)(2,1)}), bf16[8,2,128,256]{3,2,1,0:T(8,128)(2,1)S(1)}, u32[]{:S(2)}, u32[]{:S(2)}) async-start(bf16[8,2,128,256]{3,2,1,0:T(8,128)(2,1)} %project.1), calls=%async_computation | async-start | bytes 2097152 | tf_op jit(solution)/shard_map/all_to_all | solution.py:182
  105.1 13.5 %all-to-all-done = bf16[8,2,128,256]{3,2,1,0:T(8,128)(2,1)S(1)} async-done(((bf16[8,2,128,256]{3,2,1,0:T(8,128)(2,1)}), bf16[8,2,128,256]{3,2,1,0:T(8,128)(2,1)S(1)}, u32[]{:S(2)}, u32[]{:S(2)}) %all-to-all-start) | async-done | bytes 1048608 | tf_op jit(solution)/shard_map/all_to_all | solution.py:182
  118.9 3.1 %collective-permute-done.8 = bf16[128,256]{1,0:T(8,128)(2,1)S(1)} collective-permute-done((bf16[128,256]{1,0:T(8,128)(2,1)S(1)}, bf16[128,256]{1,0:T(8,128)(2,1)S(1)}, u32[]{:S(2)}, u32[]{:S(2)}) %collective-permute-start.8) | collective-permute-done | bytes 65568 | tf_op jit(solution)/shard_map/ppermute | solution.py:27
  122.3 12.5 %all_to_all.19 = bf16[8,48,512]{2,1,0:T(8,128)(2,1)S(1)} all-to-all(bf16[8,48,512]{2,1,0:T(8,128)(2,1)S(1)} %bitcast.211), channel_id=1, replica_groups=mesh['seq'=16,'exp'=8] {'exp'}, dimensions={0} | all-to-all | bytes 786432 | tf_op jit(solution)/shard_map/all_to_all | solution.py:235
  135.8 3.6 %collective-permute-start.10 = (bf16[24,4096]{1,0:T(8,128)(2,1)S(1)}, bf16[24,4096]{1,0:T(8,128)(2,1)S(1)}, u32[]{:S(2)}, u32[]{:S(2)}) collective-permute-start(bf16[24,4096]{1,0:T(8,128)(2,1)S(1)} %get-tuple-element.38), channel_id=1, source_target_pairs={{0,16},{8,24},{16,0},{24,8},{32,48},{40,56},{48,32},{56,40},{64,80... | collective-permute-start | bytes 589832 | tf_op jit(solution)/shard_map/ppermute | solution.py:22
  139.8 2.1 collective-permute-start.13
  142.6 1.7 collective-permute-start.14
  144.2 3.5 %collective-permute-done.10 = bf16[24,4096]{1,0:T(8,128)(2,1)S(1)} collective-permute-done((bf16[24,4096]{1,0:T(8,128)(2,1)S(1)}, bf16[24,4096]{1,0:T(8,128)(2,1)S(1)}, u32[]{:S(2)}, u32[]{:S(2)}) %collective-permute-start.10) | collective-permute-done | bytes 196640 | tf_op jit(solution)/shard_map/ppermute | solution.py:22
  148.3 2.4 collective-permute-start.16
  150.8 2.2 collective-permute-start.17
  154.6 1.4 fusion.16
  157.3 1.4 fusion.34
  159.3 1.4 fusion.21
  160.7 6.5 %collective-permute-done.15 = bf16[4,24,4096]{2,1,0:T(8,128)(2,1)S(1)} collective-permute-done((bf16[4,24,4096]{2,1,0:T(8,128)(2,1)S(1)}, bf16[4,24,4096]{2,1,0:T(8,128)(2,1)S(1)}, u32[]{:S(2)}, u32[]{:S(2)}) %collective-permute-start.15) | collective-permute-done | bytes 786464 | tf_op jit(solution)/shard_map/ppermute | solution.py:22
  169.9 2.6 fusion.14
  172.5 2.7 multiply_convert_fusion
  175.2 2.8 %fusion.18 = bf16[384,4096]{1,0:T(8,128)(2,1)S(1)} fusion(bf16[384,768]{1,0:T(8,128)(2,1)S(1)} %multiply_convert_fusion, bf16[1,768,4096]{2,1,0:T(8,128)(2,1)S(1)} %bitcast.236), kind=kOutput, calls=%fused_computation.18 | convolution fusion | flops 2417491968 | bytes 10027008 | tf_op jit(solution)/shard_map/dot_general | solution.py:249
  178.3 3.9 %collective-permute-start.19 = (bf16[4,24,4096]{2,1,0:T(8,128)(2,1)S(1)}, bf16[4,24,4096]{2,1,0:T(8,128)(2,1)S(1)}, u32[]{:S(2)}, u32[]{:S(2)}) collective-permute-start(bf16[4,24,4096]{2,1,0:T(8,128)(2,1)S(1)} %get-tuple-element.17), channel_id=1, source_target_pairs={{0,96},{8,104},{16,112},{24,120},{32,0},{40,8},{48,16},{56,24},{64... | collective-permute-start | bytes 2359304 | tf_op jit(solution)/shard_map/ppermute | solution.py:22
  182.2 1.4 collective-permute-done.21
  183.7 1.4 fusion.12
  185.2 1.4 multiply_convert_fusion.2
  186.6 1.4 fusion.24
  188.2 4.1 %collective-permute-start.23 = (bf16[4,24,4096]{2,1,0:T(8,128)(2,1)S(1)}, bf16[4,24,4096]{2,1,0:T(8,128)(2,1)S(1)}, u32[]{:S(2)}, u32[]{:S(2)}) collective-permute-start(bf16[4,24,4096]{2,1,0:T(8,128)(2,1)S(1)} %bitcast.223), channel_id=1, source_target_pairs={{0,64},{8,72},{16,80},{24,88},{32,96},{40,104},{48,112},{56,120},{... | collective-permute-start | bytes 2359304 | tf_op jit(solution)/shard_map/ppermute | solution.py:22
  192.4 2.0 collective-permute-start.27
  194.8 1.8 collective-permute-start.29
  196.7 6.8 %collective-permute-done.20 = bf16[4,24,4096]{2,1,0:T(8,128)(2,1)S(1)} collective-permute-done((bf16[4,24,4096]{2,1,0:T(8,128)(2,1)S(1)}, bf16[4,24,4096]{2,1,0:T(8,128)(2,1)S(1)}, u32[]{:S(2)}, u32[]{:S(2)}) %collective-permute-start.20) | collective-permute-done | bytes 786464 | tf_op jit(solution)/shard_map/ppermute | solution.py:22
  204.0 3.3 %collective-permute-start.24 = (bf16[24,4096]{1,0:T(8,128)(2,1)S(1)}, bf16[24,4096]{1,0:T(8,128)(2,1)S(1)}, u32[]{:S(2)}, u32[]{:S(2)}) collective-permute-start(bf16[24,4096]{1,0:T(8,128)(2,1)S(1)} %get-tuple-element.25), channel_id=1, source_target_pairs={{0,24},{8,0},{16,8},{24,16},{32,56},{40,32},{48,40},{56,48},{64,88... | collective-permute-start | bytes 589832 | tf_op jit(solution)/shard_map/ppermute | solution.py:22
  207.3 5.6 %collective-permute-start.26 = (bf16[24,4096]{1,0:T(8,128)(2,1)S(1)}, bf16[24,4096]{1,0:T(8,128)(2,1)S(1)}, u32[]{:S(2)}, u32[]{:S(2)}) collective-permute-start(bf16[24,4096]{1,0:T(8,128)(2,1)S(1)} %get-tuple-element.26), channel_id=1, source_target_pairs={{0,16},{8,24},{16,0},{24,8},{32,48},{40,56},{48,32},{56,40},{64,80... | collective-permute-start | bytes 589832 | tf_op jit(solution)/shard_map/ppermute | solution.py:22
  213.0 3.5 %collective-permute-done.28 = bf16[4,24,4096]{2,1,0:T(8,128)(2,1)S(1)} collective-permute-done((bf16[4,24,4096]{2,1,0:T(8,128)(2,1)S(1)}, bf16[4,24,4096]{2,1,0:T(8,128)(2,1)S(1)}, u32[]{:S(2)}, u32[]{:S(2)}) %collective-permute-start.28) | collective-permute-done | bytes 786464 | tf_op jit(solution)/shard_map/ppermute | solution.py:22
  217.0 5.5 %collective-permute-start.30 = (bf16[24,4096]{1,0:T(8,128)(2,1)S(1)}, bf16[24,4096]{1,0:T(8,128)(2,1)S(1)}, u32[]{:S(2)}, u32[]{:S(2)}) collective-permute-start(bf16[24,4096]{1,0:T(8,128)(2,1)S(1)} %get-tuple-element.28), channel_id=1, source_target_pairs={{0,96},{8,104},{16,112},{24,120},{32,0},{40,8},{48,16},{56,24},{64... | collective-permute-start | bytes 589832 | tf_op jit(solution)/shard_map/ppermute | solution.py:22
  222.5 9.6 %collective-permute-start.31 = (bf16[24,4096]{1,0:T(8,128)(2,1)S(1)}, bf16[24,4096]{1,0:T(8,128)(2,1)S(1)}, u32[]{:S(2)}, u32[]{:S(2)}) collective-permute-start(bf16[24,4096]{1,0:T(8,128)(2,1)S(1)} %get-tuple-element.30), channel_id=1, source_target_pairs={{0,32},{8,40},{16,48},{24,56},{32,64},{40,72},{48,80},{56,88},{64,... | collective-permute-start | bytes 589832 | tf_op jit(solution)/shard_map/ppermute | solution.py:22
  232.2 4.9 %collective-permute-start.32 = (bf16[24,4096]{1,0:T(8,128)(2,1)S(1)}, bf16[24,4096]{1,0:T(8,128)(2,1)S(1)}, u32[]{:S(2)}, u32[]{:S(2)}) collective-permute-start(bf16[24,4096]{1,0:T(8,128)(2,1)S(1)} %get-tuple-element.29), channel_id=1, source_target_pairs={{0,64},{8,72},{16,80},{24,88},{32,96},{40,104},{48,112},{56,120},{... | collective-permute-start | bytes 589832 | tf_op jit(solution)/shard_map/ppermute | solution.py:22
  237.3 2.8 %collective-permute-done.32 = bf16[24,4096]{1,0:T(8,128)(2,1)S(1)} collective-permute-done((bf16[24,4096]{1,0:T(8,128)(2,1)S(1)}, bf16[24,4096]{1,0:T(8,128)(2,1)S(1)}, u32[]{:S(2)}, u32[]{:S(2)}) %collective-permute-start.32) | collective-permute-done | bytes 196640 | tf_op jit(solution)/shard_map/ppermute | solution.py:22
  241.2 19.4 %all-to-all-start.2 = ((bf16[8,48,512]{2,1,0:T(8,128)(2,1)}), bf16[8,48,512]{2,1,0:T(8,128)(2,1)S(1)}, u32[]{:S(2)}, u32[]{:S(2)}) async-start(bf16[8,48,512]{2,1,0:T(8,128)(2,1)} %copy.55), calls=%async_computation.2 | async-start | bytes 786432 | tf_op jit(solution)/shard_map/all_to_all | solution.py:263
  260.6 8.1 %all-to-all-done.2 = bf16[8,48,512]{2,1,0:T(8,128)(2,1)S(1)} async-done(((bf16[8,48,512]{2,1,0:T(8,128)(2,1)}), bf16[8,48,512]{2,1,0:T(8,128)(2,1)S(1)}, u32[]{:S(2)}, u32[]{:S(2)}) %all-to-all-start.2) | async-done | bytes 393248 | tf_op jit(solution)/shard_map/all_to_all | solution.py:263
  (136 shorter events, 25.2 us)
Async XLA Ops:
  6.5 32.3 %copy-start.11 = (f32[128,16]{0,1:T(8,128)S(1)}, f32[128,16]{0,1:T(8,128)}, u32[]{:S(2)}) copy-start(f32[128,16]{0,1:T(8,128)} %param.27) | copy-start | bytes 24580
  6.5 38.8 %copy-start.7 = (f32[1024]{0:T(1024)S(1)}, f32[1024]{0:T(1024)}, u32[]{:S(2)}) copy-start(f32[1024]{0:T(1024)} %param.28) | copy-start | bytes 12292
  6.5 38.8 %copy-start.2 = (bf16[128,1024]{1,0:T(8,128)(2,1)S(1)}, bf16[128,1024]{1,0:T(8,128)(2,1)}, u32[]{:S(2)}) copy-start(bf16[128,1024]{1,0:T(8,128)(2,1)} %gate_ref.1) | copy-start | bytes 786436
  6.5 84.1 %all-gather.3.cloned.1.call-start = ((), (), s32[]{:S(2)}) async-start(), calls=%async_computation.3 | async-start | bytes 4718592 | tf_op jit(solution)/shard_map/all_gather | solution.py:217
  8.0 5.6 %collective-permute-start = (bf16[8,1024]{1,0:T(8,128)(2,1)S(1)}, bf16[8,1024]{1,0:T(8,128)(2,1)S(1)}, u32[]{:S(2)}, u32[]{:S(2)}) collective-permute-start(bf16[8,1024]{1,0:T(8,128)(2,1)S(1)} %slice.144), channel_id=1, source_target_pairs={{0,8},{8,16},{16,24},{24,32},{32,40},{40,48},{48,56},{56,64},{64,7... | collective-permute-start | bytes 49160 | tf_op jit(solution)/shard_map/ppermute | solution.py:139
  22.6 5.2 %collective-permute-start.1 = (f32[17,8,128]{2,1,0:T(8,128)S(1)}, f32[17,8,128]{2,1,0:T(8,128)S(1)}, u32[]{:S(2)}, u32[]{:S(2)}) collective-permute-start(f32[17,8,128]{2,1,0:T(8,128)S(1)} %get-tuple-element.10), channel_id=1, source_target_pairs={{0,24},{8,0},{16,8},{24,16},{32,56},{40,32},{48,40},{56,48},{64,88... | collective-permute-start | bytes 208904 | tf_op jit(solution)/shard_map/ppermute | solution.py:22
  25.1 6.5 %collective-permute-start.2 = (f32[17,8,128]{2,1,0:T(8,128)S(1)}, f32[17,8,128]{2,1,0:T(8,128)S(1)}, u32[]{:S(2)}, u32[]{:S(2)}) collective-permute-start(f32[17,8,128]{2,1,0:T(8,128)S(1)} %get-tuple-element.10), channel_id=1, source_target_pairs={{0,16},{8,24},{16,0},{24,8},{32,48},{40,56},{48,32},{56,40},{64,80... | collective-permute-start | bytes 208904 | tf_op jit(solution)/shard_map/ppermute | solution.py:22
  25.6 10.4 %collective-permute-start.3 = (f32[17,8,128]{2,1,0:T(8,128)S(1)}, f32[17,8,128]{2,1,0:T(8,128)S(1)}, u32[]{:S(2)}, u32[]{:S(2)}) collective-permute-start(f32[17,8,128]{2,1,0:T(8,128)S(1)} %get-tuple-element.10), channel_id=1, source_target_pairs={{0,8},{8,16},{16,24},{24,0},{32,40},{40,48},{48,56},{56,32},{64,72... | collective-permute-start | bytes 208904 | tf_op jit(solution)/shard_map/ppermute | solution.py:22
  36.1 6.7 %collective-permute-start.5 = (f32[17,8,128]{2,1,0:T(8,128)S(1)}, f32[17,8,128]{2,1,0:T(8,128)S(1)}, u32[]{:S(2)}, u32[]{:S(2)}) collective-permute-start(f32[17,8,128]{2,1,0:T(8,128)S(1)} %pad_maximum_fusion.5), channel_id=1, source_target_pairs={{0,64},{8,72},{16,80},{24,88},{32,96},{40,104},{48,112},{56,120},{... | collective-permute-start | bytes 208904 | tf_op jit(solution)/shard_map/ppermute | solution.py:22
  38.9 6.3 %collective-permute-start.4 = (f32[17,8,128]{2,1,0:T(8,128)S(1)}, f32[17,8,128]{2,1,0:T(8,128)S(1)}, u32[]{:S(2)}, u32[]{:S(2)}) collective-permute-start(f32[17,8,128]{2,1,0:T(8,128)S(1)} %pad_maximum_fusion.5), channel_id=1, source_target_pairs={{0,32},{8,40},{16,48},{24,56},{32,64},{40,72},{48,80},{56,88},{64,... | collective-permute-start | bytes 208904 | tf_op jit(solution)/shard_map/ppermute | solution.py:22
  39.3 5.9 %collective-permute-start.6 = (f32[17,8,128]{2,1,0:T(8,128)S(1)}, f32[17,8,128]{2,1,0:T(8,128)S(1)}, u32[]{:S(2)}, u32[]{:S(2)}) collective-permute-start(f32[17,8,128]{2,1,0:T(8,128)S(1)} %pad_maximum_fusion.5), channel_id=1, source_target_pairs={{0,96},{8,104},{16,112},{24,120},{32,0},{40,8},{48,16},{56,24},{64... | collective-permute-start | bytes 208904 | tf_op jit(solution)/shard_map/ppermute | solution.py:22
  51.5 39.2 %copy-start = (bf16[128,1024]{1,0:T(8,128)(2,1)}, bf16[128,1024]{1,0:T(8,128)(2,1)S(1)}, u32[]{:S(2)}) copy-start(bf16[128,1024]{1,0:T(8,128)(2,1)S(1)} %scan_output.1.own_ref) | copy-start | bytes 786436
  51.5 13.4 %collective-permute-start.7 = (bf16[128,1024]{1,0:T(8,128)(2,1)S(1)}, bf16[128,1024]{1,0:T(8,128)(2,1)S(1)}, u32[]{:S(2)}, u32[]{:S(2)}) collective-permute-start(bf16[128,1024]{1,0:T(8,128)(2,1)S(1)} %scan_output.1.own_ref), channel_id=1, source_target_pairs={{0,8},{8,0},{16,24},{24,16},{32,40},{40,32},{48,56},{56,48},{64,72... | collective-permute-start | bytes 786440 | tf_op jit(solution)/shard_map/ppermute | solution.py:27
  64.9 25.8 %copy-start.9 = (bf16[128,1024]{1,0:T(8,128)(2,1)}, bf16[128,1024]{1,0:T(8,128)(2,1)S(1)}, u32[]{:S(2)}) copy-start(bf16[128,1024]{1,0:T(8,128)(2,1)S(1)} %collective-permute-done.7.other_ref) | copy-start | bytes 786436
  97.8 5.7 %copy-start.12 = (s32[128,2]{0,1:T(2,128)S(1)}, s32[128,2]{0,1:T(2,128)}, u32[]{:S(2)}) copy-start(s32[128,2]{0,1:T(2,128)} %param.30) | copy-start | bytes 3076
  97.8 20.8 %all-to-all-start = ((bf16[8,2,128,256]{3,2,1,0:T(8,128)(2,1)}), bf16[8,2,128,256]{3,2,1,0:T(8,128)(2,1)S(1)}, u32[]{:S(2)}, u32[]{:S(2)}) async-start(bf16[8,2,128,256]{3,2,1,0:T(8,128)(2,1)} %project.1), calls=%async_computation | async-start | bytes 2097152 | tf_op jit(solution)/shard_map/all_to_all | solution.py:182
  103.5 18.5 %copy-start.8 = (bf16[128,512]{1,0:T(8,128)(2,1)S(1)}, bf16[128,512]{1,0:T(8,128)(2,1)}, u32[]{:S(2)}) copy-start(bf16[128,512]{1,0:T(8,128)(2,1)} %param.18) | copy-start | bytes 393220
  118.8 3.2 %collective-permute-start.8 = (bf16[128,256]{1,0:T(8,128)(2,1)S(1)}, bf16[128,256]{1,0:T(8,128)(2,1)S(1)}, u32[]{:S(2)}, u32[]{:S(2)}) collective-permute-start(bf16[128,256]{1,0:T(8,128)(2,1)S(1)} %fusion.56), channel_id=1, source_target_pairs={{0,8},{8,0},{16,24},{24,16},{32,40},{40,32},{48,56},{56,48},{64,72... | collective-permute-start | bytes 196616 | tf_op jit(solution)/shard_map/ppermute | solution.py:27
  134.9 19.7 %slice-start = ((s8[6291456]{0:T(1024)(128)(4,1)}), s8[4194304]{0:T(1024)(128)(4,1)S(1)}, s32[]{:S(2)}) async-start(s8[6291456]{0:T(1024)(128)(4,1)} %bitcast.231), calls=%async_computation.4 | async-start | bytes 8388608
  135.7 6.8 %collective-permute-start.9 = (bf16[24,4096]{1,0:T(8,128)(2,1)S(1)}, bf16[24,4096]{1,0:T(8,128)(2,1)S(1)}, u32[]{:S(2)}, u32[]{:S(2)}) collective-permute-start(bf16[24,4096]{1,0:T(8,128)(2,1)S(1)} %get-tuple-element.38), channel_id=1, source_target_pairs={{0,8},{8,16},{16,24},{24,0},{32,40},{40,48},{48,56},{56,32},{64,72... | collective-permute-start | bytes 589832 | tf_op jit(solution)/shard_map/ppermute | solution.py:22
  135.8 11.9 %collective-permute-start.10 = (bf16[24,4096]{1,0:T(8,128)(2,1)S(1)}, bf16[24,4096]{1,0:T(8,128)(2,1)S(1)}, u32[]{:S(2)}, u32[]{:S(2)}) collective-permute-start(bf16[24,4096]{1,0:T(8,128)(2,1)S(1)} %get-tuple-element.38), channel_id=1, source_target_pairs={{0,16},{8,24},{16,0},{24,8},{32,48},{40,56},{48,32},{56,40},{64,80... | collective-permute-start | bytes 589832 | tf_op jit(solution)/shard_map/ppermute | solution.py:22
  139.4 8.3 %collective-permute-start.11 = (bf16[24,4096]{1,0:T(8,128)(2,1)S(1)}, bf16[24,4096]{1,0:T(8,128)(2,1)S(1)}, u32[]{:S(2)}, u32[]{:S(2)}) collective-permute-start(bf16[24,4096]{1,0:T(8,128)(2,1)S(1)} %get-tuple-element.38), channel_id=1, source_target_pairs={{0,24},{8,0},{16,8},{24,16},{32,56},{40,32},{48,40},{56,48},{64,88... | collective-permute-start | bytes 589832 | tf_op jit(solution)/shard_map/ppermute | solution.py:22
  139.8 10.9 %collective-permute-start.12 = (bf16[24,4096]{1,0:T(8,128)(2,1)S(1)}, bf16[24,4096]{1,0:T(8,128)(2,1)S(1)}, u32[]{:S(2)}, u32[]{:S(2)}) collective-permute-start(bf16[24,4096]{1,0:T(8,128)(2,1)S(1)} %get-tuple-element.37), channel_id=1, source_target_pairs={{0,32},{8,40},{16,48},{24,56},{32,64},{40,72},{48,80},{56,88},{64,... | collective-permute-start | bytes 589832 | tf_op jit(solution)/shard_map/ppermute | solution.py:22
  139.8 10.9 %collective-permute-start.13 = (bf16[24,4096]{1,0:T(8,128)(2,1)S(1)}, bf16[24,4096]{1,0:T(8,128)(2,1)S(1)}, u32[]{:S(2)}, u32[]{:S(2)}) collective-permute-start(bf16[24,4096]{1,0:T(8,128)(2,1)S(1)} %get-tuple-element.37), channel_id=1, source_target_pairs={{0,64},{8,72},{16,80},{24,88},{32,96},{40,104},{48,112},{56,120},{... | collective-permute-start | bytes 589832 | tf_op jit(solution)/shard_map/ppermute | solution.py:22
  142.6 8.1 %collective-permute-start.14 = (bf16[24,4096]{1,0:T(8,128)(2,1)S(1)}, bf16[24,4096]{1,0:T(8,128)(2,1)S(1)}, u32[]{:S(2)}, u32[]{:S(2)}) collective-permute-start(bf16[24,4096]{1,0:T(8,128)(2,1)S(1)} %get-tuple-element.37), channel_id=1, source_target_pairs={{0,96},{8,104},{16,112},{24,120},{32,0},{40,8},{48,16},{56,24},{64... | collective-permute-start | bytes 589832 | tf_op jit(solution)/shard_map/ppermute | solution.py:22
  147.7 6.8 %slice-start.1 = ((s8[6291456]{0:T(1024)(128)(4,1)}), s8[2097152]{0:T(1024)(128)(4,1)S(1)}, s32[]{:S(2)}) async-start(s8[6291456]{0:T(1024)(128)(4,1)} %bitcast.231), calls=%async_computation.5 | async-start | bytes 4194304
  147.9 19.3 %collective-permute-start.15 = (bf16[4,24,4096]{2,1,0:T(8,128)(2,1)S(1)}, bf16[4,24,4096]{2,1,0:T(8,128)(2,1)S(1)}, u32[]{:S(2)}, u32[]{:S(2)}) collective-permute-start(bf16[4,24,4096]{2,1,0:T(8,128)(2,1)S(1)} %get-tuple-element.32), channel_id=1, source_target_pairs={{0,32},{8,40},{16,48},{24,56},{32,64},{40,72},{48,80},{56,88},{64,... | collective-permute-start | bytes 2359304 | tf_op jit(solution)/shard_map/ppermute | solution.py:22
  148.3 20.2 %collective-permute-start.16 = (bf16[4,24,4096]{2,1,0:T(8,128)(2,1)S(1)}, bf16[4,24,4096]{2,1,0:T(8,128)(2,1)S(1)}, u32[]{:S(2)}, u32[]{:S(2)}) collective-permute-start(bf16[4,24,4096]{2,1,0:T(8,128)(2,1)S(1)} %get-tuple-element.32), channel_id=1, source_target_pairs={{0,96},{8,104},{16,112},{24,120},{32,0},{40,8},{48,16},{56,24},{64... | collective-permute-start | bytes 2359304 | tf_op jit(solution)/shard_map/ppermute | solution.py:22
  150.8 17.7 %collective-permute-start.17 = (bf16[4,24,4096]{2,1,0:T(8,128)(2,1)S(1)}, bf16[4,24,4096]{2,1,0:T(8,128)(2,1)S(1)}, u32[]{:S(2)}, u32[]{:S(2)}) collective-permute-start(bf16[4,24,4096]{2,1,0:T(8,128)(2,1)S(1)} %get-tuple-element.34), channel_id=1, source_target_pairs={{0,8},{8,16},{16,24},{24,0},{32,40},{40,48},{48,56},{56,32},{64,72... | collective-permute-start | bytes 2359304 | tf_op jit(solution)/shard_map/ppermute | solution.py:22
  153.0 16.4 %collective-permute-start.18 = (bf16[4,24,4096]{2,1,0:T(8,128)(2,1)S(1)}, bf16[4,24,4096]{2,1,0:T(8,128)(2,1)S(1)}, u32[]{:S(2)}, u32[]{:S(2)}) collective-permute-start(bf16[4,24,4096]{2,1,0:T(8,128)(2,1)S(1)} %get-tuple-element.34), channel_id=1, source_target_pairs={{0,24},{8,0},{16,8},{24,16},{32,56},{40,32},{48,40},{56,48},{64,88... | collective-permute-start | bytes 2359304 | tf_op jit(solution)/shard_map/ppermute | solution.py:22
  154.1 29.5 %collective-permute-start.21 = (bf16[4,24,4096]{2,1,0:T(8,128)(2,1)S(1)}, bf16[4,24,4096]{2,1,0:T(8,128)(2,1)S(1)}, u32[]{:S(2)}, u32[]{:S(2)}) collective-permute-start(bf16[4,24,4096]{2,1,0:T(8,128)(2,1)S(1)} %get-tuple-element.32), channel_id=1, source_target_pairs={{0,64},{8,72},{16,80},{24,88},{32,96},{40,104},{48,112},{56,120},{... | collective-permute-start | bytes 2359304 | tf_op jit(solution)/shard_map/ppermute | solution.py:22
  154.6 2.7 slice-start.3
  154.6 4.2 %slice-start.4 = ((s8[6291456]{0:T(1024)(128)(4,1)}), s8[4194304]{0:T(1024)(128)(4,1)S(1)}, s32[]{:S(2)}) async-start(s8[6291456]{0:T(1024)(128)(4,1)} %bitcast.235), calls=%async_computation.8 | async-start | bytes 8388608
  167.2 16.4 %collective-permute-start.22 = (bf16[4,24,4096]{2,1,0:T(8,128)(2,1)S(1)}, bf16[4,24,4096]{2,1,0:T(8,128)(2,1)S(1)}, u32[]{:S(2)}, u32[]{:S(2)}) collective-permute-start(bf16[4,24,4096]{2,1,0:T(8,128)(2,1)S(1)} %get-tuple-element.34), channel_id=1, source_target_pairs={{0,16},{8,24},{16,0},{24,8},{32,48},{40,56},{48,32},{56,40},{64,80... | collective-permute-start | bytes 2359304 | tf_op jit(solution)/shard_map/ppermute | solution.py:22
  178.3 16.6 %collective-permute-start.19 = (bf16[4,24,4096]{2,1,0:T(8,128)(2,1)S(1)}, bf16[4,24,4096]{2,1,0:T(8,128)(2,1)S(1)}, u32[]{:S(2)}, u32[]{:S(2)}) collective-permute-start(bf16[4,24,4096]{2,1,0:T(8,128)(2,1)S(1)} %get-tuple-element.17), channel_id=1, source_target_pairs={{0,96},{8,104},{16,112},{24,120},{32,0},{40,8},{48,16},{56,24},{64... | collective-permute-start | bytes 2359304 | tf_op jit(solution)/shard_map/ppermute | solution.py:22
  182.2 21.3 %collective-permute-start.20 = (bf16[4,24,4096]{2,1,0:T(8,128)(2,1)S(1)}, bf16[4,24,4096]{2,1,0:T(8,128)(2,1)S(1)}, u32[]{:S(2)}, u32[]{:S(2)}) collective-permute-start(bf16[4,24,4096]{2,1,0:T(8,128)(2,1)S(1)} %get-tuple-element.20), channel_id=1, source_target_pairs={{0,32},{8,40},{16,48},{24,56},{32,64},{40,72},{48,80},{56,88},{64,... | collective-permute-start | bytes 2359304 | tf_op jit(solution)/shard_map/ppermute | solution.py:22
  188.2 15.3 %collective-permute-start.23 = (bf16[4,24,4096]{2,1,0:T(8,128)(2,1)S(1)}, bf16[4,24,4096]{2,1,0:T(8,128)(2,1)S(1)}, u32[]{:S(2)}, u32[]{:S(2)}) collective-permute-start(bf16[4,24,4096]{2,1,0:T(8,128)(2,1)S(1)} %bitcast.223), channel_id=1, source_target_pairs={{0,64},{8,72},{16,80},{24,88},{32,96},{40,104},{48,112},{56,120},{... | collective-permute-start | bytes 2359304 | tf_op jit(solution)/shard_map/ppermute | solution.py:22
  192.4 14.9 %collective-permute-start.27 = (bf16[4,24,4096]{2,1,0:T(8,128)(2,1)S(1)}, bf16[4,24,4096]{2,1,0:T(8,128)(2,1)S(1)}, u32[]{:S(2)}, u32[]{:S(2)}) collective-permute-start(bf16[4,24,4096]{2,1,0:T(8,128)(2,1)S(1)} %get-tuple-element.19), channel_id=1, source_target_pairs={{0,24},{8,0},{16,8},{24,16},{32,56},{40,32},{48,40},{56,48},{64,88... | collective-permute-start | bytes 2359304 | tf_op jit(solution)/shard_map/ppermute | solution.py:22
  194.5 22.0 %collective-permute-start.28 = (bf16[4,24,4096]{2,1,0:T(8,128)(2,1)S(1)}, bf16[4,24,4096]{2,1,0:T(8,128)(2,1)S(1)}, u32[]{:S(2)}, u32[]{:S(2)}) collective-permute-start(bf16[4,24,4096]{2,1,0:T(8,128)(2,1)S(1)} %get-tuple-element.18), channel_id=1, source_target_pairs={{0,8},{8,16},{16,24},{24,0},{32,40},{40,48},{48,56},{56,32},{64,72... | collective-permute-start | bytes 2359304 | tf_op jit(solution)/shard_map/ppermute | solution.py:22
  194.8 21.6 %collective-permute-start.29 = (bf16[4,24,4096]{2,1,0:T(8,128)(2,1)S(1)}, bf16[4,24,4096]{2,1,0:T(8,128)(2,1)S(1)}, u32[]{:S(2)}, u32[]{:S(2)}) collective-permute-start(bf16[4,24,4096]{2,1,0:T(8,128)(2,1)S(1)} %bitcast.220), channel_id=1, source_target_pairs={{0,16},{8,24},{16,0},{24,8},{32,48},{40,56},{48,32},{56,40},{64,80... | collective-permute-start | bytes 2359304 | tf_op jit(solution)/shard_map/ppermute | solution.py:22
  204.0 28.1 %collective-permute-start.24 = (bf16[24,4096]{1,0:T(8,128)(2,1)S(1)}, bf16[24,4096]{1,0:T(8,128)(2,1)S(1)}, u32[]{:S(2)}, u32[]{:S(2)}) collective-permute-start(bf16[24,4096]{1,0:T(8,128)(2,1)S(1)} %get-tuple-element.25), channel_id=1, source_target_pairs={{0,24},{8,0},{16,8},{24,16},{32,56},{40,32},{48,40},{56,48},{64,88... | collective-permute-start | bytes 589832 | tf_op jit(solution)/shard_map/ppermute | solution.py:22
  207.3 29.7 %collective-permute-start.25 = (bf16[24,4096]{1,0:T(8,128)(2,1)S(1)}, bf16[24,4096]{1,0:T(8,128)(2,1)S(1)}, u32[]{:S(2)}, u32[]{:S(2)}) collective-permute-start(bf16[24,4096]{1,0:T(8,128)(2,1)S(1)} %get-tuple-element.27), channel_id=1, source_target_pairs={{0,8},{8,16},{16,24},{24,0},{32,40},{40,48},{48,56},{56,32},{64,72... | collective-permute-start | bytes 589832 | tf_op jit(solution)/shard_map/ppermute | solution.py:22
  207.3 29.7 %collective-permute-start.26 = (bf16[24,4096]{1,0:T(8,128)(2,1)S(1)}, bf16[24,4096]{1,0:T(8,128)(2,1)S(1)}, u32[]{:S(2)}, u32[]{:S(2)}) collective-permute-start(bf16[24,4096]{1,0:T(8,128)(2,1)S(1)} %get-tuple-element.26), channel_id=1, source_target_pairs={{0,16},{8,24},{16,0},{24,8},{32,48},{40,56},{48,32},{56,40},{64,80... | collective-permute-start | bytes 589832 | tf_op jit(solution)/shard_map/ppermute | solution.py:22
  217.0 20.3 %collective-permute-start.30 = (bf16[24,4096]{1,0:T(8,128)(2,1)S(1)}, bf16[24,4096]{1,0:T(8,128)(2,1)S(1)}, u32[]{:S(2)}, u32[]{:S(2)}) collective-permute-start(bf16[24,4096]{1,0:T(8,128)(2,1)S(1)} %get-tuple-element.28), channel_id=1, source_target_pairs={{0,96},{8,104},{16,112},{24,120},{32,0},{40,8},{48,16},{56,24},{64... | collective-permute-start | bytes 589832 | tf_op jit(solution)/shard_map/ppermute | solution.py:22
  222.5 14.7 %collective-permute-start.31 = (bf16[24,4096]{1,0:T(8,128)(2,1)S(1)}, bf16[24,4096]{1,0:T(8,128)(2,1)S(1)}, u32[]{:S(2)}, u32[]{:S(2)}) collective-permute-start(bf16[24,4096]{1,0:T(8,128)(2,1)S(1)} %get-tuple-element.30), channel_id=1, source_target_pairs={{0,32},{8,40},{16,48},{24,56},{32,64},{40,72},{48,80},{56,88},{64,... | collective-permute-start | bytes 589832 | tf_op jit(solution)/shard_map/ppermute | solution.py:22
  232.2 8.0 %collective-permute-start.32 = (bf16[24,4096]{1,0:T(8,128)(2,1)S(1)}, bf16[24,4096]{1,0:T(8,128)(2,1)S(1)}, u32[]{:S(2)}, u32[]{:S(2)}) collective-permute-start(bf16[24,4096]{1,0:T(8,128)(2,1)S(1)} %get-tuple-element.29), channel_id=1, source_target_pairs={{0,64},{8,72},{16,80},{24,88},{32,96},{40,104},{48,112},{56,120},{... | collective-permute-start | bytes 589832 | tf_op jit(solution)/shard_map/ppermute | solution.py:22
  240.2 20.4 %copy-start.13 = (f32[128,2]{0,1:T(2,128)S(1)}, f32[128,2]{0,1:T(2,128)}, u32[]{:S(2)}) copy-start(f32[128,2]{0,1:T(2,128)} %param.31) | copy-start | bytes 3076
  241.2 27.5 %all-to-all-start.2 = ((bf16[8,48,512]{2,1,0:T(8,128)(2,1)}), bf16[8,48,512]{2,1,0:T(8,128)(2,1)S(1)}, u32[]{:S(2)}, u32[]{:S(2)}) async-start(bf16[8,48,512]{2,1,0:T(8,128)(2,1)} %copy.55), calls=%async_computation.2 | async-start | bytes 786432 | tf_op jit(solution)/shard_map/all_to_all | solution.py:263
  (8 other events, 8.9 us)
Sparse Core Ops, SparseCore 0:
  9.7 80.9 all-gather.2

commit v3 on v2

--- a/solution.py
+++ b/solution.py
@@ -102,7 +102,7 @@
         out_ref[:, cols] = (y_ref[:, k, :] * (gate * jax.nn.sigmoid(gate))).astype(BF16)
 
 
-def entering_state(final, rate):
+def entering_state(final, rate, ahead):
     along_x = lax.axis_index("seq") % SIDE
     along_y = lax.axis_index("seq") // SIDE
 
@@ -129,14 +129,22 @@
     for d in (3, 2, 1):
         total = chain(total, masked(others[d - 1], along_x < d))
     packed = jnp.concatenate([total[0], total[1][None]], 0)
+    packed, ahead = lax.optimization_barrier((packed, ahead))
     before_y, _ = spread(packed, "y", along_y)
-    return chain(before_y, before_x)[0]
-
-
-def mixer(mixer_in, gate_in, dt_raw, dt_bias, a_log, conv_weight, conv_bias, b_proj, c_proj, d_skip):
+    return chain(before_y, before_x)[0], ahead
+
+
+def mixer(
+    mixer_in, gate_in, dt_raw, dt_bias, a_log, conv_weight, conv_bias, b_proj, c_proj, d_skip, w_out
+):
     tokens, channels = mixer_in.shape
     count, index = lax.axis_size("seq"), lax.axis_index("seq")
     rim = lax.ppermute(mixer_in[tokens - 8 :], "seq", [(i, i + 1) for i in range(count - 1)])
+    split = 3 * channels // 8
+    low, high = w_out[:split], w_out[split:]
+    low_pair = jnp.stack([low, shift(low, "x", 2)])
+    dt_raw, low_pair = lax.optimization_barrier((dt_raw, low_pair))
+    high_ring = ring_gather(high, "y")
     rate = (-LOG2E * jnp.exp(a_log)).T.reshape(STATES, 8, 128)
     vmem = pl.BlockSpec(memory_space=pltpu.VMEM)
     smem = pl.BlockSpec(memory_space=pltpu.SMEM)
@@ -150,8 +158,12 @@
         compiler_params=pltpu.CompilerParams(vmem_limit_bytes=32 << 20),
         name="scan_state",
     )(mixer_in, rim, dt_raw, dt_bias[None, :], conv_weight.T, conv_bias[None, :], rate, b_proj)
-    enter = entering_state(final, rate)
-    return pl.pallas_call(
+    final, high_ring = lax.optimization_barrier((final, high_ring))
+    first = ring_gather(low_pair, "y")
+    high_ring = jnp.stack(high_ring)
+    second = [high_ring, shift(high_ring, "x", 2)]
+    enter, first = entering_state(final, rate, first)
+    mixed = pl.pallas_call(
         second_pass,
         out_shape=jax.ShapeDtypeStruct((tokens, channels), BF16),
         in_specs=[vmem] * 6 + [smem] * 2,
@@ -160,25 +172,36 @@
         compiler_params=pltpu.CompilerParams(vmem_limit_bytes=32 << 20),
         name="scan_output",
     )(step, act, gate_in, enter, rate, d_skip.reshape(8, 128), b_proj, c_proj)
-
-
-def project_kernel(own_ref, other_ref, weight_ref, out_ref):
-    for k, rows in enumerate((own_ref, other_ref)):
-        out_ref[0, k] = jnp.dot(rows[...], weight_ref[0], preferred_element_type=F32).astype(BF16)
+    return mixed, (first, second)
+
+
+def project_kernel(place_ref, own_ref, other_ref, *refs):
+    first, second, out_ref = refs[:SIDE], refs[SIDE : SIDE + 2], refs[SIDE + 2]
+    split = first[0].shape[1]
+    y, side = place_ref[0], place_ref[1]
+    for i in range(SIDE):
+        for j in range(2):
+            owner = lax.rem(y - i + SIDE, SIDE) * 2 + lax.rem(side + j, 2)
+            for k, rows in enumerate((own_ref, other_ref)):
+                total = jnp.dot(rows[:, :split], first[i][j], preferred_element_type=F32)
+                total += jnp.dot(rows[:, split:], second[j][i], preferred_element_type=F32)
+                out_ref[owner, k] = total.astype(BF16)
 
 
 def project(mixed, weights):
-    owners, channels, columns = weights.shape
-    tokens = mixed.shape[0]
-    whole = pl.BlockSpec((tokens, channels), lambda e: (0, 0))
+    first, second = weights
+    tokens, columns = mixed.shape[0], first[0].shape[2]
+    index = lax.axis_index("seq")
+    place = jnp.stack([index // SIDE, index % SIDE // 2]).astype(jnp.int32)
+    vmem = pl.BlockSpec(memory_space=pltpu.VMEM)
     partial = pl.pallas_call(
         project_kernel,
-        grid=(owners,),
-        out_shape=jax.ShapeDtypeStruct((owners, 2, tokens, columns), BF16),
-        in_specs=[whole, whole, pl.BlockSpec((1, channels, columns), lambda e: (e, 0, 0))],
-        out_specs=pl.BlockSpec((1, 2, tokens, columns), lambda e: (e, 0, 0, 0)),
+        out_shape=jax.ShapeDtypeStruct((2 * SIDE, 2, tokens, columns), BF16),
+        in_specs=[pl.BlockSpec(memory_space=pltpu.SMEM)] + [vmem] * (SIDE + 4),
+        out_specs=vmem,
+        compiler_params=pltpu.CompilerParams(vmem_limit_bytes=40 << 20),
         name="project",
-    )(mixed, partner(mixed), weights)
+    )(place, mixed, partner(mixed), *first, *second)
     partial = lax.all_to_all(partial, "exp", split_axis=0, concat_axis=0)
     total = jnp.sum(partial.astype(F32), axis=0)
     other = partner(total[1].astype(BF16)).astype(F32)
@@ -213,12 +236,10 @@
     groups = lax.axis_size("seq")
     capacity = 3 * tokens // experts
     width = stream.shape[1]
-    parity = [[i for i in range(groups) if i % 2 == p] for p in range(2)]
-    out_blocks = lax.all_gather(w_out, "seq", axis=0, axis_index_groups=parity)
-    mixed = mixer(
-        mixer_in, gate_in, dt_raw, dt_bias, a_log, conv_weight, conv_bias, b_proj, c_proj, d_skip
+    mixed, weights = mixer(
+        mixer_in, gate_in, dt_raw, dt_bias, a_log, conv_weight, conv_bias, b_proj, c_proj, d_skip, w_out
     )
-    projected = project(mixed, out_blocks)
+    projected = project(mixed, weights)
     middle = (stream.astype(F32) + projected).astype(BF16)
 
     flat_exp = expert_index.reshape(-1)

time: 278 us -> 260 us (0.935)
  waiting for transfers between devices: 105 us -> 74.9 us
  starting transfers between devices: 94.4 us -> 116 us
  between operations: 13.9 us -> 0.67 us
  local copies, waits for them, and re-layouts: 10.3 us -> 15.9 us
  Pallas kernels: 18.2 us -> 14.6 us
    all_gather x1 -> x0, waiting for transfers between devices: 25.8 us -> none  [local(): out_blocks = lax.all_gather(w_out, 'seq', axis=0, axis_index_groups=parity)]
    all_to_all x1, starting transfers between devices: 5.74 us -> 29.5 us  [project(): partial = lax.all_to_all(partial, 'exp', split_axis=0, concat_axis=0)]
    ppermute x2, waiting for transfers between devices: 16.4 us -> 10.9 us  [partner(): return lax.ppermute(value, 'seq', [(i, i ^ 1) for i in cells])]
    unnamed x47 -> x65, local copies, waits for them, and re-layouts: 7.38 us -> 11 us
    pallas_call x1, Pallas kernels: 7.11 us -> 3.5 us  [project(): pl.pallas_call(project_kernel, out_shape=jax.ShapeDtypeStruct((2 * SIDE,...]
    ppermute x30 -> x38, waiting for transfers between devices: 40.2 us -> 42.4 us  [shift(): return lax.ppermute(value, 'seq', route)]
    ppermute x30 -> x38, starting transfers between devices: 65.2 us -> 65 us  [shift(): return lax.ppermute(value, 'seq', route)]
  transfers between devices with their start and end apart: 36 -> 43, of which waited for: 19 -> 18; matrix products, arithmetic and copies ran while one was open for 9% -> 10% of each run, Pallas kernels for 4% -> 4%
where the time goes in v3:
time: 260 us; the launch traced here: 259 us
  starting transfers between devices  116 us (45%)
  waiting for transfers between devices  74.9 us (29%)
  matrix products  18.2 us (7%)
  local copies, waits for them, and re-layouts  15.9 us (6%)
  Pallas kernels  14.6 us (6%)
  blocking collectives  12.5 us (5%)
  other arithmetic  5.53 us (2%)
    ppermute x38, starting transfers between devices, shift(): return lax.ppermute(value, 'seq', route)  65 us
    ppermute x38, waiting for transfers between devices, shift(): return lax.ppermute(value, 'seq', route)  42.4 us
    all_to_all x1, starting transfers between devices, project(): partial = lax.all_to_all(partial, 'exp', split_axis=0, concat_axis=0)  29.5 us
    all_to_all x1, starting transfers between devices, local(): returned = lax.all_to_all(summed, 'exp', split_axis=0, concat_axis=0)  18.1 us
    all_to_all x1, waiting for transfers between devices, project(): partial = lax.all_to_all(partial, 'exp', split_axis=0, concat_axis=0)  13.5 us
    all_to_all x1, blocking collectives, local(): lax.all_to_all(outgoing, 'exp', split_axis=0, concat_axis=2, tiled=True)[0]  12.5 us
    unnamed x65, local copies, waits for them, and re-layouts  11 us
    ppermute x2, waiting for transfers between devices, partner(): return lax.ppermute(value, 'seq', [(i, i ^ 1) for i in cells])  10.9 us
  transfers between devices with their start and end apart: 43, of which 18 were waited for; matrix products, arithmetic and copies ran while one was open for 10% of the time, Pallas kernels for 4%

profile of v3, /device:TPU:1, one launch (start us, length us, event | category | flops | bytes accessed | tf_op | source)
XLA Modules:
  0.0 258.8 jit_solution(1493020917953642417)
XLA Ops:
  1.1 2.2 collective-permute-start.2
  3.3 2.6 %collective-permute-start.3 = (bf16[640,256]{1,0:T(8,128)(2,1)S(1)}, bf16[640,256]{1,0:T(8,128)(2,1)S(1)}, u32[]{:S(2)}, u32[]{:S(2)}) collective-permute-start(bf16[640,256]{1,0:T(8,128)(2,1)S(1)} %slice.152), channel_id=1, source_target_pairs={{0,64},{8,72},{16,80},{24,88},{32,96},{40,104},{48,112},{56,120},{... | collective-permute-start | bytes 983048 | tf_op jit(solution)/shard_map/ppermute | solution.py:22
  7.9 2.8 %collective-permute-start.1 = (bf16[384,256]{1,0:T(8,128)(2,1)S(1)}, bf16[384,256]{1,0:T(8,128)(2,1)S(1)}, u32[]{:S(2)}, u32[]{:S(2)}) collective-permute-start(bf16[384,256]{1,0:T(8,128)(2,1)S(1)} %get-tuple-element.60), channel_id=1, source_target_pairs={{0,16},{8,24},{16,0},{24,8},{32,48},{40,56},{48,32},{56,40},{64,80... | collective-permute-start | bytes 589832 | tf_op jit(solution)/shard_map/ppermute | solution.py:22
  11.5 2.2 collective-permute-start
  14.9 3.7 %collective-permute-start.8 = (bf16[2,384,256]{2,1,0:T(8,128)(2,1)S(1)}, bf16[2,384,256]{2,1,0:T(8,128)(2,1)S(1)}, u32[]{:S(2)}, u32[]{:S(2)}) collective-permute-start(bf16[2,384,256]{2,1,0:T(8,128)(2,1)S(1)} %pad_maximum_fusion.6.refs_0_), channel_id=1, source_target_pairs={{0,32},{8,40},{16,48},{24,56},{32,64},{40,72},{48,80},{56,88},{64,... | collective-permute-start | bytes 1179656 | tf_op jit(solution)/shard_map/ppermute | solution.py:22
  18.6 4.9 %scan_state.1 = (f32[128,8,128]{2,1,0:T(8,128)S(1)}, f32[128,8,128]{2,1,0:T(8,128)S(1)}, f32[17,8,128]{2,1,0:T(8,128)S(1)}) custom-call(bf16[128,1024]{1,0:T(8,128)(2,1)S(1)} %copy-done.10, bf16[8,1024]{1,0:T(8,128)(2,1)S(1)} %collective-permute-done.rim_ref, bf16[128,1024]{1,0:T(8,128)(2,1)S(1)} %copy-done.12, f32[1,1024]{1,0:T(1,128)S(1)} %bitcast.203, ...), custom_call_target="tpu_custom_call" | custom-call | tf_op jit(solution)/shard_map/scan_state/pallas_call | solution.py:152
  25.3 1.8 collective-permute-done.5
  32.1 3.2 %collective-permute-done.9.refs_2_ = bf16[2,384,256]{2,1,0:T(8,128)(2,1)S(1)} collective-permute-done((bf16[2,384,256]{2,1,0:T(8,128)(2,1)S(1)}, bf16[2,384,256]{2,1,0:T(8,128)(2,1)S(1)}, u32[]{:S(2)}, u32[]{:S(2)}) %collective-permute-start.9) | collective-permute-done | bytes 393248 | tf_op jit(solution)/shard_map/ppermute | solution.py:22
  38.0 1.6 collective-permute-start.13
  39.6 1.5 collective-permute-done.12
  45.1 6.1 %scan_output.1.own_ref = bf16[128,1024]{1,0:T(8,128)(2,1)S(1)} custom-call(f32[128,8,128]{2,1,0:T(8,128)S(1)} %copy-done.1, f32[128,8,128]{2,1,0:T(8,128)S(1)} %copy-done.3, bf16[128,1024]{1,0:T(8,128)(2,1)S(1)} %copy-done.11, f32[16,8,128]{2,1,0:T(8,128)S(1)} %fusion.59.enter_ref, f32[16,8,128]{2,1,0:T(8,128)S(1)} %bitcast.201, f32[8,128]{1,0:T(8,128)S(1)} %bitcast.205, ...), custom_call_target="tpu_custom_call" | custom-call | tf_op jit(solution)/shard_map/scan_output/pallas_call | solution.py:166
  51.2 1.6 collective-permute-start.14
  52.8 7.9 %collective-permute-done.14.other_ref = bf16[128,1024]{1,0:T(8,128)(2,1)} collective-permute-done((bf16[128,1024]{1,0:T(8,128)(2,1)S(1)}, bf16[128,1024]{1,0:T(8,128)(2,1)}, u32[]{:S(2)}, u32[]{:S(2)}) %collective-permute-start.14) | collective-permute-done | bytes 262176 | tf_op jit(solution)/shard_map/ppermute | solution.py:27
  63.7 3.5 %project.1 = bf16[8,2,128,256]{3,2,1,0:T(8,128)(2,1)} custom-call(s32[2]{0:T(128)S(1)} %pad_add_fusion.place_ref, bf16[128,1024]{1,0:T(8,128)(2,1)S(1)} %scan_output.1.own_ref, bf16[128,1024]{1,0:T(8,128)(2,1)} %collective-permute-done.14.other_ref, bf16[2,384,256]{2,1,0:T(8,128)(2,1)S(1)} %pad_maximum_fusion.6.refs_0_, bf16[2,384,256]{2,1,0:T(8,128)(2,1)S(1)} %copy-done.7, ...), custom_call_target="tpu_custom_call" | custom-call | tf_op jit(solution)/shard_map/project/pallas_call | solution.py:197
  67.2 29.5 %all-to-all-start = ((bf16[8,2,128,256]{3,2,1,0:T(8,128)(2,1)}), bf16[8,2,128,256]{3,2,1,0:T(8,128)(2,1)S(1)}, u32[]{:S(2)}, u32[]{:S(2)}) async-start(bf16[8,2,128,256]{3,2,1,0:T(8,128)(2,1)} %project.1), calls=%async_computation | async-start | bytes 2097152 | tf_op jit(solution)/shard_map/all_to_all | solution.py:205
  98.2 13.5 %all-to-all-done = bf16[8,2,128,256]{3,2,1,0:T(8,128)(2,1)S(1)} async-done(((bf16[8,2,128,256]{3,2,1,0:T(8,128)(2,1)}), bf16[8,2,128,256]{3,2,1,0:T(8,128)(2,1)S(1)}, u32[]{:S(2)}, u32[]{:S(2)}) %all-to-all-start) | async-done | bytes 1048608 | tf_op jit(solution)/shard_map/all_to_all | solution.py:205
  112.0 3.1 %collective-permute-done.16 = bf16[128,256]{1,0:T(8,128)(2,1)S(1)} collective-permute-done((bf16[128,256]{1,0:T(8,128)(2,1)S(1)}, bf16[128,256]{1,0:T(8,128)(2,1)S(1)}, u32[]{:S(2)}, u32[]{:S(2)}) %collective-permute-start.16) | collective-permute-done | bytes 65568 | tf_op jit(solution)/shard_map/ppermute | solution.py:27
  115.4 12.5 %all_to_all.19 = bf16[8,48,512]{2,1,0:T(8,128)(2,1)S(1)} all-to-all(bf16[8,48,512]{2,1,0:T(8,128)(2,1)S(1)} %bitcast.218), channel_id=1, replica_groups=mesh['seq'=16,'exp'=8] {'exp'}, dimensions={0} | all-to-all | bytes 786432 | tf_op jit(solution)/shard_map/all_to_all | solution.py:256
  129.2 2.4 collective-permute-start.19
  131.6 2.4 collective-permute-start.21
  134.0 6.3 %collective-permute-done.17 = bf16[24,4096]{1,0:T(8,128)(2,1)S(1)} collective-permute-done((bf16[24,4096]{1,0:T(8,128)(2,1)S(1)}, bf16[24,4096]{1,0:T(8,128)(2,1)S(1)}, u32[]{:S(2)}, u32[]{:S(2)}) %collective-permute-start.17) | collective-permute-done | bytes 196640 | tf_op jit(solution)/shard_map/ppermute | solution.py:22
  142.0 1.7 collective-permute-start.24
  143.8 1.6 collective-permute-done.22
  145.6 2.7 %collective-permute-start.26 = (bf16[4,24,4096]{2,1,0:T(8,128)(2,1)S(1)}, bf16[4,24,4096]{2,1,0:T(8,128)(2,1)S(1)}, u32[]{:S(2)}, u32[]{:S(2)}) collective-permute-start(bf16[4,24,4096]{2,1,0:T(8,128)(2,1)S(1)} %get-tuple-element.58), channel_id=1, source_target_pairs={{0,24},{8,0},{16,8},{24,16},{32,56},{40,32},{48,40},{56,48},{64,88... | collective-permute-start | bytes 2359304 | tf_op jit(solution)/shard_map/ppermute | solution.py:22
  148.6 1.4 fusion.16
  151.3 1.4 fusion.34
  154.7 5.0 %collective-permute-done.23 = bf16[4,24,4096]{2,1,0:T(8,128)(2,1)S(1)} collective-permute-done((bf16[4,24,4096]{2,1,0:T(8,128)(2,1)S(1)}, bf16[4,24,4096]{2,1,0:T(8,128)(2,1)S(1)}, u32[]{:S(2)}, u32[]{:S(2)}) %collective-permute-start.23) | collective-permute-done | bytes 786464 | tf_op jit(solution)/shard_map/ppermute | solution.py:22
  159.7 3.0 %collective-permute-start.30 = (bf16[4,24,4096]{2,1,0:T(8,128)(2,1)S(1)}, bf16[4,24,4096]{2,1,0:T(8,128)(2,1)S(1)}, u32[]{:S(2)}, u32[]{:S(2)}) collective-permute-start(bf16[4,24,4096]{2,1,0:T(8,128)(2,1)S(1)} %get-tuple-element.58), channel_id=1, source_target_pairs={{0,16},{8,24},{16,0},{24,8},{32,48},{40,56},{48,32},{56,40},{64,80... | collective-permute-start | bytes 2359304 | tf_op jit(solution)/shard_map/ppermute | solution.py:22
  163.2 2.6 %fusion.14 = f32[384,768]{1,0:T(8,128)S(1)} fusion(bf16[384,4096]{1,0:T(8,128)(2,1)S(1)} %bitcast.208, bf16[1,4096,768]{2,1,0:T(8,128)(2,1)S(1)} %bitcast.244), kind=kOutput, calls=%fused_computation.14 | convolution fusion | flops 2415919104 | bytes 10616832 | tf_op jit(solution)/shard_map/dot_general | solution.py:267
  165.8 2.7 %multiply_convert_fusion = bf16[384,768]{1,0:T(8,128)(2,1)S(1)} fusion(f32[384,768]{1,0:T(8,128)S(1)} %fusion.14, bf16[384,4096]{1,0:T(8,128)(2,1)S(1)} %bitcast.209, bf16[1,4096,768]{2,1,0:T(8,128)(2,1)S(1)} %bitcast.246), kind=kOutput, calls=%fused_computation.35 | convolution fusion | flops 2417688576 | bytes 11206656 | tf_op jit(solution)/shard_map/dot_general | solution.py:268
  168.5 2.8 %fusion.18 = bf16[384,4096]{1,0:T(8,128)(2,1)S(1)} fusion(bf16[384,768]{1,0:T(8,128)(2,1)S(1)} %multiply_convert_fusion, bf16[1,768,4096]{2,1,0:T(8,128)(2,1)S(1)} %bitcast.248), kind=kOutput, calls=%fused_computation.18 | convolution fusion | flops 2417491968 | bytes 10027008 | tf_op jit(solution)/shard_map/dot_general | solution.py:270
  171.6 1.8 collective-permute-start.27
  173.3 2.4 collective-permute-done.29
  175.9 1.4 fusion.12
  177.4 1.4 multiply_convert_fusion.2
  180.4 5.0 %collective-permute-start.31 = (bf16[4,24,4096]{2,1,0:T(8,128)(2,1)S(1)}, bf16[4,24,4096]{2,1,0:T(8,128)(2,1)S(1)}, u32[]{:S(2)}, u32[]{:S(2)}) collective-permute-start(bf16[4,24,4096]{2,1,0:T(8,128)(2,1)S(1)} %bitcast.231), channel_id=1, source_target_pairs={{0,64},{8,72},{16,80},{24,88},{32,96},{40,104},{48,112},{56,120},{... | collective-permute-start | bytes 2359304 | tf_op jit(solution)/shard_map/ppermute | solution.py:22
  185.5 1.8 collective-permute-start.35
  187.3 2.1 collective-permute-done.27
  189.4 6.5 %collective-permute-done.28 = bf16[4,24,4096]{2,1,0:T(8,128)(2,1)S(1)} collective-permute-done((bf16[4,24,4096]{2,1,0:T(8,128)(2,1)S(1)}, bf16[4,24,4096]{2,1,0:T(8,128)(2,1)S(1)}, u32[]{:S(2)}, u32[]{:S(2)}) %collective-permute-start.28) | collective-permute-done | bytes 786464 | tf_op jit(solution)/shard_map/ppermute | solution.py:22
  196.4 2.8 %collective-permute-start.32 = (bf16[24,4096]{1,0:T(8,128)(2,1)S(1)}, bf16[24,4096]{1,0:T(8,128)(2,1)S(1)}, u32[]{:S(2)}, u32[]{:S(2)}) collective-permute-start(bf16[24,4096]{1,0:T(8,128)(2,1)S(1)} %get-tuple-element.49), channel_id=1, source_target_pairs={{0,24},{8,0},{16,8},{24,16},{32,56},{40,32},{48,40},{56,48},{64,88... | collective-permute-start | bytes 589832 | tf_op jit(solution)/shard_map/ppermute | solution.py:22
  199.9 2.6 %collective-permute-start.34 = (bf16[24,4096]{1,0:T(8,128)(2,1)S(1)}, bf16[24,4096]{1,0:T(8,128)(2,1)S(1)}, u32[]{:S(2)}, u32[]{:S(2)}) collective-permute-start(bf16[24,4096]{1,0:T(8,128)(2,1)S(1)} %get-tuple-element.50), channel_id=1, source_target_pairs={{0,16},{8,24},{16,0},{24,8},{32,48},{40,56},{48,32},{56,40},{64,80... | collective-permute-start | bytes 589832 | tf_op jit(solution)/shard_map/ppermute | solution.py:22
  202.5 4.1 %collective-permute-done.36 = bf16[4,24,4096]{2,1,0:T(8,128)(2,1)S(1)} collective-permute-done((bf16[4,24,4096]{2,1,0:T(8,128)(2,1)S(1)}, bf16[4,24,4096]{2,1,0:T(8,128)(2,1)S(1)}, u32[]{:S(2)}, u32[]{:S(2)}) %collective-permute-start.36) | collective-permute-done | bytes 786464 | tf_op jit(solution)/shard_map/ppermute | solution.py:22
  206.6 3.5 %collective-permute-done.37 = bf16[4,24,4096]{2,1,0:T(8,128)(2,1)S(1)} collective-permute-done((bf16[4,24,4096]{2,1,0:T(8,128)(2,1)S(1)}, bf16[4,24,4096]{2,1,0:T(8,128)(2,1)S(1)}, u32[]{:S(2)}, u32[]{:S(2)}) %collective-permute-start.37) | collective-permute-done | bytes 786464 | tf_op jit(solution)/shard_map/ppermute | solution.py:22
  211.4 10.3 %collective-permute-start.39 = (bf16[24,4096]{1,0:T(8,128)(2,1)S(1)}, bf16[24,4096]{1,0:T(8,128)(2,1)S(1)}, u32[]{:S(2)}, u32[]{:S(2)}) collective-permute-start(bf16[24,4096]{1,0:T(8,128)(2,1)S(1)} %get-tuple-element.54), channel_id=1, source_target_pairs={{0,32},{8,40},{16,48},{24,56},{32,64},{40,72},{48,80},{56,88},{64,... | collective-permute-start | bytes 589832 | tf_op jit(solution)/shard_map/ppermute | solution.py:22
  221.7 5.4 %collective-permute-start.40 = (bf16[24,4096]{1,0:T(8,128)(2,1)S(1)}, bf16[24,4096]{1,0:T(8,128)(2,1)S(1)}, u32[]{:S(2)}, u32[]{:S(2)}) collective-permute-start(bf16[24,4096]{1,0:T(8,128)(2,1)S(1)} %get-tuple-element.53), channel_id=1, source_target_pairs={{0,64},{8,72},{16,80},{24,88},{32,96},{40,104},{48,112},{56,120},{... | collective-permute-start | bytes 589832 | tf_op jit(solution)/shard_map/ppermute | solution.py:22
  227.4 2.8 %collective-permute-done.40 = bf16[24,4096]{1,0:T(8,128)(2,1)S(1)} collective-permute-done((bf16[24,4096]{1,0:T(8,128)(2,1)S(1)}, bf16[24,4096]{1,0:T(8,128)(2,1)S(1)}, u32[]{:S(2)}, u32[]{:S(2)}) %collective-permute-start.40) | collective-permute-done | bytes 196640 | tf_op jit(solution)/shard_map/ppermute | solution.py:22
  231.3 18.1 %all-to-all-start.2 = ((bf16[8,48,512]{2,1,0:T(8,128)(2,1)}), bf16[8,48,512]{2,1,0:T(8,128)(2,1)S(1)}, u32[]{:S(2)}, u32[]{:S(2)}) async-start(bf16[8,48,512]{2,1,0:T(8,128)(2,1)} %copy.55), calls=%async_computation.2 | async-start | bytes 786432 | tf_op jit(solution)/shard_map/all_to_all | solution.py:284
  249.5 8.1 %all-to-all-done.2 = bf16[8,48,512]{2,1,0:T(8,128)(2,1)S(1)} async-done(((bf16[8,48,512]{2,1,0:T(8,128)(2,1)}), bf16[8,48,512]{2,1,0:T(8,128)(2,1)S(1)}, u32[]{:S(2)}, u32[]{:S(2)}) %all-to-all-start.2) | async-done | bytes 393248 | tf_op jit(solution)/shard_map/all_to_all | solution.py:284
  (172 shorter events, 37.4 us)
Async XLA Ops:
  0.0 18.6 %copy-start.10 = (bf16[128,1024]{1,0:T(8,128)(2,1)S(1)}, bf16[128,1024]{1,0:T(8,128)(2,1)}, u32[]{:S(2)}) copy-start(bf16[128,1024]{1,0:T(8,128)(2,1)} %x_ref.1) | copy-start | bytes 786436
  0.0 18.6 %copy-start.12 = (bf16[128,1024]{1,0:T(8,128)(2,1)S(1)}, bf16[128,1024]{1,0:T(8,128)(2,1)}, u32[]{:S(2)}) copy-start(bf16[128,1024]{1,0:T(8,128)(2,1)} %dt_ref) | copy-start | bytes 786436
  1.1 22.5 %collective-permute-start.2 = (bf16[640,256]{1,0:T(8,128)(2,1)S(1)}, bf16[640,256]{1,0:T(8,128)(2,1)S(1)}, u32[]{:S(2)}, u32[]{:S(2)}) collective-permute-start(bf16[640,256]{1,0:T(8,128)(2,1)S(1)} %slice.152), channel_id=1, source_target_pairs={{0,32},{8,40},{16,48},{24,56},{32,64},{40,72},{48,80},{56,88},{64,... | collective-permute-start | bytes 983048 | tf_op jit(solution)/shard_map/ppermute | solution.py:22
  3.3 20.3 %collective-permute-start.3 = (bf16[640,256]{1,0:T(8,128)(2,1)S(1)}, bf16[640,256]{1,0:T(8,128)(2,1)S(1)}, u32[]{:S(2)}, u32[]{:S(2)}) collective-permute-start(bf16[640,256]{1,0:T(8,128)(2,1)S(1)} %slice.152), channel_id=1, source_target_pairs={{0,64},{8,72},{16,80},{24,88},{32,96},{40,104},{48,112},{56,120},{... | collective-permute-start | bytes 983048 | tf_op jit(solution)/shard_map/ppermute | solution.py:22
  5.9 17.7 %collective-permute-start.4 = (bf16[640,256]{1,0:T(8,128)(2,1)S(1)}, bf16[640,256]{1,0:T(8,128)(2,1)S(1)}, u32[]{:S(2)}, u32[]{:S(2)}) collective-permute-start(bf16[640,256]{1,0:T(8,128)(2,1)S(1)} %slice.152), channel_id=1, source_target_pairs={{0,96},{8,104},{16,112},{24,120},{32,0},{40,8},{48,16},{56,24},{64... | collective-permute-start | bytes 983048 | tf_op jit(solution)/shard_map/ppermute | solution.py:22
  7.9 6.8 %collective-permute-start.1 = (bf16[384,256]{1,0:T(8,128)(2,1)S(1)}, bf16[384,256]{1,0:T(8,128)(2,1)S(1)}, u32[]{:S(2)}, u32[]{:S(2)}) collective-permute-start(bf16[384,256]{1,0:T(8,128)(2,1)S(1)} %get-tuple-element.60), channel_id=1, source_target_pairs={{0,16},{8,24},{16,0},{24,8},{32,48},{40,56},{48,32},{56,40},{64,80... | collective-permute-start | bytes 589832 | tf_op jit(solution)/shard_map/ppermute | solution.py:22
  11.5 3.4 %collective-permute-start = (bf16[8,1024]{1,0:T(8,128)(2,1)S(1)}, bf16[8,1024]{1,0:T(8,128)(2,1)S(1)}, u32[]{:S(2)}, u32[]{:S(2)}) collective-permute-start(bf16[8,1024]{1,0:T(8,128)(2,1)S(1)} %slice.150), channel_id=1, source_target_pairs={{0,8},{8,16},{16,24},{24,32},{32,40},{40,48},{48,56},{56,64},{64,7... | collective-permute-start | bytes 49160 | tf_op jit(solution)/shard_map/ppermute | solution.py:142
  14.8 15.8 %collective-permute-start.10 = (bf16[2,384,256]{2,1,0:T(8,128)(2,1)S(1)}, bf16[2,384,256]{2,1,0:T(8,128)(2,1)S(1)}, u32[]{:S(2)}, u32[]{:S(2)}) collective-permute-start(bf16[2,384,256]{2,1,0:T(8,128)(2,1)S(1)} %pad_maximum_fusion.6.refs_0_), channel_id=1, source_target_pairs={{0,96},{8,104},{16,112},{24,120},{32,0},{40,8},{48,16},{56,24},{64... | collective-permute-start | bytes 1179656 | tf_op jit(solution)/shard_map/ppermute | solution.py:22
  14.9 16.4 %collective-permute-start.8 = (bf16[2,384,256]{2,1,0:T(8,128)(2,1)S(1)}, bf16[2,384,256]{2,1,0:T(8,128)(2,1)S(1)}, u32[]{:S(2)}, u32[]{:S(2)}) collective-permute-start(bf16[2,384,256]{2,1,0:T(8,128)(2,1)S(1)} %pad_maximum_fusion.6.refs_0_), channel_id=1, source_target_pairs={{0,32},{8,40},{16,48},{24,56},{32,64},{40,72},{48,80},{56,88},{64,... | collective-permute-start | bytes 1179656 | tf_op jit(solution)/shard_map/ppermute | solution.py:22
  23.6 3.5 %collective-permute-start.5 = (f32[17,8,128]{2,1,0:T(8,128)S(1)}, f32[17,8,128]{2,1,0:T(8,128)S(1)}, u32[]{:S(2)}, u32[]{:S(2)}) collective-permute-start(f32[17,8,128]{2,1,0:T(8,128)S(1)} %get-tuple-element.24), channel_id=1, source_target_pairs={{0,24},{8,0},{16,8},{24,16},{32,56},{40,32},{48,40},{56,48},{64,88... | collective-permute-start | bytes 208904 | tf_op jit(solution)/shard_map/ppermute | solution.py:22
  23.9 4.7 %collective-permute-start.6 = (f32[17,8,128]{2,1,0:T(8,128)S(1)}, f32[17,8,128]{2,1,0:T(8,128)S(1)}, u32[]{:S(2)}, u32[]{:S(2)}) collective-permute-start(f32[17,8,128]{2,1,0:T(8,128)S(1)} %get-tuple-element.24), channel_id=1, source_target_pairs={{0,16},{8,24},{16,0},{24,8},{32,48},{40,56},{48,32},{56,40},{64,80... | collective-permute-start | bytes 208904 | tf_op jit(solution)/shard_map/ppermute | solution.py:22
  24.1 5.7 %collective-permute-start.7 = (f32[17,8,128]{2,1,0:T(8,128)S(1)}, f32[17,8,128]{2,1,0:T(8,128)S(1)}, u32[]{:S(2)}, u32[]{:S(2)}) collective-permute-start(f32[17,8,128]{2,1,0:T(8,128)S(1)} %get-tuple-element.24), channel_id=1, source_target_pairs={{0,8},{8,16},{16,24},{24,0},{32,40},{40,48},{48,56},{56,32},{64,72... | collective-permute-start | bytes 208904 | tf_op jit(solution)/shard_map/ppermute | solution.py:22
  27.1 8.1 %collective-permute-start.9 = (bf16[2,384,256]{2,1,0:T(8,128)(2,1)S(1)}, bf16[2,384,256]{2,1,0:T(8,128)(2,1)S(1)}, u32[]{:S(2)}, u32[]{:S(2)}) collective-permute-start(bf16[2,384,256]{2,1,0:T(8,128)(2,1)S(1)} %pad_maximum_fusion.6.refs_0_), channel_id=1, source_target_pairs={{0,64},{8,72},{16,80},{24,88},{32,96},{40,104},{48,112},{56,120},{... | collective-permute-start | bytes 1179656 | tf_op jit(solution)/shard_map/ppermute | solution.py:22
  28.5 32.1 %collective-permute-start.15 = (bf16[4,640,256]{2,1,0:T(8,128)(2,1)S(1)}, bf16[4,640,256]{2,1,0:T(8,128)(2,1)S(1)}, u32[]{:S(2)}, u32[]{:S(2)}) collective-permute-start(bf16[4,640,256]{2,1,0:T(8,128)(2,1)S(1)} %pad_maximum_fusion.3.refs_4_), channel_id=1, source_target_pairs={{0,16},{8,24},{16,0},{24,8},{32,48},{40,56},{48,32},{56,40},{64,80... | collective-permute-start | bytes 3932168 | tf_op jit(solution)/shard_map/ppermute | solution.py:22
  36.0 5.2 %collective-permute-start.12 = (f32[17,8,128]{2,1,0:T(8,128)}, f32[17,8,128]{2,1,0:T(8,128)S(1)}, u32[]{:S(2)}, u32[]{:S(2)}) collective-permute-start(f32[17,8,128]{2,1,0:T(8,128)} %pad_maximum_fusion.7), channel_id=1, source_target_pairs={{0,64},{8,72},{16,80},{24,88},{32,96},{40,104},{48,112},{56,120},{... | collective-permute-start | bytes 208904 | tf_op jit(solution)/shard_map/ppermute | solution.py:22
  36.9 5.0 %collective-permute-start.11 = (f32[17,8,128]{2,1,0:T(8,128)}, f32[17,8,128]{2,1,0:T(8,128)S(1)}, u32[]{:S(2)}, u32[]{:S(2)}) collective-permute-start(f32[17,8,128]{2,1,0:T(8,128)} %pad_maximum_fusion.7), channel_id=1, source_target_pairs={{0,32},{8,40},{16,48},{24,56},{32,64},{40,72},{48,80},{56,88},{64,... | collective-permute-start | bytes 208904 | tf_op jit(solution)/shard_map/ppermute | solution.py:22
  38.0 3.9 %collective-permute-start.13 = (f32[17,8,128]{2,1,0:T(8,128)}, f32[17,8,128]{2,1,0:T(8,128)S(1)}, u32[]{:S(2)}, u32[]{:S(2)}) collective-permute-start(f32[17,8,128]{2,1,0:T(8,128)} %pad_maximum_fusion.7), channel_id=1, source_target_pairs={{0,96},{8,104},{16,112},{24,120},{32,0},{40,8},{48,16},{56,24},{64... | collective-permute-start | bytes 208904 | tf_op jit(solution)/shard_map/ppermute | solution.py:22
  51.2 9.5 %collective-permute-start.14 = (bf16[128,1024]{1,0:T(8,128)(2,1)S(1)}, bf16[128,1024]{1,0:T(8,128)(2,1)}, u32[]{:S(2)}, u32[]{:S(2)}) collective-permute-start(bf16[128,1024]{1,0:T(8,128)(2,1)S(1)} %scan_output.1.own_ref), channel_id=1, source_target_pairs={{0,8},{8,0},{16,24},{24,16},{32,40},{40,32},{48,56},{56,48},{64,72... | collective-permute-start | bytes 786440 | tf_op jit(solution)/shard_map/ppermute | solution.py:27
  67.2 29.5 %copy-start.21 = (s32[128,2]{0,1:T(2,128)S(1)}, s32[128,2]{0,1:T(2,128)}, u32[]{:S(2)}) copy-start(s32[128,2]{0,1:T(2,128)} %param.30) | copy-start | bytes 3076
  67.2 44.6 %all-to-all-start = ((bf16[8,2,128,256]{3,2,1,0:T(8,128)(2,1)}), bf16[8,2,128,256]{3,2,1,0:T(8,128)(2,1)S(1)}, u32[]{:S(2)}, u32[]{:S(2)}) async-start(bf16[8,2,128,256]{3,2,1,0:T(8,128)(2,1)} %project.1), calls=%async_computation | async-start | bytes 2097152 | tf_op jit(solution)/shard_map/all_to_all | solution.py:205
  111.9 3.2 %collective-permute-start.16 = (bf16[128,256]{1,0:T(8,128)(2,1)S(1)}, bf16[128,256]{1,0:T(8,128)(2,1)S(1)}, u32[]{:S(2)}, u32[]{:S(2)}) collective-permute-start(bf16[128,256]{1,0:T(8,128)(2,1)S(1)} %fusion.56), channel_id=1, source_target_pairs={{0,8},{8,0},{16,24},{24,16},{32,40},{40,32},{48,56},{56,48},{64,72... | collective-permute-start | bytes 196616 | tf_op jit(solution)/shard_map/ppermute | solution.py:27
  128.0 20.5 %slice-start = ((s8[6291456]{0:T(1024)(128)(4,1)}), s8[4194304]{0:T(1024)(128)(4,1)S(1)}, s32[]{:S(2)}) async-start(s8[6291456]{0:T(1024)(128)(4,1)} %bitcast.243), calls=%async_computation.3 | async-start | bytes 8388608
  128.8 11.5 %collective-permute-start.17 = (bf16[24,4096]{1,0:T(8,128)(2,1)S(1)}, bf16[24,4096]{1,0:T(8,128)(2,1)S(1)}, u32[]{:S(2)}, u32[]{:S(2)}) collective-permute-start(bf16[24,4096]{1,0:T(8,128)(2,1)S(1)} %get-tuple-element.64), channel_id=1, source_target_pairs={{0,8},{8,16},{16,24},{24,0},{32,40},{40,48},{48,56},{56,32},{64,72... | collective-permute-start | bytes 589832 | tf_op jit(solution)/shard_map/ppermute | solution.py:22
  128.9 11.9 %collective-permute-start.18 = (bf16[24,4096]{1,0:T(8,128)(2,1)S(1)}, bf16[24,4096]{1,0:T(8,128)(2,1)S(1)}, u32[]{:S(2)}, u32[]{:S(2)}) collective-permute-start(bf16[24,4096]{1,0:T(8,128)(2,1)S(1)} %get-tuple-element.64), channel_id=1, source_target_pairs={{0,16},{8,24},{16,0},{24,8},{32,48},{40,56},{48,32},{56,40},{64,80... | collective-permute-start | bytes 589832 | tf_op jit(solution)/shard_map/ppermute | solution.py:22
  129.2 11.6 %collective-permute-start.19 = (bf16[24,4096]{1,0:T(8,128)(2,1)S(1)}, bf16[24,4096]{1,0:T(8,128)(2,1)S(1)}, u32[]{:S(2)}, u32[]{:S(2)}) collective-permute-start(bf16[24,4096]{1,0:T(8,128)(2,1)S(1)} %get-tuple-element.64), channel_id=1, source_target_pairs={{0,24},{8,0},{16,8},{24,16},{32,56},{40,32},{48,40},{56,48},{64,88... | collective-permute-start | bytes 589832 | tf_op jit(solution)/shard_map/ppermute | solution.py:22
  131.6 12.2 %collective-permute-start.20 = (bf16[24,4096]{1,0:T(8,128)(2,1)S(1)}, bf16[24,4096]{1,0:T(8,128)(2,1)S(1)}, u32[]{:S(2)}, u32[]{:S(2)}) collective-permute-start(bf16[24,4096]{1,0:T(8,128)(2,1)S(1)} %get-tuple-element.63), channel_id=1, source_target_pairs={{0,32},{8,40},{16,48},{24,56},{32,64},{40,72},{48,80},{56,88},{64,... | collective-permute-start | bytes 589832 | tf_op jit(solution)/shard_map/ppermute | solution.py:22
  131.6 12.2 %collective-permute-start.21 = (bf16[24,4096]{1,0:T(8,128)(2,1)S(1)}, bf16[24,4096]{1,0:T(8,128)(2,1)S(1)}, u32[]{:S(2)}, u32[]{:S(2)}) collective-permute-start(bf16[24,4096]{1,0:T(8,128)(2,1)S(1)} %get-tuple-element.63), channel_id=1, source_target_pairs={{0,64},{8,72},{16,80},{24,88},{32,96},{40,104},{48,112},{56,120},{... | collective-permute-start | bytes 589832 | tf_op jit(solution)/shard_map/ppermute | solution.py:22
  140.3 5.1 %collective-permute-start.22 = (bf16[24,4096]{1,0:T(8,128)(2,1)S(1)}, bf16[24,4096]{1,0:T(8,128)(2,1)S(1)}, u32[]{:S(2)}, u32[]{:S(2)}) collective-permute-start(bf16[24,4096]{1,0:T(8,128)(2,1)S(1)} %get-tuple-element.63), channel_id=1, source_target_pairs={{0,96},{8,104},{16,112},{24,120},{32,0},{40,8},{48,16},{56,24},{64... | collective-permute-start | bytes 589832 | tf_op jit(solution)/shard_map/ppermute | solution.py:22
  141.0 18.7 %collective-permute-start.23 = (bf16[4,24,4096]{2,1,0:T(8,128)(2,1)S(1)}, bf16[4,24,4096]{2,1,0:T(8,128)(2,1)S(1)}, u32[]{:S(2)}, u32[]{:S(2)}) collective-permute-start(bf16[4,24,4096]{2,1,0:T(8,128)(2,1)S(1)} %get-tuple-element.56), channel_id=1, source_target_pairs={{0,32},{8,40},{16,48},{24,56},{32,64},{40,72},{48,80},{56,88},{64,... | collective-permute-start | bytes 2359304 | tf_op jit(solution)/shard_map/ppermute | solution.py:22
  142.0 20.7 %collective-permute-start.24 = (bf16[4,24,4096]{2,1,0:T(8,128)(2,1)S(1)}, bf16[4,24,4096]{2,1,0:T(8,128)(2,1)S(1)}, u32[]{:S(2)}, u32[]{:S(2)}) collective-permute-start(bf16[4,24,4096]{2,1,0:T(8,128)(2,1)S(1)} %get-tuple-element.56), channel_id=1, source_target_pairs={{0,96},{8,104},{16,112},{24,120},{32,0},{40,8},{48,16},{56,24},{64... | collective-permute-start | bytes 2359304 | tf_op jit(solution)/shard_map/ppermute | solution.py:22
  145.5 17.2 %collective-permute-start.25 = (bf16[4,24,4096]{2,1,0:T(8,128)(2,1)S(1)}, bf16[4,24,4096]{2,1,0:T(8,128)(2,1)S(1)}, u32[]{:S(2)}, u32[]{:S(2)}) collective-permute-start(bf16[4,24,4096]{2,1,0:T(8,128)(2,1)S(1)} %get-tuple-element.58), channel_id=1, source_target_pairs={{0,8},{8,16},{16,24},{24,0},{32,40},{40,48},{48,56},{56,32},{64,72... | collective-permute-start | bytes 2359304 | tf_op jit(solution)/shard_map/ppermute | solution.py:22
  145.6 17.1 %collective-permute-start.26 = (bf16[4,24,4096]{2,1,0:T(8,128)(2,1)S(1)}, bf16[4,24,4096]{2,1,0:T(8,128)(2,1)S(1)}, u32[]{:S(2)}, u32[]{:S(2)}) collective-permute-start(bf16[4,24,4096]{2,1,0:T(8,128)(2,1)S(1)} %get-tuple-element.58), channel_id=1, source_target_pairs={{0,24},{8,0},{16,8},{24,16},{32,56},{40,32},{48,40},{56,48},{64,88... | collective-permute-start | bytes 2359304 | tf_op jit(solution)/shard_map/ppermute | solution.py:22
  148.3 27.5 %collective-permute-start.29 = (bf16[4,24,4096]{2,1,0:T(8,128)(2,1)S(1)}, bf16[4,24,4096]{2,1,0:T(8,128)(2,1)S(1)}, u32[]{:S(2)}, u32[]{:S(2)}) collective-permute-start(bf16[4,24,4096]{2,1,0:T(8,128)(2,1)S(1)} %get-tuple-element.56), channel_id=1, source_target_pairs={{0,64},{8,72},{16,80},{24,88},{32,96},{40,104},{48,112},{56,120},{... | collective-permute-start | bytes 2359304 | tf_op jit(solution)/shard_map/ppermute | solution.py:22
  159.7 16.1 %collective-permute-start.30 = (bf16[4,24,4096]{2,1,0:T(8,128)(2,1)S(1)}, bf16[4,24,4096]{2,1,0:T(8,128)(2,1)S(1)}, u32[]{:S(2)}, u32[]{:S(2)}) collective-permute-start(bf16[4,24,4096]{2,1,0:T(8,128)(2,1)S(1)} %get-tuple-element.58), channel_id=1, source_target_pairs={{0,16},{8,24},{16,0},{24,8},{32,48},{40,56},{48,32},{56,40},{64,80... | collective-permute-start | bytes 2359304 | tf_op jit(solution)/shard_map/ppermute | solution.py:22
  171.6 17.9 %collective-permute-start.27 = (bf16[4,24,4096]{2,1,0:T(8,128)(2,1)S(1)}, bf16[4,24,4096]{2,1,0:T(8,128)(2,1)S(1)}, u32[]{:S(2)}, u32[]{:S(2)}) collective-permute-start(bf16[4,24,4096]{2,1,0:T(8,128)(2,1)S(1)} %get-tuple-element.41), channel_id=1, source_target_pairs={{0,96},{8,104},{16,112},{24,120},{32,0},{40,8},{48,16},{56,24},{64... | collective-permute-start | bytes 2359304 | tf_op jit(solution)/shard_map/ppermute | solution.py:22
  173.3 22.6 %collective-permute-start.28 = (bf16[4,24,4096]{2,1,0:T(8,128)(2,1)S(1)}, bf16[4,24,4096]{2,1,0:T(8,128)(2,1)S(1)}, u32[]{:S(2)}, u32[]{:S(2)}) collective-permute-start(bf16[4,24,4096]{2,1,0:T(8,128)(2,1)S(1)} %get-tuple-element.44), channel_id=1, source_target_pairs={{0,32},{8,40},{16,48},{24,56},{32,64},{40,72},{48,80},{56,88},{64,... | collective-permute-start | bytes 2359304 | tf_op jit(solution)/shard_map/ppermute | solution.py:22
  180.4 15.5 %collective-permute-start.31 = (bf16[4,24,4096]{2,1,0:T(8,128)(2,1)S(1)}, bf16[4,24,4096]{2,1,0:T(8,128)(2,1)S(1)}, u32[]{:S(2)}, u32[]{:S(2)}) collective-permute-start(bf16[4,24,4096]{2,1,0:T(8,128)(2,1)S(1)} %bitcast.231), channel_id=1, source_target_pairs={{0,64},{8,72},{16,80},{24,88},{32,96},{40,104},{48,112},{56,120},{... | collective-permute-start | bytes 2359304 | tf_op jit(solution)/shard_map/ppermute | solution.py:22
  185.5 14.4 %collective-permute-start.35 = (bf16[4,24,4096]{2,1,0:T(8,128)(2,1)S(1)}, bf16[4,24,4096]{2,1,0:T(8,128)(2,1)S(1)}, u32[]{:S(2)}, u32[]{:S(2)}) collective-permute-start(bf16[4,24,4096]{2,1,0:T(8,128)(2,1)S(1)} %get-tuple-element.43), channel_id=1, source_target_pairs={{0,24},{8,0},{16,8},{24,16},{32,56},{40,32},{48,40},{56,48},{64,88... | collective-permute-start | bytes 2359304 | tf_op jit(solution)/shard_map/ppermute | solution.py:22
  187.3 19.3 %collective-permute-start.36 = (bf16[4,24,4096]{2,1,0:T(8,128)(2,1)S(1)}, bf16[4,24,4096]{2,1,0:T(8,128)(2,1)S(1)}, u32[]{:S(2)}, u32[]{:S(2)}) collective-permute-start(bf16[4,24,4096]{2,1,0:T(8,128)(2,1)S(1)} %get-tuple-element.42), channel_id=1, source_target_pairs={{0,8},{8,16},{16,24},{24,0},{32,40},{40,48},{48,56},{56,32},{64,72... | collective-permute-start | bytes 2359304 | tf_op jit(solution)/shard_map/ppermute | solution.py:22
  189.4 20.7 %collective-permute-start.37 = (bf16[4,24,4096]{2,1,0:T(8,128)(2,1)S(1)}, bf16[4,24,4096]{2,1,0:T(8,128)(2,1)S(1)}, u32[]{:S(2)}, u32[]{:S(2)}) collective-permute-start(bf16[4,24,4096]{2,1,0:T(8,128)(2,1)S(1)} %bitcast.228), channel_id=1, source_target_pairs={{0,16},{8,24},{16,0},{24,8},{32,48},{40,56},{48,32},{56,40},{64,80... | collective-permute-start | bytes 2359304 | tf_op jit(solution)/shard_map/ppermute | solution.py:22
  196.4 25.3 %collective-permute-start.32 = (bf16[24,4096]{1,0:T(8,128)(2,1)S(1)}, bf16[24,4096]{1,0:T(8,128)(2,1)S(1)}, u32[]{:S(2)}, u32[]{:S(2)}) collective-permute-start(bf16[24,4096]{1,0:T(8,128)(2,1)S(1)} %get-tuple-element.49), channel_id=1, source_target_pairs={{0,24},{8,0},{16,8},{24,16},{32,56},{40,32},{48,40},{56,48},{64,88... | collective-permute-start | bytes 589832 | tf_op jit(solution)/shard_map/ppermute | solution.py:22
  199.2 27.9 %collective-permute-start.33 = (bf16[24,4096]{1,0:T(8,128)(2,1)S(1)}, bf16[24,4096]{1,0:T(8,128)(2,1)S(1)}, u32[]{:S(2)}, u32[]{:S(2)}) collective-permute-start(bf16[24,4096]{1,0:T(8,128)(2,1)S(1)} %get-tuple-element.51), channel_id=1, source_target_pairs={{0,8},{8,16},{16,24},{24,0},{32,40},{40,48},{48,56},{56,32},{64,72... | collective-permute-start | bytes 589832 | tf_op jit(solution)/shard_map/ppermute | solution.py:22
  199.9 27.2 %collective-permute-start.34 = (bf16[24,4096]{1,0:T(8,128)(2,1)S(1)}, bf16[24,4096]{1,0:T(8,128)(2,1)S(1)}, u32[]{:S(2)}, u32[]{:S(2)}) collective-permute-start(bf16[24,4096]{1,0:T(8,128)(2,1)S(1)} %get-tuple-element.50), channel_id=1, source_target_pairs={{0,16},{8,24},{16,0},{24,8},{32,48},{40,56},{48,32},{56,40},{64,80... | collective-permute-start | bytes 589832 | tf_op jit(solution)/shard_map/ppermute | solution.py:22
  210.7 16.7 %collective-permute-start.38 = (bf16[24,4096]{1,0:T(8,128)(2,1)S(1)}, bf16[24,4096]{1,0:T(8,128)(2,1)S(1)}, u32[]{:S(2)}, u32[]{:S(2)}) collective-permute-start(bf16[24,4096]{1,0:T(8,128)(2,1)S(1)} %get-tuple-element.52), channel_id=1, source_target_pairs={{0,96},{8,104},{16,112},{24,120},{32,0},{40,8},{48,16},{56,24},{64... | collective-permute-start | bytes 589832 | tf_op jit(solution)/shard_map/ppermute | solution.py:22
  211.4 15.9 %collective-permute-start.39 = (bf16[24,4096]{1,0:T(8,128)(2,1)S(1)}, bf16[24,4096]{1,0:T(8,128)(2,1)S(1)}, u32[]{:S(2)}, u32[]{:S(2)}) collective-permute-start(bf16[24,4096]{1,0:T(8,128)(2,1)S(1)} %get-tuple-element.54), channel_id=1, source_target_pairs={{0,32},{8,40},{16,48},{24,56},{32,64},{40,72},{48,80},{56,88},{64,... | collective-permute-start | bytes 589832 | tf_op jit(solution)/shard_map/ppermute | solution.py:22
  221.7 8.5 %collective-permute-start.40 = (bf16[24,4096]{1,0:T(8,128)(2,1)S(1)}, bf16[24,4096]{1,0:T(8,128)(2,1)S(1)}, u32[]{:S(2)}, u32[]{:S(2)}) collective-permute-start(bf16[24,4096]{1,0:T(8,128)(2,1)S(1)} %get-tuple-element.53), channel_id=1, source_target_pairs={{0,64},{8,72},{16,80},{24,88},{32,96},{40,104},{48,112},{56,120},{... | collective-permute-start | bytes 589832 | tf_op jit(solution)/shard_map/ppermute | solution.py:22
  230.3 19.1 %copy-start.22 = (f32[128,2]{0,1:T(2,128)S(1)}, f32[128,2]{0,1:T(2,128)}, u32[]{:S(2)}) copy-start(f32[128,2]{0,1:T(2,128)} %param.31) | copy-start | bytes 3076
  231.3 26.2 %all-to-all-start.2 = ((bf16[8,48,512]{2,1,0:T(8,128)(2,1)}), bf16[8,48,512]{2,1,0:T(8,128)(2,1)S(1)}, u32[]{:S(2)}, u32[]{:S(2)}) async-start(bf16[8,48,512]{2,1,0:T(8,128)(2,1)} %copy.55), calls=%async_computation.2 | async-start | bytes 786432 | tf_op jit(solution)/shard_map/all_to_all | solution.py:284
  (24 other events, 159.0 us)

commit v4 on v3

--- a/solution.py
+++ b/solution.py
@@ -102,7 +102,7 @@
         out_ref[:, cols] = (y_ref[:, k, :] * (gate * jax.nn.sigmoid(gate))).astype(BF16)
 
 
-def entering_state(final, rate, ahead):
+def entering_state(final, rate, ahead, after):
     along_x = lax.axis_index("seq") % SIDE
     along_y = lax.axis_index("seq") // SIDE
 
@@ -129,9 +129,11 @@
     for d in (3, 2, 1):
         total = chain(total, masked(others[d - 1], along_x < d))
     packed = jnp.concatenate([total[0], total[1][None]], 0)
+    packed, after = lax.optimization_barrier((packed, after))
+    far = shift(after, "x", 2)
     packed, ahead = lax.optimization_barrier((packed, ahead))
     before_y, _ = spread(packed, "y", along_y)
-    return chain(before_y, before_x)[0], ahead
+    return chain(before_y, before_x)[0], ahead, [after, far]
 
 
 def mixer(
@@ -140,7 +142,7 @@
     tokens, channels = mixer_in.shape
     count, index = lax.axis_size("seq"), lax.axis_index("seq")
     rim = lax.ppermute(mixer_in[tokens - 8 :], "seq", [(i, i + 1) for i in range(count - 1)])
-    split = 3 * channels // 8
+    split = 7 * channels // 16
     low, high = w_out[:split], w_out[split:]
     low_pair = jnp.stack([low, shift(low, "x", 2)])
     dt_raw, low_pair = lax.optimization_barrier((dt_raw, low_pair))
@@ -161,8 +163,7 @@
     final, high_ring = lax.optimization_barrier((final, high_ring))
     first = ring_gather(low_pair, "y")
     high_ring = jnp.stack(high_ring)
-    second = [high_ring, shift(high_ring, "x", 2)]
-    enter, first = entering_state(final, rate, first)
+    enter, first, second = entering_state(final, rate, first, high_ring)
     mixed = pl.pallas_call(
         second_pass,
         out_shape=jax.ShapeDtypeStruct((tokens, channels), BF16),
@@ -176,16 +177,20 @@
 
 
 def project_kernel(place_ref, own_ref, other_ref, *refs):
-    first, second, out_ref = refs[:SIDE], refs[SIDE : SIDE + 2], refs[SIDE + 2]
+    first, second, out_ref, rows = refs[:SIDE], refs[SIDE : SIDE + 2], refs[SIDE + 2], refs[SIDE + 3]
+    tokens = own_ref.shape[0]
+    rows[:tokens] = own_ref[...]
+    rows[tokens:] = other_ref[...]
     split = first[0].shape[1]
     y, side = place_ref[0], place_ref[1]
     for i in range(SIDE):
         for j in range(2):
             owner = lax.rem(y - i + SIDE, SIDE) * 2 + lax.rem(side + j, 2)
-            for k, rows in enumerate((own_ref, other_ref)):
-                total = jnp.dot(rows[:, :split], first[i][j], preferred_element_type=F32)
-                total += jnp.dot(rows[:, split:], second[j][i], preferred_element_type=F32)
-                out_ref[owner, k] = total.astype(BF16)
+            total = jnp.dot(rows[:, :split], first[i][j], preferred_element_type=F32)
+            total += jnp.dot(rows[:, split:], second[j][i], preferred_element_type=F32)
+            total = total.astype(BF16)
+            out_ref[owner, 0] = total[:tokens]
+            out_ref[owner, 1] = total[tokens:]
 
 
 def project(mixed, weights):
@@ -199,6 +204,7 @@
         out_shape=jax.ShapeDtypeStruct((2 * SIDE, 2, tokens, columns), BF16),
         in_specs=[pl.BlockSpec(memory_space=pltpu.SMEM)] + [vmem] * (SIDE + 4),
         out_specs=vmem,
+        scratch_shapes=[pltpu.VMEM((2 * tokens, mixed.shape[1]), BF16)],
         compiler_params=pltpu.CompilerParams(vmem_limit_bytes=40 << 20),
         name="project",
     )(place, mixed, partner(mixed), *first, *second)

time: 260 us -> 244 us (0.938)
  starting transfers between devices: 116 us -> 102 us
    all_to_all x1, starting transfers between devices: 29.5 us -> 9.76 us  [project(): partial = lax.all_to_all(partial, 'exp', split_axis=0, concat_axis=0)]
    ppermute x38, starting transfers between devices: 65 us -> 69.6 us  [shift(): return lax.ppermute(value, 'seq', route)]
    ppermute x2, waiting for transfers between devices: 10.9 us -> 7.63 us  [partner(): return lax.ppermute(value, 'seq', [(i, i ^ 1) for i in cells])]
  transfers between devices with their start and end apart: 43 -> 43, of which waited for: 18 -> 23; matrix products, arithmetic and copies ran while one was open for 10% -> 11% of each run, Pallas kernels for 4% -> 5%
where the time goes in v4:
time: 244 us
  starting transfers between devices  102 us (42%)
  waiting for transfers between devices  74.2 us (30%)
  matrix products  18.2 us (7%)
  local copies, waits for them, and re-layouts  15.1 us (6%)
  Pallas kernels  14.3 us (6%)
  blocking collectives  12.5 us (5%)
  other arithmetic  7.04 us (3%)
    ppermute x38, starting transfers between devices, shift(): return lax.ppermute(value, 'seq', route)  69.6 us
    ppermute x38, waiting for transfers between devices, shift(): return lax.ppermute(value, 'seq', route)  44.9 us
    all_to_all x1, starting transfers between devices, local(): returned = lax.all_to_all(summed, 'exp', split_axis=0, concat_axis=0)  19.4 us
    all_to_all x1, waiting for transfers between devices, project(): partial = lax.all_to_all(partial, 'exp', split_axis=0, concat_axis=0)  13.5 us
    all_to_all x1, blocking collectives, local(): lax.all_to_all(outgoing, 'exp', split_axis=0, concat_axis=2, tiled=True)[0]  12.5 us
    unnamed x65, local copies, waits for them, and re-layouts  10.2 us
    all_to_all x1, starting transfers between devices, project(): partial = lax.all_to_all(partial, 'exp', split_axis=0, concat_axis=0)  9.76 us
    all_to_all x1, waiting for transfers between devices, local(): returned = lax.all_to_all(summed, 'exp', split_axis=0, concat_axis=0)  8.09 us
  transfers between devices with their start and end apart: 43, of which 23 were waited for; matrix products, arithmetic and copies ran while one was open for 11% of the time, Pallas kernels for 5%

profile of v4, /device:TPU:1, one launch (start us, length us, event | category | flops | bytes accessed | tf_op | source)
XLA Modules:
  0.0 243.6 jit_solution(331855872792386960)
XLA Ops:
  1.1 3.7 %collective-permute-start.1 = (bf16[448,256]{1,0:T(8,128)(2,1)S(1)}, bf16[448,256]{1,0:T(8,128)(2,1)S(1)}, u32[]{:S(2)}, u32[]{:S(2)}) collective-permute-start(bf16[448,256]{1,0:T(8,128)(2,1)S(1)} %get-tuple-element.64), channel_id=1, source_target_pairs={{0,16},{8,24},{16,0},{24,8},{32,48},{40,56},{48,32},{56,40},{64,80... | collective-permute-start | bytes 688136 | tf_op jit(solution)/shard_map/ppermute | solution.py:22
  7.1 2.6 %collective-permute-start.3 = (bf16[576,256]{1,0:T(8,128)(2,1)S(1)}, bf16[576,256]{1,0:T(8,128)(2,1)S(1)}, u32[]{:S(2)}, u32[]{:S(2)}) collective-permute-start(bf16[576,256]{1,0:T(8,128)(2,1)S(1)} %slice.152), channel_id=1, source_target_pairs={{0,64},{8,72},{16,80},{24,88},{32,96},{40,104},{48,112},{56,120},{... | collective-permute-start | bytes 884744 | tf_op jit(solution)/shard_map/ppermute | solution.py:22
  11.5 2.2 collective-permute-start
  14.9 3.7 %collective-permute-start.8 = (bf16[2,448,256]{2,1,0:T(8,128)(2,1)S(1)}, bf16[2,448,256]{2,1,0:T(8,128)(2,1)S(1)}, u32[]{:S(2)}, u32[]{:S(2)}) collective-permute-start(bf16[2,448,256]{2,1,0:T(8,128)(2,1)S(1)} %pad_maximum_fusion.6.refs_0_), channel_id=1, source_target_pairs={{0,32},{8,40},{16,48},{24,56},{32,64},{40,72},{48,80},{56,88},{64,... | collective-permute-start | bytes 1376264 | tf_op jit(solution)/shard_map/ppermute | solution.py:22
  18.6 4.9 %scan_state.1 = (f32[128,8,128]{2,1,0:T(8,128)S(1)}, f32[128,8,128]{2,1,0:T(8,128)S(1)}, f32[17,8,128]{2,1,0:T(8,128)S(1)}) custom-call(bf16[128,1024]{1,0:T(8,128)(2,1)S(1)} %copy-done.10, bf16[8,1024]{1,0:T(8,128)(2,1)S(1)} %collective-permute-done.rim_ref, bf16[128,1024]{1,0:T(8,128)(2,1)S(1)} %copy-done.12, f32[1,1024]{1,0:T(1,128)S(1)} %bitcast.203, ...), custom_call_target="tpu_custom_call" | custom-call | tf_op jit(solution)/shard_map/scan_state/pallas_call | solution.py:154
  25.3 1.8 collective-permute-done.5
  31.1 1.7 collective-permute-done.10.refs_3_
  35.2 6.2 %collective-permute-done.9.refs_2_ = bf16[2,448,256]{2,1,0:T(8,128)(2,1)S(1)} collective-permute-done((bf16[2,448,256]{2,1,0:T(8,128)(2,1)S(1)}, bf16[2,448,256]{2,1,0:T(8,128)(2,1)S(1)}, u32[]{:S(2)}, u32[]{:S(2)}) %collective-permute-start.9) | collective-permute-done | bytes 458784 | tf_op jit(solution)/shard_map/ppermute | solution.py:22
  42.3 2.8 %collective-permute-start.11 = (f32[17,8,128]{2,1,0:T(8,128)}, f32[17,8,128]{2,1,0:T(8,128)S(1)}, u32[]{:S(2)}, u32[]{:S(2)}) collective-permute-start(f32[17,8,128]{2,1,0:T(8,128)} %pad_maximum_fusion.7), channel_id=1, source_target_pairs={{0,32},{8,40},{16,48},{24,56},{32,64},{40,72},{48,80},{56,88},{64,... | collective-permute-start | bytes 208904 | tf_op jit(solution)/shard_map/ppermute | solution.py:22
  45.1 1.6 collective-permute-start.13
  52.0 6.1 %scan_output.1.own_ref = bf16[128,1024]{1,0:T(8,128)(2,1)S(1)} custom-call(f32[128,8,128]{2,1,0:T(8,128)S(1)} %copy-done.1, f32[128,8,128]{2,1,0:T(8,128)S(1)} %copy-done.3, bf16[128,1024]{1,0:T(8,128)(2,1)S(1)} %copy-done.11, f32[16,8,128]{2,1,0:T(8,128)S(1)} %fusion.59.enter_ref, f32[16,8,128]{2,1,0:T(8,128)S(1)} %bitcast.201, f32[8,128]{1,0:T(8,128)S(1)} %bitcast.205, ...), custom_call_target="tpu_custom_call" | custom-call | tf_op jit(solution)/shard_map/scan_output/pallas_call | solution.py:167
  58.6 4.8 %collective-permute-done.14.other_ref = bf16[128,1024]{1,0:T(8,128)(2,1)S(1)} collective-permute-done((bf16[128,1024]{1,0:T(8,128)(2,1)S(1)}, bf16[128,1024]{1,0:T(8,128)(2,1)S(1)}, u32[]{:S(2)}, u32[]{:S(2)}) %collective-permute-start.14) | collective-permute-done | bytes 262176 | tf_op jit(solution)/shard_map/ppermute | solution.py:27
  66.5 3.2 %project.1 = bf16[8,2,128,256]{3,2,1,0:T(8,128)(2,1)} custom-call(s32[2]{0:T(128)S(1)} %pad_add_fusion.place_ref, bf16[128,1024]{1,0:T(8,128)(2,1)S(1)} %scan_output.1.own_ref, bf16[128,1024]{1,0:T(8,128)(2,1)S(1)} %collective-permute-done.14.other_ref, bf16[2,448,256]{2,1,0:T(8,128)(2,1)S(1)} %pad_maximum_fusion.6.refs_0_, ...), custom_call_target="tpu_custom_call" | custom-call | tf_op jit(solution)/shard_map/project/pallas_call | solution.py:202
  69.7 9.8 %all-to-all-start = ((bf16[8,2,128,256]{3,2,1,0:T(8,128)(2,1)}), bf16[8,2,128,256]{3,2,1,0:T(8,128)(2,1)S(1)}, u32[]{:S(2)}, u32[]{:S(2)}) async-start(bf16[8,2,128,256]{3,2,1,0:T(8,128)(2,1)} %project.1), calls=%async_computation | async-start | bytes 2097152 | tf_op jit(solution)/shard_map/all_to_all | solution.py:211
  81.1 13.5 %all-to-all-done = bf16[8,2,128,256]{3,2,1,0:T(8,128)(2,1)S(1)} async-done(((bf16[8,2,128,256]{3,2,1,0:T(8,128)(2,1)}), bf16[8,2,128,256]{3,2,1,0:T(8,128)(2,1)S(1)}, u32[]{:S(2)}, u32[]{:S(2)}) %all-to-all-start) | async-done | bytes 1048608 | tf_op jit(solution)/shard_map/all_to_all | solution.py:211
  95.2 2.8 %collective-permute-done.16 = bf16[128,256]{1,0:T(8,128)(2,1)S(1)} collective-permute-done((bf16[128,256]{1,0:T(8,128)(2,1)S(1)}, bf16[128,256]{1,0:T(8,128)(2,1)S(1)}, u32[]{:S(2)}, u32[]{:S(2)}) %collective-permute-start.16) | collective-permute-done | bytes 65568 | tf_op jit(solution)/shard_map/ppermute | solution.py:27
  98.3 12.5 %all_to_all.19 = bf16[8,48,512]{2,1,0:T(8,128)(2,1)S(1)} all-to-all(bf16[8,48,512]{2,1,0:T(8,128)(2,1)S(1)} %bitcast.218), channel_id=1, replica_groups=mesh['seq'=16,'exp'=8] {'exp'}, dimensions={0} | all-to-all | bytes 786432 | tf_op jit(solution)/shard_map/all_to_all | solution.py:262
  112.1 1.7 collective-permute-start.18
  115.3 3.0 %collective-permute-start.21 = (bf16[24,4096]{1,0:T(8,128)(2,1)S(1)}, bf16[24,4096]{1,0:T(8,128)(2,1)S(1)}, u32[]{:S(2)}, u32[]{:S(2)}) collective-permute-start(bf16[24,4096]{1,0:T(8,128)(2,1)S(1)} %get-tuple-element.67), channel_id=1, source_target_pairs={{0,64},{8,72},{16,80},{24,88},{32,96},{40,104},{48,112},{56,120},{... | collective-permute-start | bytes 589832 | tf_op jit(solution)/shard_map/ppermute | solution.py:22
  119.1 2.6 %collective-permute-start.22 = (bf16[24,4096]{1,0:T(8,128)(2,1)S(1)}, bf16[24,4096]{1,0:T(8,128)(2,1)S(1)}, u32[]{:S(2)}, u32[]{:S(2)}) collective-permute-start(bf16[24,4096]{1,0:T(8,128)(2,1)S(1)} %get-tuple-element.67), channel_id=1, source_target_pairs={{0,96},{8,104},{16,112},{24,120},{32,0},{40,8},{48,16},{56,24},{64... | collective-permute-start | bytes 589832 | tf_op jit(solution)/shard_map/ppermute | solution.py:22
  124.2 1.9 collective-permute-start.24
  126.2 1.5 collective-permute-start.25
  127.7 2.1 collective-permute-start.26
  129.8 1.6 collective-permute-start.29
  131.6 1.4 fusion.16
  134.3 1.4 fusion.34
  137.7 3.2 %collective-permute-done.23 = bf16[4,24,4096]{2,1,0:T(8,128)(2,1)S(1)} collective-permute-done((bf16[4,24,4096]{2,1,0:T(8,128)(2,1)S(1)}, bf16[4,24,4096]{2,1,0:T(8,128)(2,1)S(1)}, u32[]{:S(2)}, u32[]{:S(2)}) %collective-permute-start.23) | collective-permute-done | bytes 786464 | tf_op jit(solution)/shard_map/ppermute | solution.py:22
  140.8 6.6 %collective-permute-start.30 = (bf16[4,24,4096]{2,1,0:T(8,128)(2,1)S(1)}, bf16[4,24,4096]{2,1,0:T(8,128)(2,1)S(1)}, u32[]{:S(2)}, u32[]{:S(2)}) collective-permute-start(bf16[4,24,4096]{2,1,0:T(8,128)(2,1)S(1)} %get-tuple-element.62), channel_id=1, source_target_pairs={{0,16},{8,24},{16,0},{24,8},{32,48},{40,56},{48,32},{56,40},{64,80... | collective-permute-start | bytes 2359304 | tf_op jit(solution)/shard_map/ppermute | solution.py:22
  147.8 2.6 %fusion.14 = f32[384,768]{1,0:T(8,128)S(1)} fusion(bf16[384,4096]{1,0:T(8,128)(2,1)S(1)} %bitcast.208, bf16[1,4096,768]{2,1,0:T(8,128)(2,1)S(1)} %bitcast.244), kind=kOutput, calls=%fused_computation.14 | convolution fusion | flops 2415919104 | bytes 10616832 | tf_op jit(solution)/shard_map/dot_general | solution.py:273
  150.5 2.7 %multiply_convert_fusion = bf16[384,768]{1,0:T(8,128)(2,1)S(1)} fusion(f32[384,768]{1,0:T(8,128)S(1)} %fusion.14, bf16[384,4096]{1,0:T(8,128)(2,1)S(1)} %bitcast.209, bf16[1,4096,768]{2,1,0:T(8,128)(2,1)S(1)} %bitcast.246), kind=kOutput, calls=%fused_computation.35 | convolution fusion | flops 2417688576 | bytes 11206656 | tf_op jit(solution)/shard_map/dot_general | solution.py:274
  153.2 2.8 %fusion.18 = bf16[384,4096]{1,0:T(8,128)(2,1)S(1)} fusion(bf16[384,768]{1,0:T(8,128)(2,1)S(1)} %multiply_convert_fusion, bf16[1,768,4096]{2,1,0:T(8,128)(2,1)S(1)} %bitcast.248), kind=kOutput, calls=%fused_computation.18 | convolution fusion | flops 2417491968 | bytes 10027008 | tf_op jit(solution)/shard_map/dot_general | solution.py:276
  156.3 1.5 collective-permute-start.28
  157.7 1.8 collective-permute-done.29
  159.6 3.2 %collective-permute-done.30 = bf16[4,24,4096]{2,1,0:T(8,128)(2,1)S(1)} collective-permute-done((bf16[4,24,4096]{2,1,0:T(8,128)(2,1)S(1)}, bf16[4,24,4096]{2,1,0:T(8,128)(2,1)S(1)}, u32[]{:S(2)}, u32[]{:S(2)}) %collective-permute-start.30) | collective-permute-done | bytes 786464 | tf_op jit(solution)/shard_map/ppermute | solution.py:22
  162.9 1.4 fusion.12
  164.4 1.4 multiply_convert_fusion.2
  165.8 1.4 fusion.24
  167.6 2.7 %collective-permute-start.35 = (bf16[4,24,4096]{2,1,0:T(8,128)(2,1)S(1)}, bf16[4,24,4096]{2,1,0:T(8,128)(2,1)S(1)}, u32[]{:S(2)}, u32[]{:S(2)}) collective-permute-start(bf16[4,24,4096]{2,1,0:T(8,128)(2,1)S(1)} %get-tuple-element.47), channel_id=1, source_target_pairs={{0,24},{8,0},{16,8},{24,16},{32,56},{40,32},{48,40},{56,48},{64,88... | collective-permute-start | bytes 2359304 | tf_op jit(solution)/shard_map/ppermute | solution.py:22
  170.6 2.1 collective-permute-done.27
  172.7 13.6 %collective-permute-start.37 = (bf16[4,24,4096]{2,1,0:T(8,128)(2,1)S(1)}, bf16[4,24,4096]{2,1,0:T(8,128)(2,1)S(1)}, u32[]{:S(2)}, u32[]{:S(2)}) collective-permute-start(bf16[4,24,4096]{2,1,0:T(8,128)(2,1)S(1)} %bitcast.228), channel_id=1, source_target_pairs={{0,16},{8,24},{16,0},{24,8},{32,48},{40,56},{48,32},{56,40},{64,80... | collective-permute-start | bytes 2359304 | tf_op jit(solution)/shard_map/ppermute | solution.py:22
  186.9 1.5 collective-permute-start.33
  188.4 2.0 collective-permute-start.34
  190.4 11.9 %collective-permute-done.37 = bf16[4,24,4096]{2,1,0:T(8,128)(2,1)S(1)} collective-permute-done((bf16[4,24,4096]{2,1,0:T(8,128)(2,1)S(1)}, bf16[4,24,4096]{2,1,0:T(8,128)(2,1)S(1)}, u32[]{:S(2)}, u32[]{:S(2)}) %collective-permute-start.37) | collective-permute-done | bytes 786464 | tf_op jit(solution)/shard_map/ppermute | solution.py:22
  202.9 2.8 %collective-permute-start.38 = (bf16[24,4096]{1,0:T(8,128)(2,1)S(1)}, bf16[24,4096]{1,0:T(8,128)(2,1)S(1)}, u32[]{:S(2)}, u32[]{:S(2)}) collective-permute-start(bf16[24,4096]{1,0:T(8,128)(2,1)S(1)} %get-tuple-element.56), channel_id=1, source_target_pairs={{0,96},{8,104},{16,112},{24,120},{32,0},{40,8},{48,16},{56,24},{64... | collective-permute-start | bytes 589832 | tf_op jit(solution)/shard_map/ppermute | solution.py:22
  207.0 3.9 %collective-permute-done.34 = bf16[24,4096]{1,0:T(8,128)(2,1)S(1)} collective-permute-done((bf16[24,4096]{1,0:T(8,128)(2,1)S(1)}, bf16[24,4096]{1,0:T(8,128)(2,1)S(1)}, u32[]{:S(2)}, u32[]{:S(2)}) %collective-permute-start.34) | collective-permute-done | bytes 196640 | tf_op jit(solution)/shard_map/ppermute | solution.py:22
  211.0 2.8 %collective-permute-done.39 = bf16[24,4096]{1,0:T(8,128)(2,1)S(1)} collective-permute-done((bf16[24,4096]{1,0:T(8,128)(2,1)S(1)}, bf16[24,4096]{1,0:T(8,128)(2,1)S(1)}, u32[]{:S(2)}, u32[]{:S(2)}) %collective-permute-start.39) | collective-permute-done | bytes 196640 | tf_op jit(solution)/shard_map/ppermute | solution.py:22
  214.9 19.4 %all-to-all-start.2 = ((bf16[8,48,512]{2,1,0:T(8,128)(2,1)}), bf16[8,48,512]{2,1,0:T(8,128)(2,1)S(1)}, u32[]{:S(2)}, u32[]{:S(2)}) async-start(bf16[8,48,512]{2,1,0:T(8,128)(2,1)} %copy.55), calls=%async_computation.2 | async-start | bytes 786432 | tf_op jit(solution)/shard_map/all_to_all | solution.py:290
  234.3 8.1 %all-to-all-done.2 = bf16[8,48,512]{2,1,0:T(8,128)(2,1)S(1)} async-done(((bf16[8,48,512]{2,1,0:T(8,128)(2,1)}), bf16[8,48,512]{2,1,0:T(8,128)(2,1)S(1)}, u32[]{:S(2)}, u32[]{:S(2)}) %all-to-all-start.2) | async-done | bytes 393248 | tf_op jit(solution)/shard_map/all_to_all | solution.py:290
  (172 shorter events, 42.5 us)
Async XLA Ops:
  1.1 13.6 %collective-permute-start.1 = (bf16[448,256]{1,0:T(8,128)(2,1)S(1)}, bf16[448,256]{1,0:T(8,128)(2,1)S(1)}, u32[]{:S(2)}, u32[]{:S(2)}) collective-permute-start(bf16[448,256]{1,0:T(8,128)(2,1)S(1)} %get-tuple-element.64), channel_id=1, source_target_pairs={{0,16},{8,24},{16,0},{24,8},{32,48},{40,56},{48,32},{56,40},{64,80... | collective-permute-start | bytes 688136 | tf_op jit(solution)/shard_map/ppermute | solution.py:22
  5.7 17.9 %collective-permute-start.2 = (bf16[576,256]{1,0:T(8,128)(2,1)S(1)}, bf16[576,256]{1,0:T(8,128)(2,1)S(1)}, u32[]{:S(2)}, u32[]{:S(2)}) collective-permute-start(bf16[576,256]{1,0:T(8,128)(2,1)S(1)} %slice.152), channel_id=1, source_target_pairs={{0,32},{8,40},{16,48},{24,56},{32,64},{40,72},{48,80},{56,88},{64,... | collective-permute-start | bytes 884744 | tf_op jit(solution)/shard_map/ppermute | solution.py:22
  7.1 16.5 %collective-permute-start.3 = (bf16[576,256]{1,0:T(8,128)(2,1)S(1)}, bf16[576,256]{1,0:T(8,128)(2,1)S(1)}, u32[]{:S(2)}, u32[]{:S(2)}) collective-permute-start(bf16[576,256]{1,0:T(8,128)(2,1)S(1)} %slice.152), channel_id=1, source_target_pairs={{0,64},{8,72},{16,80},{24,88},{32,96},{40,104},{48,112},{56,120},{... | collective-permute-start | bytes 884744 | tf_op jit(solution)/shard_map/ppermute | solution.py:22
  9.7 13.9 %collective-permute-start.4 = (bf16[576,256]{1,0:T(8,128)(2,1)S(1)}, bf16[576,256]{1,0:T(8,128)(2,1)S(1)}, u32[]{:S(2)}, u32[]{:S(2)}) collective-permute-start(bf16[576,256]{1,0:T(8,128)(2,1)S(1)} %slice.152), channel_id=1, source_target_pairs={{0,96},{8,104},{16,112},{24,120},{32,0},{40,8},{48,16},{56,24},{64... | collective-permute-start | bytes 884744 | tf_op jit(solution)/shard_map/ppermute | solution.py:22
  11.5 3.4 %collective-permute-start = (bf16[8,1024]{1,0:T(8,128)(2,1)S(1)}, bf16[8,1024]{1,0:T(8,128)(2,1)S(1)}, u32[]{:S(2)}, u32[]{:S(2)}) collective-permute-start(bf16[8,1024]{1,0:T(8,128)(2,1)S(1)} %slice.150), channel_id=1, source_target_pairs={{0,8},{8,16},{16,24},{24,32},{32,40},{40,48},{48,56},{56,64},{64,7... | collective-permute-start | bytes 49160 | tf_op jit(solution)/shard_map/ppermute | solution.py:144
  14.8 18.0 %collective-permute-start.10 = (bf16[2,448,256]{2,1,0:T(8,128)(2,1)S(1)}, bf16[2,448,256]{2,1,0:T(8,128)(2,1)S(1)}, u32[]{:S(2)}, u32[]{:S(2)}) collective-permute-start(bf16[2,448,256]{2,1,0:T(8,128)(2,1)S(1)} %pad_maximum_fusion.6.refs_0_), channel_id=1, source_target_pairs={{0,96},{8,104},{16,112},{24,120},{32,0},{40,8},{48,16},{56,24},{64... | collective-permute-start | bytes 1376264 | tf_op jit(solution)/shard_map/ppermute | solution.py:22
  14.9 19.5 %collective-permute-start.8 = (bf16[2,448,256]{2,1,0:T(8,128)(2,1)S(1)}, bf16[2,448,256]{2,1,0:T(8,128)(2,1)S(1)}, u32[]{:S(2)}, u32[]{:S(2)}) collective-permute-start(bf16[2,448,256]{2,1,0:T(8,128)(2,1)S(1)} %pad_maximum_fusion.6.refs_0_), channel_id=1, source_target_pairs={{0,32},{8,40},{16,48},{24,56},{32,64},{40,72},{48,80},{56,88},{64,... | collective-permute-start | bytes 1376264 | tf_op jit(solution)/shard_map/ppermute | solution.py:22
  23.5 18.7 %copy-start.20 = (f32[128,16]{0,1:T(8,128)S(1)}, f32[128,16]{0,1:T(8,128)}, u32[]{:S(2)}) copy-start(f32[128,16]{0,1:T(8,128)} %param.27) | copy-start | bytes 24580
  23.6 3.5 %collective-permute-start.5 = (f32[17,8,128]{2,1,0:T(8,128)S(1)}, f32[17,8,128]{2,1,0:T(8,128)S(1)}, u32[]{:S(2)}, u32[]{:S(2)}) collective-permute-start(f32[17,8,128]{2,1,0:T(8,128)S(1)} %get-tuple-element.26), channel_id=1, source_target_pairs={{0,24},{8,0},{16,8},{24,16},{32,56},{40,32},{48,40},{56,48},{64,88... | collective-permute-start | bytes 208904 | tf_op jit(solution)/shard_map/ppermute | solution.py:22
  23.9 4.7 %collective-permute-start.6 = (f32[17,8,128]{2,1,0:T(8,128)S(1)}, f32[17,8,128]{2,1,0:T(8,128)S(1)}, u32[]{:S(2)}, u32[]{:S(2)}) collective-permute-start(f32[17,8,128]{2,1,0:T(8,128)S(1)} %get-tuple-element.26), channel_id=1, source_target_pairs={{0,16},{8,24},{16,0},{24,8},{32,48},{40,56},{48,32},{56,40},{64,80... | collective-permute-start | bytes 208904 | tf_op jit(solution)/shard_map/ppermute | solution.py:22
  24.2 5.4 %collective-permute-start.7 = (f32[17,8,128]{2,1,0:T(8,128)S(1)}, f32[17,8,128]{2,1,0:T(8,128)S(1)}, u32[]{:S(2)}, u32[]{:S(2)}) collective-permute-start(f32[17,8,128]{2,1,0:T(8,128)S(1)} %get-tuple-element.26), channel_id=1, source_target_pairs={{0,8},{8,16},{16,24},{24,0},{32,40},{40,48},{48,56},{56,32},{64,72... | collective-permute-start | bytes 208904 | tf_op jit(solution)/shard_map/ppermute | solution.py:22
  25.1 24.8 %copy-start.11 = (bf16[128,1024]{1,0:T(8,128)(2,1)S(1)}, bf16[128,1024]{1,0:T(8,128)(2,1)}, u32[]{:S(2)}) copy-start(bf16[128,1024]{1,0:T(8,128)(2,1)} %gate_ref.1) | copy-start | bytes 786436
  25.1 24.8 %copy-start.16 = (f32[1024]{0:T(1024)S(1)}, f32[1024]{0:T(1024)}, u32[]{:S(2)}) copy-start(f32[1024]{0:T(1024)} %param.28) | copy-start | bytes 12292
  27.1 14.3 %collective-permute-start.9 = (bf16[2,448,256]{2,1,0:T(8,128)(2,1)S(1)}, bf16[2,448,256]{2,1,0:T(8,128)(2,1)S(1)}, u32[]{:S(2)}, u32[]{:S(2)}) collective-permute-start(bf16[2,448,256]{2,1,0:T(8,128)(2,1)S(1)} %pad_maximum_fusion.6.refs_0_), channel_id=1, source_target_pairs={{0,64},{8,72},{16,80},{24,88},{32,96},{40,104},{48,112},{56,120},{... | collective-permute-start | bytes 1376264 | tf_op jit(solution)/shard_map/ppermute | solution.py:22
  30.4 33.1 %collective-permute-start.15 = (bf16[4,576,256]{2,1,0:T(8,128)(2,1)S(1)}, bf16[4,576,256]{2,1,0:T(8,128)(2,1)S(1)}, u32[]{:S(2)}, u32[]{:S(2)}) collective-permute-start(bf16[4,576,256]{2,1,0:T(8,128)(2,1)S(1)} %pad_maximum_fusion.3.refs_4_), channel_id=1, source_target_pairs={{0,16},{8,24},{16,0},{24,8},{32,48},{40,56},{48,32},{56,40},{64,80... | collective-permute-start | bytes 3538952 | tf_op jit(solution)/shard_map/ppermute | solution.py:22
  42.2 5.2 %collective-permute-start.12 = (f32[17,8,128]{2,1,0:T(8,128)}, f32[17,8,128]{2,1,0:T(8,128)}, u32[]{:S(2)}, u32[]{:S(2)}) collective-permute-start(f32[17,8,128]{2,1,0:T(8,128)} %pad_maximum_fusion.7), channel_id=1, source_target_pairs={{0,64},{8,72},{16,80},{24,88},{32,96},{40,104},{48,112},{56,120},{... | collective-permute-start | bytes 208904 | tf_op jit(solution)/shard_map/ppermute | solution.py:22
  42.3 6.5 %collective-permute-start.11 = (f32[17,8,128]{2,1,0:T(8,128)}, f32[17,8,128]{2,1,0:T(8,128)S(1)}, u32[]{:S(2)}, u32[]{:S(2)}) collective-permute-start(f32[17,8,128]{2,1,0:T(8,128)} %pad_maximum_fusion.7), channel_id=1, source_target_pairs={{0,32},{8,40},{16,48},{24,56},{32,64},{40,72},{48,80},{56,88},{64,... | collective-permute-start | bytes 208904 | tf_op jit(solution)/shard_map/ppermute | solution.py:22
  45.1 3.9 %collective-permute-start.13 = (f32[17,8,128]{2,1,0:T(8,128)}, f32[17,8,128]{2,1,0:T(8,128)S(1)}, u32[]{:S(2)}, u32[]{:S(2)}) collective-permute-start(f32[17,8,128]{2,1,0:T(8,128)} %pad_maximum_fusion.7), channel_id=1, source_target_pairs={{0,96},{8,104},{16,112},{24,120},{32,0},{40,8},{48,16},{56,24},{64... | collective-permute-start | bytes 208904 | tf_op jit(solution)/shard_map/ppermute | solution.py:22
  58.2 5.3 %collective-permute-start.14 = (bf16[128,1024]{1,0:T(8,128)(2,1)S(1)}, bf16[128,1024]{1,0:T(8,128)(2,1)S(1)}, u32[]{:S(2)}, u32[]{:S(2)}) collective-permute-start(bf16[128,1024]{1,0:T(8,128)(2,1)S(1)} %scan_output.1.own_ref), channel_id=1, source_target_pairs={{0,8},{8,0},{16,24},{24,16},{32,40},{40,32},{48,56},{56,48},{64,72... | collective-permute-start | bytes 786440 | tf_op jit(solution)/shard_map/ppermute | solution.py:27
  69.7 24.9 %all-to-all-start = ((bf16[8,2,128,256]{3,2,1,0:T(8,128)(2,1)}), bf16[8,2,128,256]{3,2,1,0:T(8,128)(2,1)S(1)}, u32[]{:S(2)}, u32[]{:S(2)}) async-start(bf16[8,2,128,256]{3,2,1,0:T(8,128)(2,1)} %project.1), calls=%async_computation | async-start | bytes 2097152 | tf_op jit(solution)/shard_map/all_to_all | solution.py:211
  94.8 3.2 %collective-permute-start.16 = (bf16[128,256]{1,0:T(8,128)(2,1)S(1)}, bf16[128,256]{1,0:T(8,128)(2,1)S(1)}, u32[]{:S(2)}, u32[]{:S(2)}) collective-permute-start(bf16[128,256]{1,0:T(8,128)(2,1)S(1)} %fusion.56), channel_id=1, source_target_pairs={{0,8},{8,0},{16,24},{24,16},{32,40},{40,32},{48,56},{56,48},{64,72... | collective-permute-start | bytes 196616 | tf_op jit(solution)/shard_map/ppermute | solution.py:27
  110.8 20.7 %slice-start = ((s8[6291456]{0:T(1024)(128)(4,1)}), s8[4194304]{0:T(1024)(128)(4,1)S(1)}, s32[]{:S(2)}) async-start(s8[6291456]{0:T(1024)(128)(4,1)} %bitcast.243), calls=%async_computation.3 | async-start | bytes 8388608
  111.7 7.5 %collective-permute-start.17 = (bf16[24,4096]{1,0:T(8,128)(2,1)S(1)}, bf16[24,4096]{1,0:T(8,128)(2,1)S(1)}, u32[]{:S(2)}, u32[]{:S(2)}) collective-permute-start(bf16[24,4096]{1,0:T(8,128)(2,1)S(1)} %get-tuple-element.68), channel_id=1, source_target_pairs={{0,8},{8,16},{16,24},{24,0},{32,40},{40,48},{48,56},{56,32},{64,72... | collective-permute-start | bytes 589832 | tf_op jit(solution)/shard_map/ppermute | solution.py:22
  112.1 10.1 %collective-permute-start.18 = (bf16[24,4096]{1,0:T(8,128)(2,1)S(1)}, bf16[24,4096]{1,0:T(8,128)(2,1)S(1)}, u32[]{:S(2)}, u32[]{:S(2)}) collective-permute-start(bf16[24,4096]{1,0:T(8,128)(2,1)S(1)} %get-tuple-element.68), channel_id=1, source_target_pairs={{0,16},{8,24},{16,0},{24,8},{32,48},{40,56},{48,32},{56,40},{64,80... | collective-permute-start | bytes 589832 | tf_op jit(solution)/shard_map/ppermute | solution.py:22
  113.8 9.4 %collective-permute-start.19 = (bf16[24,4096]{1,0:T(8,128)(2,1)S(1)}, bf16[24,4096]{1,0:T(8,128)(2,1)S(1)}, u32[]{:S(2)}, u32[]{:S(2)}) collective-permute-start(bf16[24,4096]{1,0:T(8,128)(2,1)S(1)} %get-tuple-element.68), channel_id=1, source_target_pairs={{0,24},{8,0},{16,8},{24,16},{32,56},{40,32},{48,40},{56,48},{64,88... | collective-permute-start | bytes 589832 | tf_op jit(solution)/shard_map/ppermute | solution.py:22
  114.6 11.5 %collective-permute-start.20 = (bf16[24,4096]{1,0:T(8,128)(2,1)S(1)}, bf16[24,4096]{1,0:T(8,128)(2,1)S(1)}, u32[]{:S(2)}, u32[]{:S(2)}) collective-permute-start(bf16[24,4096]{1,0:T(8,128)(2,1)S(1)} %get-tuple-element.67), channel_id=1, source_target_pairs={{0,32},{8,40},{16,48},{24,56},{32,64},{40,72},{48,80},{56,88},{64,... | collective-permute-start | bytes 589832 | tf_op jit(solution)/shard_map/ppermute | solution.py:22
  115.3 10.8 %collective-permute-start.21 = (bf16[24,4096]{1,0:T(8,128)(2,1)S(1)}, bf16[24,4096]{1,0:T(8,128)(2,1)S(1)}, u32[]{:S(2)}, u32[]{:S(2)}) collective-permute-start(bf16[24,4096]{1,0:T(8,128)(2,1)S(1)} %get-tuple-element.67), channel_id=1, source_target_pairs={{0,64},{8,72},{16,80},{24,88},{32,96},{40,104},{48,112},{56,120},{... | collective-permute-start | bytes 589832 | tf_op jit(solution)/shard_map/ppermute | solution.py:22
  119.1 7.0 %collective-permute-start.22 = (bf16[24,4096]{1,0:T(8,128)(2,1)S(1)}, bf16[24,4096]{1,0:T(8,128)(2,1)S(1)}, u32[]{:S(2)}, u32[]{:S(2)}) collective-permute-start(bf16[24,4096]{1,0:T(8,128)(2,1)S(1)} %get-tuple-element.67), channel_id=1, source_target_pairs={{0,96},{8,104},{16,112},{24,120},{32,0},{40,8},{48,16},{56,24},{64... | collective-permute-start | bytes 589832 | tf_op jit(solution)/shard_map/ppermute | solution.py:22
  123.3 17.5 %collective-permute-start.23 = (bf16[4,24,4096]{2,1,0:T(8,128)(2,1)S(1)}, bf16[4,24,4096]{2,1,0:T(8,128)(2,1)S(1)}, u32[]{:S(2)}, u32[]{:S(2)}) collective-permute-start(bf16[4,24,4096]{2,1,0:T(8,128)(2,1)S(1)} %get-tuple-element.60), channel_id=1, source_target_pairs={{0,32},{8,40},{16,48},{24,56},{32,64},{40,72},{48,80},{56,88},{64,... | collective-permute-start | bytes 2359304 | tf_op jit(solution)/shard_map/ppermute | solution.py:22
  124.2 23.2 %collective-permute-start.24 = (bf16[4,24,4096]{2,1,0:T(8,128)(2,1)S(1)}, bf16[4,24,4096]{2,1,0:T(8,128)(2,1)S(1)}, u32[]{:S(2)}, u32[]{:S(2)}) collective-permute-start(bf16[4,24,4096]{2,1,0:T(8,128)(2,1)S(1)} %get-tuple-element.60), channel_id=1, source_target_pairs={{0,96},{8,104},{16,112},{24,120},{32,0},{40,8},{48,16},{56,24},{64... | collective-permute-start | bytes 2359304 | tf_op jit(solution)/shard_map/ppermute | solution.py:22
  126.2 21.1 %collective-permute-start.25 = (bf16[4,24,4096]{2,1,0:T(8,128)(2,1)S(1)}, bf16[4,24,4096]{2,1,0:T(8,128)(2,1)S(1)}, u32[]{:S(2)}, u32[]{:S(2)}) collective-permute-start(bf16[4,24,4096]{2,1,0:T(8,128)(2,1)S(1)} %get-tuple-element.62), channel_id=1, source_target_pairs={{0,8},{8,16},{16,24},{24,0},{32,40},{40,48},{48,56},{56,32},{64,72... | collective-permute-start | bytes 2359304 | tf_op jit(solution)/shard_map/ppermute | solution.py:22
  127.7 19.7 %collective-permute-start.26 = (bf16[4,24,4096]{2,1,0:T(8,128)(2,1)S(1)}, bf16[4,24,4096]{2,1,0:T(8,128)(2,1)S(1)}, u32[]{:S(2)}, u32[]{:S(2)}) collective-permute-start(bf16[4,24,4096]{2,1,0:T(8,128)(2,1)S(1)} %get-tuple-element.62), channel_id=1, source_target_pairs={{0,24},{8,0},{16,8},{24,16},{32,56},{40,32},{48,40},{56,48},{64,88... | collective-permute-start | bytes 2359304 | tf_op jit(solution)/shard_map/ppermute | solution.py:22
  129.8 29.8 %collective-permute-start.29 = (bf16[4,24,4096]{2,1,0:T(8,128)(2,1)S(1)}, bf16[4,24,4096]{2,1,0:T(8,128)(2,1)S(1)}, u32[]{:S(2)}, u32[]{:S(2)}) collective-permute-start(bf16[4,24,4096]{2,1,0:T(8,128)(2,1)S(1)} %get-tuple-element.60), channel_id=1, source_target_pairs={{0,64},{8,72},{16,80},{24,88},{32,96},{40,104},{48,112},{56,120},{... | collective-permute-start | bytes 2359304 | tf_op jit(solution)/shard_map/ppermute | solution.py:22
  140.8 22.0 %collective-permute-start.30 = (bf16[4,24,4096]{2,1,0:T(8,128)(2,1)S(1)}, bf16[4,24,4096]{2,1,0:T(8,128)(2,1)S(1)}, u32[]{:S(2)}, u32[]{:S(2)}) collective-permute-start(bf16[4,24,4096]{2,1,0:T(8,128)(2,1)S(1)} %get-tuple-element.62), channel_id=1, source_target_pairs={{0,16},{8,24},{16,0},{24,8},{32,48},{40,56},{48,32},{56,40},{64,80... | collective-permute-start | bytes 2359304 | tf_op jit(solution)/shard_map/ppermute | solution.py:22
  156.2 16.5 %collective-permute-start.27 = (bf16[4,24,4096]{2,1,0:T(8,128)(2,1)S(1)}, bf16[4,24,4096]{2,1,0:T(8,128)(2,1)S(1)}, u32[]{:S(2)}, u32[]{:S(2)}) collective-permute-start(bf16[4,24,4096]{2,1,0:T(8,128)(2,1)S(1)} %get-tuple-element.45), channel_id=1, source_target_pairs={{0,96},{8,104},{16,112},{24,120},{32,0},{40,8},{48,16},{56,24},{64... | collective-permute-start | bytes 2359304 | tf_op jit(solution)/shard_map/ppermute | solution.py:22
  156.3 30.0 %collective-permute-start.28 = (bf16[4,24,4096]{2,1,0:T(8,128)(2,1)S(1)}, bf16[4,24,4096]{2,1,0:T(8,128)(2,1)S(1)}, u32[]{:S(2)}, u32[]{:S(2)}) collective-permute-start(bf16[4,24,4096]{2,1,0:T(8,128)(2,1)S(1)} %get-tuple-element.48), channel_id=1, source_target_pairs={{0,32},{8,40},{16,48},{24,56},{32,64},{40,72},{48,80},{56,88},{64,... | collective-permute-start | bytes 2359304 | tf_op jit(solution)/shard_map/ppermute | solution.py:22
  167.4 18.9 %collective-permute-start.31 = (bf16[4,24,4096]{2,1,0:T(8,128)(2,1)S(1)}, bf16[4,24,4096]{2,1,0:T(8,128)(2,1)S(1)}, u32[]{:S(2)}, u32[]{:S(2)}) collective-permute-start(bf16[4,24,4096]{2,1,0:T(8,128)(2,1)S(1)} %bitcast.231), channel_id=1, source_target_pairs={{0,64},{8,72},{16,80},{24,88},{32,96},{40,104},{48,112},{56,120},{... | collective-permute-start | bytes 2359304 | tf_op jit(solution)/shard_map/ppermute | solution.py:22
  167.6 20.8 %collective-permute-start.35 = (bf16[4,24,4096]{2,1,0:T(8,128)(2,1)S(1)}, bf16[4,24,4096]{2,1,0:T(8,128)(2,1)S(1)}, u32[]{:S(2)}, u32[]{:S(2)}) collective-permute-start(bf16[4,24,4096]{2,1,0:T(8,128)(2,1)S(1)} %get-tuple-element.47), channel_id=1, source_target_pairs={{0,24},{8,0},{16,8},{24,16},{32,56},{40,32},{48,40},{56,48},{64,88... | collective-permute-start | bytes 2359304 | tf_op jit(solution)/shard_map/ppermute | solution.py:22
  170.3 20.1 %collective-permute-start.36 = (bf16[4,24,4096]{2,1,0:T(8,128)(2,1)S(1)}, bf16[4,24,4096]{2,1,0:T(8,128)(2,1)S(1)}, u32[]{:S(2)}, u32[]{:S(2)}) collective-permute-start(bf16[4,24,4096]{2,1,0:T(8,128)(2,1)S(1)} %get-tuple-element.46), channel_id=1, source_target_pairs={{0,8},{8,16},{16,24},{24,0},{32,40},{40,48},{48,56},{56,32},{64,72... | collective-permute-start | bytes 2359304 | tf_op jit(solution)/shard_map/ppermute | solution.py:22
  172.7 29.7 %collective-permute-start.37 = (bf16[4,24,4096]{2,1,0:T(8,128)(2,1)S(1)}, bf16[4,24,4096]{2,1,0:T(8,128)(2,1)S(1)}, u32[]{:S(2)}, u32[]{:S(2)}) collective-permute-start(bf16[4,24,4096]{2,1,0:T(8,128)(2,1)S(1)} %bitcast.228), channel_id=1, source_target_pairs={{0,16},{8,24},{16,0},{24,8},{32,48},{40,56},{48,32},{56,40},{64,80... | collective-permute-start | bytes 2359304 | tf_op jit(solution)/shard_map/ppermute | solution.py:22
  186.9 18.8 %collective-permute-start.32 = (bf16[24,4096]{1,0:T(8,128)(2,1)S(1)}, bf16[24,4096]{1,0:T(8,128)(2,1)S(1)}, u32[]{:S(2)}, u32[]{:S(2)}) collective-permute-start(bf16[24,4096]{1,0:T(8,128)(2,1)S(1)} %get-tuple-element.53), channel_id=1, source_target_pairs={{0,24},{8,0},{16,8},{24,16},{32,56},{40,32},{48,40},{56,48},{64,88... | collective-permute-start | bytes 589832 | tf_op jit(solution)/shard_map/ppermute | solution.py:22
  186.9 20.0 %collective-permute-start.33 = (bf16[24,4096]{1,0:T(8,128)(2,1)S(1)}, bf16[24,4096]{1,0:T(8,128)(2,1)S(1)}, u32[]{:S(2)}, u32[]{:S(2)}) collective-permute-start(bf16[24,4096]{1,0:T(8,128)(2,1)S(1)} %get-tuple-element.55), channel_id=1, source_target_pairs={{0,8},{8,16},{16,24},{24,0},{32,40},{40,48},{48,56},{56,32},{64,72... | collective-permute-start | bytes 589832 | tf_op jit(solution)/shard_map/ppermute | solution.py:22
  188.4 22.4 %collective-permute-start.34 = (bf16[24,4096]{1,0:T(8,128)(2,1)S(1)}, bf16[24,4096]{1,0:T(8,128)(2,1)S(1)}, u32[]{:S(2)}, u32[]{:S(2)}) collective-permute-start(bf16[24,4096]{1,0:T(8,128)(2,1)S(1)} %get-tuple-element.54), channel_id=1, source_target_pairs={{0,16},{8,24},{16,0},{24,8},{32,48},{40,56},{48,32},{56,40},{64,80... | collective-permute-start | bytes 589832 | tf_op jit(solution)/shard_map/ppermute | solution.py:22
  202.9 8.1 %collective-permute-start.38 = (bf16[24,4096]{1,0:T(8,128)(2,1)S(1)}, bf16[24,4096]{1,0:T(8,128)(2,1)S(1)}, u32[]{:S(2)}, u32[]{:S(2)}) collective-permute-start(bf16[24,4096]{1,0:T(8,128)(2,1)S(1)} %get-tuple-element.56), channel_id=1, source_target_pairs={{0,96},{8,104},{16,112},{24,120},{32,0},{40,8},{48,16},{56,24},{64... | collective-permute-start | bytes 589832 | tf_op jit(solution)/shard_map/ppermute | solution.py:22
  205.7 8.1 %collective-permute-start.39 = (bf16[24,4096]{1,0:T(8,128)(2,1)S(1)}, bf16[24,4096]{1,0:T(8,128)(2,1)S(1)}, u32[]{:S(2)}, u32[]{:S(2)}) collective-permute-start(bf16[24,4096]{1,0:T(8,128)(2,1)S(1)} %get-tuple-element.58), channel_id=1, source_target_pairs={{0,32},{8,40},{16,48},{24,56},{32,64},{40,72},{48,80},{56,88},{64,... | collective-permute-start | bytes 589832 | tf_op jit(solution)/shard_map/ppermute | solution.py:22
  205.7 8.1 %collective-permute-start.40 = (bf16[24,4096]{1,0:T(8,128)(2,1)S(1)}, bf16[24,4096]{1,0:T(8,128)(2,1)S(1)}, u32[]{:S(2)}, u32[]{:S(2)}) collective-permute-start(bf16[24,4096]{1,0:T(8,128)(2,1)S(1)} %get-tuple-element.57), channel_id=1, source_target_pairs={{0,64},{8,72},{16,80},{24,88},{32,96},{40,104},{48,112},{56,120},{... | collective-permute-start | bytes 589832 | tf_op jit(solution)/shard_map/ppermute | solution.py:22
  213.9 20.4 %copy-start.22 = (f32[128,2]{0,1:T(2,128)S(1)}, f32[128,2]{0,1:T(2,128)}, u32[]{:S(2)}) copy-start(f32[128,2]{0,1:T(2,128)} %param.31) | copy-start | bytes 3076
  214.9 27.5 %all-to-all-start.2 = ((bf16[8,48,512]{2,1,0:T(8,128)(2,1)}), bf16[8,48,512]{2,1,0:T(8,128)(2,1)S(1)}, u32[]{:S(2)}, u32[]{:S(2)}) async-start(bf16[8,48,512]{2,1,0:T(8,128)(2,1)} %copy.55), calls=%async_computation.2 | async-start | bytes 786432 | tf_op jit(solution)/shard_map/all_to_all | solution.py:290
  (24 other events, 198.9 us)

commit v5 on v4

--- a/solution.py
+++ b/solution.py
@@ -31,9 +31,17 @@
     return [block] + [shift(block, axis, distance) for distance in range(1, SIDE)]
 
 
+def relay_gather(blocks, axis):
+    half = blocks.shape[0] // 2
+    before = shift(blocks, axis, 1)
+    after = shift(blocks, axis, -1)
+    far = [shift(before[:half], axis, 1), shift(after[half:], axis, -1)]
+    return [blocks, before, jnp.concatenate(far), after]
+
+
 def grid_gather(block, order):
     near = jnp.stack(ring_gather(block, order[0]))
-    return ring_gather(near, order[1])
+    return relay_gather(near, order[1])
 
 
 def ring_scatter(blocks, axis):
@@ -142,7 +150,8 @@
     tokens, channels = mixer_in.shape
     count, index = lax.axis_size("seq"), lax.axis_index("seq")
     rim = lax.ppermute(mixer_in[tokens - 8 :], "seq", [(i, i + 1) for i in range(count - 1)])
-    split = 7 * channels // 16
+    rim, w_out = lax.optimization_barrier((rim, w_out))
+    split = 3 * channels // 8
     low, high = w_out[:split], w_out[split:]
     low_pair = jnp.stack([low, shift(low, "x", 2)])
     dt_raw, low_pair = lax.optimization_barrier((dt_raw, low_pair))

time: 244 us -> 250 us (1.025)
  waiting for transfers between devices: 74.2 us -> 101 us
  starting transfers between devices: 102 us -> 80.5 us
    ppermute x38 -> x40, waiting for transfers between devices: 44.9 us -> 67.7 us  [shift(): return lax.ppermute(value, 'seq', route)]
    ppermute x38 -> x40, starting transfers between devices: 69.6 us -> 50.7 us  [shift(): return lax.ppermute(value, 'seq', route)]
    all_to_all x1, starting transfers between devices: 19.4 us -> 9.7 us  [local(): returned = lax.all_to_all(summed, 'exp', split_axis=0, concat_axis=0)]
    all_to_all x1, starting transfers between devices: 9.76 us -> 15.8 us  [project(): partial = lax.all_to_all(partial, 'exp', split_axis=0, concat_axis=0)]
    ppermute x2, waiting for transfers between devices: 7.63 us -> 11.1 us  [partner(): return lax.ppermute(value, 'seq', [(i, i ^ 1) for i in cells])]
  transfers between devices with their start and end apart: 43 -> 45, of which waited for: 23 -> 21; matrix products, arithmetic and copies ran while one was open for 11% -> 9% of each run, Pallas kernels for 5% -> 4%
where the time goes in v5:
time: 250 us; the launch traced here: 249 us
  waiting for transfers between devices  101 us (40%)
  starting transfers between devices  80.5 us (32%)
  matrix products  18.2 us (7%)
  local copies, waits for them, and re-layouts  16 us (6%)
  Pallas kernels  14.6 us (6%)
  blocking collectives  12.5 us (5%)
  other arithmetic  5.64 us (2%)
    ppermute x40, waiting for transfers between devices, shift(): return lax.ppermute(value, 'seq', route)  67.7 us
    ppermute x40, starting transfers between devices, shift(): return lax.ppermute(value, 'seq', route)  50.7 us
    all_to_all x1, starting transfers between devices, project(): partial = lax.all_to_all(partial, 'exp', split_axis=0, concat_axis=0)  15.8 us
    all_to_all x1, waiting for transfers between devices, project(): partial = lax.all_to_all(partial, 'exp', split_axis=0, concat_axis=0)  13.5 us
    all_to_all x1, blocking collectives, local(): lax.all_to_all(outgoing, 'exp', split_axis=0, concat_axis=2, tiled=True)[0]  12.5 us
    ppermute x2, waiting for transfers between devices, partner(): return lax.ppermute(value, 'seq', [(i, i ^ 1) for i in cells])  11.1 us
    unnamed x65, local copies, waits for them, and re-layouts  11 us
    all_to_all x1, starting transfers between devices, local(): returned = lax.all_to_all(summed, 'exp', split_axis=0, concat_axis=0)  9.7 us
  transfers between devices with their start and end apart: 45, of which 21 were waited for; matrix products, arithmetic and copies ran while one was open for 9% of the time, Pallas kernels for 4%

profile of v5, /device:TPU:1, one launch (start us, length us, event | category | flops | bytes accessed | tf_op | source)
XLA Modules:
  0.0 249.3 jit_solution(12919692568167899505)
XLA Ops:
  0.8 3.9 %collective-permute-start = (bf16[8,1024]{1,0:T(8,128)(2,1)S(1)}, bf16[8,1024]{1,0:T(8,128)(2,1)S(1)}, u32[]{:S(2)}, u32[]{:S(2)}) collective-permute-start(bf16[8,1024]{1,0:T(8,128)(2,1)S(1)} %slice.162), channel_id=1, source_target_pairs={{0,8},{8,16},{16,24},{24,32},{32,40},{40,48},{48,56},{56,64},{64,7... | collective-permute-start | bytes 49160 | tf_op jit(solution)/shard_map/ppermute | solution.py:152
  7.6 4.0 %collective-permute-start.2 = (bf16[640,256]{1,0:T(8,128)(2,1)S(1)}, bf16[640,256]{1,0:T(8,128)(2,1)S(1)}, u32[]{:S(2)}, u32[]{:S(2)}) collective-permute-start(bf16[640,256]{1,0:T(8,128)(2,1)S(1)} %slice.164), channel_id=1, source_target_pairs={{0,32},{8,40},{16,48},{24,56},{32,64},{40,72},{48,80},{56,88},{64,... | collective-permute-start | bytes 983048 | tf_op jit(solution)/shard_map/ppermute | solution.py:22
  11.5 2.6 %collective-permute-start.3 = (bf16[640,256]{1,0:T(8,128)(2,1)S(1)}, bf16[640,256]{1,0:T(8,128)(2,1)S(1)}, u32[]{:S(2)}, u32[]{:S(2)}) collective-permute-start(bf16[640,256]{1,0:T(8,128)(2,1)S(1)} %slice.164), channel_id=1, source_target_pairs={{0,64},{8,72},{16,80},{24,88},{32,96},{40,104},{48,112},{56,120},{... | collective-permute-start | bytes 983048 | tf_op jit(solution)/shard_map/ppermute | solution.py:22
  16.9 4.4 %collective-permute-done.1 = bf16[384,256]{1,0:T(8,128)(2,1)S(1)} collective-permute-done((bf16[384,256]{1,0:T(8,128)(2,1)S(1)}, bf16[384,256]{1,0:T(8,128)(2,1)S(1)}, u32[]{:S(2)}, u32[]{:S(2)}) %collective-permute-start.1) | collective-permute-done | bytes 196640 | tf_op jit(solution)/shard_map/ppermute | solution.py:22
  22.9 4.9 %scan_state.1 = (f32[128,8,128]{2,1,0:T(8,128)S(1)}, f32[128,8,128]{2,1,0:T(8,128)S(1)}, f32[17,8,128]{2,1,0:T(8,128)S(1)}) custom-call(bf16[128,1024]{1,0:T(8,128)(2,1)S(1)} %copy-done.10, bf16[8,1024]{1,0:T(8,128)(2,1)S(1)} %collective-permute-done.rim_ref, bf16[128,1024]{1,0:T(8,128)(2,1)S(1)} %copy-done.12, f32[1,1024]{1,0:T(1,128)S(1)} %bitcast.207, ...), custom_call_target="tpu_custom_call" | custom-call | tf_op jit(solution)/shard_map/scan_state/pallas_call | solution.py:163
  27.9 1.7 collective-permute-done.4
  29.5 1.7 collective-permute-start.6
  32.5 2.4 collective-permute-done.7
  34.9 3.7 %collective-permute-start.10 = (bf16[2,384,256]{2,1,0:T(8,128)(2,1)S(1)}, bf16[2,384,256]{2,1,0:T(8,128)(2,1)S(1)}, u32[]{:S(2)}, u32[]{:S(2)}) collective-permute-start(bf16[2,384,256]{2,1,0:T(8,128)(2,1)S(1)} %pad_maximum_fusion.6.refs_0_), channel_id=1, source_target_pairs={{0,96},{8,104},{16,112},{24,120},{32,0},{40,8},{48,16},{56,24},{64... | collective-permute-start | bytes 1179656 | tf_op jit(solution)/shard_map/ppermute | solution.py:22
  40.3 3.7 %collective-permute-done.9.refs_2_ = bf16[2,384,256]{2,1,0:T(8,128)(2,1)S(1)} collective-permute-done((bf16[2,384,256]{2,1,0:T(8,128)(2,1)S(1)}, bf16[2,384,256]{2,1,0:T(8,128)(2,1)S(1)}, u32[]{:S(2)}, u32[]{:S(2)}) %collective-permute-start.9) | collective-permute-done | bytes 393248 | tf_op jit(solution)/shard_map/ppermute | solution.py:22
  45.8 1.4 collective-permute-start.12
  47.3 2.7 %collective-permute-start.11 = (f32[17,8,128]{2,1,0:T(8,128)}, f32[17,8,128]{2,1,0:T(8,128)S(1)}, u32[]{:S(2)}, u32[]{:S(2)}) collective-permute-start(f32[17,8,128]{2,1,0:T(8,128)} %pad_maximum_fusion.7), channel_id=1, source_target_pairs={{0,32},{8,40},{16,48},{24,56},{32,64},{40,72},{48,80},{56,88},{64,... | collective-permute-start | bytes 208904 | tf_op jit(solution)/shard_map/ppermute | solution.py:22
  52.2 1.4 collective-permute-done.13
  56.8 6.1 %scan_output.1.own_ref = bf16[128,1024]{1,0:T(8,128)(2,1)S(1)} custom-call(f32[128,8,128]{2,1,0:T(8,128)S(1)} %copy-done.1, f32[128,8,128]{2,1,0:T(8,128)S(1)} %copy-done.3, bf16[128,1024]{1,0:T(8,128)(2,1)S(1)} %copy-done.11, f32[16,8,128]{2,1,0:T(8,128)S(1)} %fusion.65.enter_ref, f32[16,8,128]{2,1,0:T(8,128)S(1)} %bitcast.205, f32[8,128]{1,0:T(8,128)S(1)} %bitcast.209, ...), custom_call_target="tpu_custom_call" | custom-call | tf_op jit(solution)/shard_map/scan_output/pallas_call | solution.py:176
  63.1 8.2 %collective-permute-done.14.other_ref = bf16[128,1024]{1,0:T(8,128)(2,1)} collective-permute-done((bf16[128,1024]{1,0:T(8,128)(2,1)S(1)}, bf16[128,1024]{1,0:T(8,128)(2,1)}, u32[]{:S(2)}, u32[]{:S(2)}) %collective-permute-start.14) | collective-permute-done | bytes 262176 | tf_op jit(solution)/shard_map/ppermute | solution.py:27
  74.2 3.5 %project.1 = bf16[8,2,128,256]{3,2,1,0:T(8,128)(2,1)} custom-call(s32[2]{0:T(128)S(1)} %pad_add_fusion.place_ref, bf16[128,1024]{1,0:T(8,128)(2,1)S(1)} %scan_output.1.own_ref, bf16[128,1024]{1,0:T(8,128)(2,1)} %collective-permute-done.14.other_ref, bf16[2,384,256]{2,1,0:T(8,128)(2,1)S(1)} %pad_maximum_fusion.6.refs_0_, bf16[2,384,256]{2,1,0:T(8,128)(2,1)S(1)} %copy-done.5, ...), custom_call_target="tpu_custom_call" | custom-call | tf_op jit(solution)/shard_map/project/pallas_call | solution.py:211
  77.7 15.8 %all-to-all-start = ((bf16[8,2,128,256]{3,2,1,0:T(8,128)(2,1)}), bf16[8,2,128,256]{3,2,1,0:T(8,128)(2,1)S(1)}, u32[]{:S(2)}, u32[]{:S(2)}) async-start(bf16[8,2,128,256]{3,2,1,0:T(8,128)(2,1)} %project.1), calls=%async_computation | async-start | bytes 2097152 | tf_op jit(solution)/shard_map/all_to_all | solution.py:220
  95.1 13.5 %all-to-all-done = bf16[8,2,128,256]{3,2,1,0:T(8,128)(2,1)S(1)} async-done(((bf16[8,2,128,256]{3,2,1,0:T(8,128)(2,1)}), bf16[8,2,128,256]{3,2,1,0:T(8,128)(2,1)S(1)}, u32[]{:S(2)}, u32[]{:S(2)}) %all-to-all-start) | async-done | bytes 1048608 | tf_op jit(solution)/shard_map/all_to_all | solution.py:220
  109.1 3.0 %collective-permute-done.16 = bf16[128,256]{1,0:T(8,128)(2,1)S(1)} collective-permute-done((bf16[128,256]{1,0:T(8,128)(2,1)S(1)}, bf16[128,256]{1,0:T(8,128)(2,1)S(1)}, u32[]{:S(2)}, u32[]{:S(2)}) %collective-permute-start.16) | collective-permute-done | bytes 65568 | tf_op jit(solution)/shard_map/ppermute | solution.py:27
  112.3 12.5 %all_to_all.19 = bf16[8,48,512]{2,1,0:T(8,128)(2,1)S(1)} all-to-all(bf16[8,48,512]{2,1,0:T(8,128)(2,1)S(1)} %bitcast.226), channel_id=1, replica_groups=mesh['seq'=16,'exp'=8] {'exp'}, dimensions={0} | all-to-all | bytes 786432 | tf_op jit(solution)/shard_map/all_to_all | solution.py:271
  125.7 3.0 %collective-permute-start.22 = (bf16[24,4096]{1,0:T(8,128)(2,1)S(1)}, bf16[24,4096]{1,0:T(8,128)(2,1)S(1)}, u32[]{:S(2)}, u32[]{:S(2)}) collective-permute-start(bf16[24,4096]{1,0:T(8,128)(2,1)S(1)} %get-tuple-element.71), channel_id=1, source_target_pairs={{0,96},{8,104},{16,112},{24,120},{32,0},{40,8},{48,16},{56,24},{64... | collective-permute-start | bytes 589832 | tf_op jit(solution)/shard_map/ppermute | solution.py:22
  129.4 2.8 %collective-permute-start.19 = (bf16[24,4096]{1,0:T(8,128)(2,1)S(1)}, bf16[24,4096]{1,0:T(8,128)(2,1)S(1)}, u32[]{:S(2)}, u32[]{:S(2)}) collective-permute-start(bf16[24,4096]{1,0:T(8,128)(2,1)S(1)} %get-tuple-element.72), channel_id=1, source_target_pairs={{0,24},{8,0},{16,8},{24,16},{32,56},{40,32},{48,40},{56,48},{64,88... | collective-permute-start | bytes 589832 | tf_op jit(solution)/shard_map/ppermute | solution.py:22
  132.3 4.1 %collective-permute-done.22 = bf16[24,4096]{1,0:T(8,128)(2,1)S(1)} collective-permute-done((bf16[24,4096]{1,0:T(8,128)(2,1)S(1)}, bf16[24,4096]{1,0:T(8,128)(2,1)S(1)}, u32[]{:S(2)}, u32[]{:S(2)}) %collective-permute-start.22) | collective-permute-done | bytes 196640 | tf_op jit(solution)/shard_map/ppermute | solution.py:22
  136.5 4.2 %collective-permute-done.20 = bf16[24,4096]{1,0:T(8,128)(2,1)S(1)} collective-permute-done((bf16[24,4096]{1,0:T(8,128)(2,1)S(1)}, bf16[24,4096]{1,0:T(8,128)(2,1)S(1)}, u32[]{:S(2)}, u32[]{:S(2)}) %collective-permute-start.20) | collective-permute-done | bytes 196640 | tf_op jit(solution)/shard_map/ppermute | solution.py:22
  140.8 2.9 %collective-permute-start.26 = (bf16[4,24,4096]{2,1,0:T(8,128)(2,1)S(1)}, bf16[4,24,4096]{2,1,0:T(8,128)(2,1)S(1)}, u32[]{:S(2)}, u32[]{:S(2)}) collective-permute-start(bf16[4,24,4096]{2,1,0:T(8,128)(2,1)S(1)} %get-tuple-element.66), channel_id=1, source_target_pairs={{0,24},{8,0},{16,8},{24,16},{32,56},{40,32},{48,40},{56,48},{64,88... | collective-permute-start | bytes 2359304 | tf_op jit(solution)/shard_map/ppermute | solution.py:22
  143.8 2.5 collective-permute-start.24
  146.6 1.4 fusion.16
  149.3 1.4 fusion.40
  151.3 1.4 fusion.21
  152.7 7.0 %collective-permute-done.26 = bf16[4,24,4096]{2,1,0:T(8,128)(2,1)S(1)} collective-permute-done((bf16[4,24,4096]{2,1,0:T(8,128)(2,1)S(1)}, bf16[4,24,4096]{2,1,0:T(8,128)(2,1)S(1)}, u32[]{:S(2)}, u32[]{:S(2)}) %collective-permute-start.26) | collective-permute-done | bytes 786464 | tf_op jit(solution)/shard_map/ppermute | solution.py:22
  159.7 3.5 %collective-permute-start.32 = (bf16[2,24,4096]{2,1,0:T(8,128)(2,1)S(1)}, bf16[2,24,4096]{2,1,0:T(8,128)(2,1)S(1)}, u32[]{:S(2)}, u32[]{:S(2)}) collective-permute-start(bf16[2,24,4096]{2,1,0:T(8,128)(2,1)S(1)} %slice.230), channel_id=1, source_target_pairs={{0,24},{8,0},{16,8},{24,16},{32,56},{40,32},{48,40},{56,48},{64,88... | collective-permute-start | bytes 1179656 | tf_op jit(solution)/shard_map/ppermute | solution.py:22
  163.5 1.7 collective-permute-start.29
  165.6 2.6 %fusion.14 = f32[384,768]{1,0:T(8,128)S(1)} fusion(bf16[384,4096]{1,0:T(8,128)(2,1)S(1)} %bitcast.212, bf16[1,4096,768]{2,1,0:T(8,128)(2,1)S(1)} %bitcast.246), kind=kOutput, calls=%fused_computation.14 | convolution fusion | flops 2415919104 | bytes 10616832 | tf_op jit(solution)/shard_map/dot_general | solution.py:282
  168.3 2.7 %multiply_convert_fusion = bf16[384,768]{1,0:T(8,128)(2,1)S(1)} fusion(f32[384,768]{1,0:T(8,128)S(1)} %fusion.14, bf16[384,4096]{1,0:T(8,128)(2,1)S(1)} %bitcast.213, bf16[1,4096,768]{2,1,0:T(8,128)(2,1)S(1)} %bitcast.248), kind=kOutput, calls=%fused_computation.37 | convolution fusion | flops 2417688576 | bytes 11206656 | tf_op jit(solution)/shard_map/dot_general | solution.py:283
  171.0 2.8 %fusion.18 = bf16[384,4096]{1,0:T(8,128)(2,1)S(1)} fusion(bf16[384,768]{1,0:T(8,128)(2,1)S(1)} %multiply_convert_fusion, bf16[1,768,4096]{2,1,0:T(8,128)(2,1)S(1)} %bitcast.250), kind=kOutput, calls=%fused_computation.18 | convolution fusion | flops 2417491968 | bytes 10027008 | tf_op jit(solution)/shard_map/dot_general | solution.py:285
  174.1 2.7 %collective-permute-start.37 = (bf16[4,24,4096]{2,1,0:T(8,128)(2,1)S(1)}, bf16[4,24,4096]{2,1,0:T(8,128)(2,1)S(1)}, u32[]{:S(2)}, u32[]{:S(2)}) collective-permute-start(bf16[4,24,4096]{2,1,0:T(8,128)(2,1)S(1)} %get-tuple-element.51), channel_id=1, source_target_pairs={{0,24},{8,0},{16,8},{24,16},{32,56},{40,32},{48,40},{56,48},{64,88... | collective-permute-start | bytes 2359304 | tf_op jit(solution)/shard_map/ppermute | solution.py:22
  177.2 1.4 fusion.12
  178.6 1.4 fusion.37
  180.1 1.4 fusion.24
  183.0 2.6 %collective-permute-start.27 = (bf16[4,24,4096]{2,1,0:T(8,128)(2,1)S(1)}, bf16[4,24,4096]{2,1,0:T(8,128)(2,1)S(1)}, u32[]{:S(2)}, u32[]{:S(2)}) collective-permute-start(bf16[4,24,4096]{2,1,0:T(8,128)(2,1)S(1)} %get-tuple-element.49), channel_id=1, source_target_pairs={{0,96},{8,104},{16,112},{24,120},{32,0},{40,8},{48,16},{56,24},{64... | collective-permute-start | bytes 2359304 | tf_op jit(solution)/shard_map/ppermute | solution.py:22
  185.7 5.7 %collective-permute-done.38 = bf16[4,24,4096]{2,1,0:T(8,128)(2,1)S(1)} collective-permute-done((bf16[4,24,4096]{2,1,0:T(8,128)(2,1)S(1)}, bf16[4,24,4096]{2,1,0:T(8,128)(2,1)S(1)}, u32[]{:S(2)}, u32[]{:S(2)}) %collective-permute-start.38) | collective-permute-done | bytes 786464 | tf_op jit(solution)/shard_map/ppermute | solution.py:22
  192.4 17.1 %collective-permute-done.39 = bf16[4,24,4096]{2,1,0:T(8,128)(2,1)S(1)} collective-permute-done((bf16[4,24,4096]{2,1,0:T(8,128)(2,1)S(1)}, bf16[4,24,4096]{2,1,0:T(8,128)(2,1)S(1)}, u32[]{:S(2)}, u32[]{:S(2)}) %collective-permute-start.39) | collective-permute-done | bytes 786464 | tf_op jit(solution)/shard_map/ppermute | solution.py:22
  211.7 2.0 collective-permute-start.40
  213.7 2.1 collective-permute-done.33
  217.5 2.5 %collective-permute-done.42 = bf16[24,4096]{1,0:T(8,128)(2,1)S(1)} collective-permute-done((bf16[24,4096]{1,0:T(8,128)(2,1)S(1)}, bf16[24,4096]{1,0:T(8,128)(2,1)S(1)}, u32[]{:S(2)}, u32[]{:S(2)}) %collective-permute-start.42) | collective-permute-done | bytes 196640 | tf_op jit(solution)/shard_map/ppermute | solution.py:22
  220.0 8.9 %collective-permute-done.41 = bf16[24,4096]{1,0:T(8,128)(2,1)S(1)} collective-permute-done((bf16[24,4096]{1,0:T(8,128)(2,1)S(1)}, bf16[24,4096]{1,0:T(8,128)(2,1)S(1)}, u32[]{:S(2)}, u32[]{:S(2)}) %collective-permute-start.41) | collective-permute-done | bytes 196640 | tf_op jit(solution)/shard_map/ppermute | solution.py:22
  230.3 9.7 %all-to-all-start.2 = ((bf16[8,48,512]{2,1,0:T(8,128)(2,1)}), bf16[8,48,512]{2,1,0:T(8,128)(2,1)S(1)}, u32[]{:S(2)}, u32[]{:S(2)}) async-start(bf16[8,48,512]{2,1,0:T(8,128)(2,1)} %copy.55), calls=%async_computation.2 | async-start | bytes 786432 | tf_op jit(solution)/shard_map/all_to_all | solution.py:299
  240.0 8.1 %all-to-all-done.2 = bf16[8,48,512]{2,1,0:T(8,128)(2,1)S(1)} async-done(((bf16[8,48,512]{2,1,0:T(8,128)(2,1)}), bf16[8,48,512]{2,1,0:T(8,128)(2,1)S(1)}, u32[]{:S(2)}, u32[]{:S(2)}) %all-to-all-start.2) | async-done | bytes 393248 | tf_op jit(solution)/shard_map/all_to_all | solution.py:299
  (182 shorter events, 37.7 us)
Async XLA Ops:
  0.0 22.9 %copy-start.10 = (bf16[128,1024]{1,0:T(8,128)(2,1)S(1)}, bf16[128,1024]{1,0:T(8,128)(2,1)}, u32[]{:S(2)}) copy-start(bf16[128,1024]{1,0:T(8,128)(2,1)} %x_ref.1) | copy-start | bytes 786436
  0.0 22.9 %copy-start.12 = (bf16[128,1024]{1,0:T(8,128)(2,1)S(1)}, bf16[128,1024]{1,0:T(8,128)(2,1)}, u32[]{:S(2)}) copy-start(bf16[128,1024]{1,0:T(8,128)(2,1)} %dt_ref) | copy-start | bytes 786436
  0.0 22.8 %copy-start.14 = (f32[1024]{0:T(1024)S(1)}, f32[1024]{0:T(1024)}, u32[]{:S(2)}) copy-start(f32[1024]{0:T(1024)} %param.22) | copy-start | bytes 12292
  0.8 4.8 %collective-permute-start = (bf16[8,1024]{1,0:T(8,128)(2,1)S(1)}, bf16[8,1024]{1,0:T(8,128)(2,1)S(1)}, u32[]{:S(2)}, u32[]{:S(2)}) collective-permute-start(bf16[8,1024]{1,0:T(8,128)(2,1)S(1)} %slice.162), channel_id=1, source_target_pairs={{0,8},{8,16},{16,24},{24,32},{32,40},{40,48},{48,56},{56,64},{64,7... | collective-permute-start | bytes 49160 | tf_op jit(solution)/shard_map/ppermute | solution.py:152
  7.6 20.3 %collective-permute-start.2 = (bf16[640,256]{1,0:T(8,128)(2,1)S(1)}, bf16[640,256]{1,0:T(8,128)(2,1)S(1)}, u32[]{:S(2)}, u32[]{:S(2)}) collective-permute-start(bf16[640,256]{1,0:T(8,128)(2,1)S(1)} %slice.164), channel_id=1, source_target_pairs={{0,32},{8,40},{16,48},{24,56},{32,64},{40,72},{48,80},{56,88},{64,... | collective-permute-start | bytes 983048 | tf_op jit(solution)/shard_map/ppermute | solution.py:22
  11.5 16.3 %collective-permute-start.3 = (bf16[640,256]{1,0:T(8,128)(2,1)S(1)}, bf16[640,256]{1,0:T(8,128)(2,1)S(1)}, u32[]{:S(2)}, u32[]{:S(2)}) collective-permute-start(bf16[640,256]{1,0:T(8,128)(2,1)S(1)} %slice.164), channel_id=1, source_target_pairs={{0,64},{8,72},{16,80},{24,88},{32,96},{40,104},{48,112},{56,120},{... | collective-permute-start | bytes 983048 | tf_op jit(solution)/shard_map/ppermute | solution.py:22
  14.2 15.4 %collective-permute-start.4 = (bf16[640,256]{1,0:T(8,128)(2,1)S(1)}, bf16[640,256]{1,0:T(8,128)(2,1)S(1)}, u32[]{:S(2)}, u32[]{:S(2)}) collective-permute-start(bf16[640,256]{1,0:T(8,128)(2,1)S(1)} %slice.164), channel_id=1, source_target_pairs={{0,96},{8,104},{16,112},{24,120},{32,0},{40,8},{48,16},{56,24},{64... | collective-permute-start | bytes 983048 | tf_op jit(solution)/shard_map/ppermute | solution.py:22
  15.2 6.0 %collective-permute-start.1 = (bf16[384,256]{1,0:T(8,128)(2,1)S(1)}, bf16[384,256]{1,0:T(8,128)(2,1)S(1)}, u32[]{:S(2)}, u32[]{:S(2)}) collective-permute-start(bf16[384,256]{1,0:T(8,128)(2,1)S(1)} %get-tuple-element.68), channel_id=1, source_target_pairs={{0,16},{8,24},{16,0},{24,8},{32,48},{40,56},{48,32},{56,40},{64,80... | collective-permute-start | bytes 589832 | tf_op jit(solution)/shard_map/ppermute | solution.py:22
  21.3 18.2 %collective-permute-start.8 = (bf16[2,384,256]{2,1,0:T(8,128)(2,1)S(1)}, bf16[2,384,256]{2,1,0:T(8,128)(2,1)S(1)}, u32[]{:S(2)}, u32[]{:S(2)}) collective-permute-start(bf16[2,384,256]{2,1,0:T(8,128)(2,1)S(1)} %pad_maximum_fusion.6.refs_0_), channel_id=1, source_target_pairs={{0,32},{8,40},{16,48},{24,56},{32,64},{40,72},{48,80},{56,88},{64,... | collective-permute-start | bytes 1179656 | tf_op jit(solution)/shard_map/ppermute | solution.py:22
  21.8 22.2 %collective-permute-start.9 = (bf16[2,384,256]{2,1,0:T(8,128)(2,1)S(1)}, bf16[2,384,256]{2,1,0:T(8,128)(2,1)S(1)}, u32[]{:S(2)}, u32[]{:S(2)}) collective-permute-start(bf16[2,384,256]{2,1,0:T(8,128)(2,1)S(1)} %pad_maximum_fusion.6.refs_0_), channel_id=1, source_target_pairs={{0,64},{8,72},{16,80},{24,88},{32,96},{40,104},{48,112},{56,120},{... | collective-permute-start | bytes 1179656 | tf_op jit(solution)/shard_map/ppermute | solution.py:22
  29.5 5.4 %collective-permute-start.7 = (f32[17,8,128]{2,1,0:T(8,128)S(1)}, f32[17,8,128]{2,1,0:T(8,128)S(1)}, u32[]{:S(2)}, u32[]{:S(2)}) collective-permute-start(f32[17,8,128]{2,1,0:T(8,128)S(1)} %get-tuple-element.30), channel_id=1, source_target_pairs={{0,8},{8,16},{16,24},{24,0},{32,40},{40,48},{48,56},{56,32},{64,72... | collective-permute-start | bytes 208904 | tf_op jit(solution)/shard_map/ppermute | solution.py:22
  29.5 9.2 %collective-permute-start.6 = (f32[17,8,128]{2,1,0:T(8,128)S(1)}, f32[17,8,128]{2,1,0:T(8,128)S(1)}, u32[]{:S(2)}, u32[]{:S(2)}) collective-permute-start(f32[17,8,128]{2,1,0:T(8,128)S(1)} %get-tuple-element.30), channel_id=1, source_target_pairs={{0,16},{8,24},{16,0},{24,8},{32,48},{40,56},{48,32},{56,40},{64,80... | collective-permute-start | bytes 208904 | tf_op jit(solution)/shard_map/ppermute | solution.py:22
  31.2 7.5 %collective-permute-start.5 = (f32[17,8,128]{2,1,0:T(8,128)S(1)}, f32[17,8,128]{2,1,0:T(8,128)S(1)}, u32[]{:S(2)}, u32[]{:S(2)}) collective-permute-start(f32[17,8,128]{2,1,0:T(8,128)S(1)} %get-tuple-element.30), channel_id=1, source_target_pairs={{0,24},{8,0},{16,8},{24,16},{32,56},{40,32},{48,40},{56,48},{64,88... | collective-permute-start | bytes 208904 | tf_op jit(solution)/shard_map/ppermute | solution.py:22
  34.9 10.1 %collective-permute-start.10 = (bf16[2,384,256]{2,1,0:T(8,128)(2,1)S(1)}, bf16[2,384,256]{2,1,0:T(8,128)(2,1)S(1)}, u32[]{:S(2)}, u32[]{:S(2)}) collective-permute-start(bf16[2,384,256]{2,1,0:T(8,128)(2,1)S(1)} %pad_maximum_fusion.6.refs_0_), channel_id=1, source_target_pairs={{0,96},{8,104},{16,112},{24,120},{32,0},{40,8},{48,16},{56,24},{64... | collective-permute-start | bytes 1179656 | tf_op jit(solution)/shard_map/ppermute | solution.py:22
  39.5 31.8 %collective-permute-start.15 = (bf16[4,640,256]{2,1,0:T(8,128)(2,1)S(1)}, bf16[4,640,256]{2,1,0:T(8,128)(2,1)S(1)}, u32[]{:S(2)}, u32[]{:S(2)}) collective-permute-start(bf16[4,640,256]{2,1,0:T(8,128)(2,1)S(1)} %pad_maximum_fusion.3.refs_4_), channel_id=1, source_target_pairs={{0,16},{8,24},{16,0},{24,8},{32,48},{40,56},{48,32},{56,40},{64,80... | collective-permute-start | bytes 3932168 | tf_op jit(solution)/shard_map/ppermute | solution.py:22
  45.8 5.2 %collective-permute-start.12 = (f32[17,8,128]{2,1,0:T(8,128)}, f32[17,8,128]{2,1,0:T(8,128)S(1)}, u32[]{:S(2)}, u32[]{:S(2)}) collective-permute-start(f32[17,8,128]{2,1,0:T(8,128)} %pad_maximum_fusion.7), channel_id=1, source_target_pairs={{0,64},{8,72},{16,80},{24,88},{32,96},{40,104},{48,112},{56,120},{... | collective-permute-start | bytes 208904 | tf_op jit(solution)/shard_map/ppermute | solution.py:22
  47.3 4.9 %collective-permute-start.11 = (f32[17,8,128]{2,1,0:T(8,128)}, f32[17,8,128]{2,1,0:T(8,128)S(1)}, u32[]{:S(2)}, u32[]{:S(2)}) collective-permute-start(f32[17,8,128]{2,1,0:T(8,128)} %pad_maximum_fusion.7), channel_id=1, source_target_pairs={{0,32},{8,40},{16,48},{24,56},{32,64},{40,72},{48,80},{56,88},{64,... | collective-permute-start | bytes 208904 | tf_op jit(solution)/shard_map/ppermute | solution.py:22
  50.0 3.7 %collective-permute-start.13 = (f32[17,8,128]{2,1,0:T(8,128)}, f32[17,8,128]{2,1,0:T(8,128)S(1)}, u32[]{:S(2)}, u32[]{:S(2)}) collective-permute-start(f32[17,8,128]{2,1,0:T(8,128)} %pad_maximum_fusion.7), channel_id=1, source_target_pairs={{0,96},{8,104},{16,112},{24,120},{32,0},{40,8},{48,16},{56,24},{64... | collective-permute-start | bytes 208904 | tf_op jit(solution)/shard_map/ppermute | solution.py:22
  62.9 8.3 %collective-permute-start.14 = (bf16[128,1024]{1,0:T(8,128)(2,1)S(1)}, bf16[128,1024]{1,0:T(8,128)(2,1)}, u32[]{:S(2)}, u32[]{:S(2)}) collective-permute-start(bf16[128,1024]{1,0:T(8,128)(2,1)S(1)} %scan_output.1.own_ref), channel_id=1, source_target_pairs={{0,8},{8,0},{16,24},{24,16},{32,40},{40,32},{48,56},{56,48},{64,72... | collective-permute-start | bytes 786440 | tf_op jit(solution)/shard_map/ppermute | solution.py:27
  77.7 30.9 %all-to-all-start = ((bf16[8,2,128,256]{3,2,1,0:T(8,128)(2,1)}), bf16[8,2,128,256]{3,2,1,0:T(8,128)(2,1)S(1)}, u32[]{:S(2)}, u32[]{:S(2)}) async-start(bf16[8,2,128,256]{3,2,1,0:T(8,128)(2,1)} %project.1), calls=%async_computation | async-start | bytes 2097152 | tf_op jit(solution)/shard_map/all_to_all | solution.py:220
  108.8 3.2 %collective-permute-start.16 = (bf16[128,256]{1,0:T(8,128)(2,1)S(1)}, bf16[128,256]{1,0:T(8,128)(2,1)S(1)}, u32[]{:S(2)}, u32[]{:S(2)}) collective-permute-start(bf16[128,256]{1,0:T(8,128)(2,1)S(1)} %fusion.62), channel_id=1, source_target_pairs={{0,8},{8,0},{16,24},{24,16},{32,40},{40,32},{48,56},{56,48},{64,72... | collective-permute-start | bytes 196616 | tf_op jit(solution)/shard_map/ppermute | solution.py:27
  125.7 10.6 %collective-permute-start.22 = (bf16[24,4096]{1,0:T(8,128)(2,1)S(1)}, bf16[24,4096]{1,0:T(8,128)(2,1)S(1)}, u32[]{:S(2)}, u32[]{:S(2)}) collective-permute-start(bf16[24,4096]{1,0:T(8,128)(2,1)S(1)} %get-tuple-element.71), channel_id=1, source_target_pairs={{0,96},{8,104},{16,112},{24,120},{32,0},{40,8},{48,16},{56,24},{64... | collective-permute-start | bytes 589832 | tf_op jit(solution)/shard_map/ppermute | solution.py:22
  128.8 7.7 %collective-permute-start.21 = (bf16[24,4096]{1,0:T(8,128)(2,1)S(1)}, bf16[24,4096]{1,0:T(8,128)(2,1)S(1)}, u32[]{:S(2)}, u32[]{:S(2)}) collective-permute-start(bf16[24,4096]{1,0:T(8,128)(2,1)S(1)} %get-tuple-element.71), channel_id=1, source_target_pairs={{0,64},{8,72},{16,80},{24,88},{32,96},{40,104},{48,112},{56,120},{... | collective-permute-start | bytes 589832 | tf_op jit(solution)/shard_map/ppermute | solution.py:22
  128.8 11.9 %collective-permute-start.20 = (bf16[24,4096]{1,0:T(8,128)(2,1)S(1)}, bf16[24,4096]{1,0:T(8,128)(2,1)S(1)}, u32[]{:S(2)}, u32[]{:S(2)}) collective-permute-start(bf16[24,4096]{1,0:T(8,128)(2,1)S(1)} %get-tuple-element.71), channel_id=1, source_target_pairs={{0,32},{8,40},{16,48},{24,56},{32,64},{40,72},{48,80},{56,88},{64,... | collective-permute-start | bytes 589832 | tf_op jit(solution)/shard_map/ppermute | solution.py:22
  129.4 14.2 %collective-permute-start.19 = (bf16[24,4096]{1,0:T(8,128)(2,1)S(1)}, bf16[24,4096]{1,0:T(8,128)(2,1)S(1)}, u32[]{:S(2)}, u32[]{:S(2)}) collective-permute-start(bf16[24,4096]{1,0:T(8,128)(2,1)S(1)} %get-tuple-element.72), channel_id=1, source_target_pairs={{0,24},{8,0},{16,8},{24,16},{32,56},{40,32},{48,40},{56,48},{64,88... | collective-permute-start | bytes 589832 | tf_op jit(solution)/shard_map/ppermute | solution.py:22
  132.2 11.4 %collective-permute-start.18 = (bf16[24,4096]{1,0:T(8,128)(2,1)S(1)}, bf16[24,4096]{1,0:T(8,128)(2,1)S(1)}, u32[]{:S(2)}, u32[]{:S(2)}) collective-permute-start(bf16[24,4096]{1,0:T(8,128)(2,1)S(1)} %get-tuple-element.72), channel_id=1, source_target_pairs={{0,16},{8,24},{16,0},{24,8},{32,48},{40,56},{48,32},{56,40},{64,80... | collective-permute-start | bytes 589832 | tf_op jit(solution)/shard_map/ppermute | solution.py:22
  136.3 7.4 %collective-permute-start.17 = (bf16[24,4096]{1,0:T(8,128)(2,1)S(1)}, bf16[24,4096]{1,0:T(8,128)(2,1)S(1)}, u32[]{:S(2)}, u32[]{:S(2)}) collective-permute-start(bf16[24,4096]{1,0:T(8,128)(2,1)S(1)} %get-tuple-element.72), channel_id=1, source_target_pairs={{0,8},{8,16},{16,24},{24,0},{32,40},{40,48},{48,56},{56,32},{64,72... | collective-permute-start | bytes 589832 | tf_op jit(solution)/shard_map/ppermute | solution.py:22
  140.8 18.9 %collective-permute-start.26 = (bf16[4,24,4096]{2,1,0:T(8,128)(2,1)S(1)}, bf16[4,24,4096]{2,1,0:T(8,128)(2,1)S(1)}, u32[]{:S(2)}, u32[]{:S(2)}) collective-permute-start(bf16[4,24,4096]{2,1,0:T(8,128)(2,1)S(1)} %get-tuple-element.66), channel_id=1, source_target_pairs={{0,24},{8,0},{16,8},{24,16},{32,56},{40,32},{48,40},{56,48},{64,88... | collective-permute-start | bytes 2359304 | tf_op jit(solution)/shard_map/ppermute | solution.py:22
  143.7 19.5 %collective-permute-start.25 = (bf16[4,24,4096]{2,1,0:T(8,128)(2,1)S(1)}, bf16[4,24,4096]{2,1,0:T(8,128)(2,1)S(1)}, u32[]{:S(2)}, u32[]{:S(2)}) collective-permute-start(bf16[4,24,4096]{2,1,0:T(8,128)(2,1)S(1)} %get-tuple-element.66), channel_id=1, source_target_pairs={{0,8},{8,16},{16,24},{24,0},{32,40},{40,48},{48,56},{56,32},{64,72... | collective-permute-start | bytes 2359304 | tf_op jit(solution)/shard_map/ppermute | solution.py:22
  143.8 19.5 %collective-permute-start.24 = (bf16[4,24,4096]{2,1,0:T(8,128)(2,1)S(1)}, bf16[4,24,4096]{2,1,0:T(8,128)(2,1)S(1)}, u32[]{:S(2)}, u32[]{:S(2)}) collective-permute-start(bf16[4,24,4096]{2,1,0:T(8,128)(2,1)S(1)} %get-tuple-element.64), channel_id=1, source_target_pairs={{0,96},{8,104},{16,112},{24,120},{32,0},{40,8},{48,16},{56,24},{64... | collective-permute-start | bytes 2359304 | tf_op jit(solution)/shard_map/ppermute | solution.py:22
  146.3 17.2 %collective-permute-start.23 = (bf16[4,24,4096]{2,1,0:T(8,128)(2,1)S(1)}, bf16[4,24,4096]{2,1,0:T(8,128)(2,1)S(1)}, u32[]{:S(2)}, u32[]{:S(2)}) collective-permute-start(bf16[4,24,4096]{2,1,0:T(8,128)(2,1)S(1)} %get-tuple-element.64), channel_id=1, source_target_pairs={{0,32},{8,40},{16,48},{24,56},{32,64},{40,72},{48,80},{56,88},{64,... | collective-permute-start | bytes 2359304 | tf_op jit(solution)/shard_map/ppermute | solution.py:22
  159.7 14.4 %collective-permute-start.32 = (bf16[2,24,4096]{2,1,0:T(8,128)(2,1)S(1)}, bf16[2,24,4096]{2,1,0:T(8,128)(2,1)S(1)}, u32[]{:S(2)}, u32[]{:S(2)}) collective-permute-start(bf16[2,24,4096]{2,1,0:T(8,128)(2,1)S(1)} %slice.230), channel_id=1, source_target_pairs={{0,24},{8,0},{16,8},{24,16},{32,56},{40,32},{48,40},{56,48},{64,88... | collective-permute-start | bytes 1179656 | tf_op jit(solution)/shard_map/ppermute | solution.py:22
  163.2 13.6 %collective-permute-start.31 = (bf16[2,24,4096]{2,1,0:T(8,128)(2,1)S(1)}, bf16[2,24,4096]{2,1,0:T(8,128)(2,1)S(1)}, u32[]{:S(2)}, u32[]{:S(2)}) collective-permute-start(bf16[2,24,4096]{2,1,0:T(8,128)(2,1)S(1)} %slice.229), channel_id=1, source_target_pairs={{0,8},{8,16},{16,24},{24,0},{32,40},{40,48},{48,56},{56,32},{64,72... | collective-permute-start | bytes 1179656 | tf_op jit(solution)/shard_map/ppermute | solution.py:22
  163.4 13.6 %collective-permute-start.30 = (bf16[2,24,4096]{2,1,0:T(8,128)(2,1)S(1)}, bf16[2,24,4096]{2,1,0:T(8,128)(2,1)S(1)}, u32[]{:S(2)}, u32[]{:S(2)}) collective-permute-start(bf16[2,24,4096]{2,1,0:T(8,128)(2,1)S(1)} %slice.228), channel_id=1, source_target_pairs={{0,96},{8,104},{16,112},{24,120},{32,0},{40,8},{48,16},{56,24},{64... | collective-permute-start | bytes 1179656 | tf_op jit(solution)/shard_map/ppermute | solution.py:22
  163.5 13.4 %collective-permute-start.29 = (bf16[2,24,4096]{2,1,0:T(8,128)(2,1)S(1)}, bf16[2,24,4096]{2,1,0:T(8,128)(2,1)S(1)}, u32[]{:S(2)}, u32[]{:S(2)}) collective-permute-start(bf16[2,24,4096]{2,1,0:T(8,128)(2,1)S(1)} %slice.227), channel_id=1, source_target_pairs={{0,32},{8,40},{16,48},{24,56},{32,64},{40,72},{48,80},{56,88},{64,... | collective-permute-start | bytes 1179656 | tf_op jit(solution)/shard_map/ppermute | solution.py:22
  174.0 17.3 %collective-permute-start.38 = (bf16[4,24,4096]{2,1,0:T(8,128)(2,1)S(1)}, bf16[4,24,4096]{2,1,0:T(8,128)(2,1)S(1)}, u32[]{:S(2)}, u32[]{:S(2)}) collective-permute-start(bf16[4,24,4096]{2,1,0:T(8,128)(2,1)S(1)} %get-tuple-element.50), channel_id=1, source_target_pairs={{0,8},{8,16},{16,24},{24,0},{32,40},{40,48},{48,56},{56,32},{64,72... | collective-permute-start | bytes 2359304 | tf_op jit(solution)/shard_map/ppermute | solution.py:22
  174.1 18.3 %collective-permute-start.37 = (bf16[4,24,4096]{2,1,0:T(8,128)(2,1)S(1)}, bf16[4,24,4096]{2,1,0:T(8,128)(2,1)S(1)}, u32[]{:S(2)}, u32[]{:S(2)}) collective-permute-start(bf16[4,24,4096]{2,1,0:T(8,128)(2,1)S(1)} %get-tuple-element.51), channel_id=1, source_target_pairs={{0,24},{8,0},{16,8},{24,16},{32,56},{40,32},{48,40},{56,48},{64,88... | collective-permute-start | bytes 2359304 | tf_op jit(solution)/shard_map/ppermute | solution.py:22
  181.6 27.9 %collective-permute-start.39 = (bf16[4,24,4096]{2,1,0:T(8,128)(2,1)S(1)}, bf16[4,24,4096]{2,1,0:T(8,128)(2,1)S(1)}, u32[]{:S(2)}, u32[]{:S(2)}) collective-permute-start(bf16[4,24,4096]{2,1,0:T(8,128)(2,1)S(1)} %bitcast.233), channel_id=1, source_target_pairs={{0,16},{8,24},{16,0},{24,8},{32,48},{40,56},{48,32},{56,40},{64,80... | collective-permute-start | bytes 2359304 | tf_op jit(solution)/shard_map/ppermute | solution.py:22
  182.9 28.8 %collective-permute-start.28 = (bf16[4,24,4096]{2,1,0:T(8,128)(2,1)S(1)}, bf16[4,24,4096]{2,1,0:T(8,128)(2,1)S(1)}, u32[]{:S(2)}, u32[]{:S(2)}) collective-permute-start(bf16[4,24,4096]{2,1,0:T(8,128)(2,1)S(1)} %get-tuple-element.52), channel_id=1, source_target_pairs={{0,32},{8,40},{16,48},{24,56},{32,64},{40,72},{48,80},{56,88},{64,... | collective-permute-start | bytes 2359304 | tf_op jit(solution)/shard_map/ppermute | solution.py:22
  183.0 30.7 %collective-permute-start.27 = (bf16[4,24,4096]{2,1,0:T(8,128)(2,1)S(1)}, bf16[4,24,4096]{2,1,0:T(8,128)(2,1)S(1)}, u32[]{:S(2)}, u32[]{:S(2)}) collective-permute-start(bf16[4,24,4096]{2,1,0:T(8,128)(2,1)S(1)} %get-tuple-element.49), channel_id=1, source_target_pairs={{0,96},{8,104},{16,112},{24,120},{32,0},{40,8},{48,16},{56,24},{64... | collective-permute-start | bytes 2359304 | tf_op jit(solution)/shard_map/ppermute | solution.py:22
  191.3 24.5 %collective-permute-start.33 = (bf16[4,24,4096]{2,1,0:T(8,128)(2,1)S(1)}, bf16[4,24,4096]{2,1,0:T(8,128)(2,1)S(1)}, u32[]{:S(2)}, u32[]{:S(2)}) collective-permute-start(bf16[4,24,4096]{2,1,0:T(8,128)(2,1)S(1)} %bitcast.232), channel_id=1, source_target_pairs={{0,64},{8,72},{16,80},{24,88},{32,96},{40,104},{48,112},{56,120},{... | collective-permute-start | bytes 2359304 | tf_op jit(solution)/shard_map/ppermute | solution.py:22
  210.0 10.0 %collective-permute-start.42 = (bf16[24,4096]{1,0:T(8,128)(2,1)S(1)}, bf16[24,4096]{1,0:T(8,128)(2,1)S(1)}, u32[]{:S(2)}, u32[]{:S(2)}) collective-permute-start(bf16[24,4096]{1,0:T(8,128)(2,1)S(1)} %get-tuple-element.61), channel_id=1, source_target_pairs={{0,64},{8,72},{16,80},{24,88},{32,96},{40,104},{48,112},{56,120},{... | collective-permute-start | bytes 589832 | tf_op jit(solution)/shard_map/ppermute | solution.py:22
  211.1 17.9 %collective-permute-start.41 = (bf16[24,4096]{1,0:T(8,128)(2,1)S(1)}, bf16[24,4096]{1,0:T(8,128)(2,1)S(1)}, u32[]{:S(2)}, u32[]{:S(2)}) collective-permute-start(bf16[24,4096]{1,0:T(8,128)(2,1)S(1)} %get-tuple-element.62), channel_id=1, source_target_pairs={{0,32},{8,40},{16,48},{24,56},{32,64},{40,72},{48,80},{56,88},{64,... | collective-permute-start | bytes 589832 | tf_op jit(solution)/shard_map/ppermute | solution.py:22
  211.7 17.2 %collective-permute-start.40 = (bf16[24,4096]{1,0:T(8,128)(2,1)S(1)}, bf16[24,4096]{1,0:T(8,128)(2,1)S(1)}, u32[]{:S(2)}, u32[]{:S(2)}) collective-permute-start(bf16[24,4096]{1,0:T(8,128)(2,1)S(1)} %get-tuple-element.60), channel_id=1, source_target_pairs={{0,96},{8,104},{16,112},{24,120},{32,0},{40,8},{48,16},{56,24},{64... | collective-permute-start | bytes 589832 | tf_op jit(solution)/shard_map/ppermute | solution.py:22
  216.4 12.8 %collective-permute-start.36 = (bf16[24,4096]{1,0:T(8,128)(2,1)S(1)}, bf16[24,4096]{1,0:T(8,128)(2,1)S(1)}, u32[]{:S(2)}, u32[]{:S(2)}) collective-permute-start(bf16[24,4096]{1,0:T(8,128)(2,1)S(1)} %get-tuple-element.58), channel_id=1, source_target_pairs={{0,16},{8,24},{16,0},{24,8},{32,48},{40,56},{48,32},{56,40},{64,80... | collective-permute-start | bytes 589832 | tf_op jit(solution)/shard_map/ppermute | solution.py:22
  217.0 12.2 %collective-permute-start.35 = (bf16[24,4096]{1,0:T(8,128)(2,1)S(1)}, bf16[24,4096]{1,0:T(8,128)(2,1)S(1)}, u32[]{:S(2)}, u32[]{:S(2)}) collective-permute-start(bf16[24,4096]{1,0:T(8,128)(2,1)S(1)} %get-tuple-element.59), channel_id=1, source_target_pairs={{0,8},{8,16},{16,24},{24,0},{32,40},{40,48},{48,56},{56,32},{64,72... | collective-permute-start | bytes 589832 | tf_op jit(solution)/shard_map/ppermute | solution.py:22
  220.0 9.1 %collective-permute-start.34 = (bf16[24,4096]{1,0:T(8,128)(2,1)S(1)}, bf16[24,4096]{1,0:T(8,128)(2,1)S(1)}, u32[]{:S(2)}, u32[]{:S(2)}) collective-permute-start(bf16[24,4096]{1,0:T(8,128)(2,1)S(1)} %get-tuple-element.57), channel_id=1, source_target_pairs={{0,24},{8,0},{16,8},{24,16},{32,56},{40,32},{48,40},{56,48},{64,88... | collective-permute-start | bytes 589832 | tf_op jit(solution)/shard_map/ppermute | solution.py:22
  230.3 17.8 %all-to-all-start.2 = ((bf16[8,48,512]{2,1,0:T(8,128)(2,1)}), bf16[8,48,512]{2,1,0:T(8,128)(2,1)S(1)}, u32[]{:S(2)}, u32[]{:S(2)}) async-start(bf16[8,48,512]{2,1,0:T(8,128)(2,1)} %copy.55), calls=%async_computation.2 | async-start | bytes 786432 | tf_op jit(solution)/shard_map/all_to_all | solution.py:299
  (26 other events, 214.6 us)
